TPU v7x, 32 devices: a whole 2x2x4 slice. The times are simulated.
32 devices in a mesh: dp: 8 (over y, x, core), tensor: 4 (over z).
Axes of the slice: x: 2, y: 2, z: 4, core: 2. Of those that a mesh axis runs over, the one named last changes fastest.
Arguments:
- latents: bfloat16 [1024, 16, 1408], P('tensor', 'dp'), may hold values from -6 to 6
- skips: bfloat16 [1024, 16, 1408], P('tensor', 'dp'), may hold values from -6 to 6
- text_states: bfloat16 [16, 333, 1024], P('dp'), may hold values from -6 to 6
- time_embedding: bfloat16 [16, 1408], P('dp'), may hold values from -6 to 6
- merger: bfloat16 [2816, 1408], P(('dp', 'tensor')), may hold values from -0.109375 to 0.109375
- modulator: bfloat16 [1408, 1408], P(('dp', 'tensor')), may hold values from -0.15625 to 0.15625
- norm_gains: float32 [5, 1408], P(None, ('dp', 'tensor')), may hold values from 0.1 to 1.9
- norm_biases: float32 [9, 1408], P(None, ('dp', 'tensor')), may hold values from -1.75 to 1.75
- output_bias: float32 [1408], P(('dp', 'tensor')), may hold values from -8 to 8
- projector: bfloat16 [1408, 3, 1408], P('dp', None, 'tensor'), may hold values from -0.15625 to 0.15625
- combiner: bfloat16 [1408, 1408], P('tensor', 'dp'), may hold values from -1.25 to 1.25
- cross_query: bfloat16 [1408, 1408], P('dp', 'tensor'), may hold values from -0.15625 to 0.15625
- cross_memory: bfloat16 [1024, 2, 1408], P('dp', None, 'tensor'), may hold values from -0.1875 to 0.1875
- blender: bfloat16 [1408, 1408], P('tensor', 'dp'), may hold values from -1.25 to 1.25
- expander: bfloat16 [1408, 6144], P('dp', 'tensor'), may hold values from -0.15625 to 0.15625
- reducer: bfloat16 [6144, 1408], P('tensor', 'dp'), may hold values from -0.078125 to 0.078125
- column_biases: float32 [6, 1408], P(None, ('dp', 'tensor')), may hold values from -1.75 to 1.75
- hidden_bias: float32 [6144], P(('dp', 'tensor')), may hold values from -1.75 to 1.75
- per_head_norm_gains: float32 [4, 88], replicated, may hold values from 0.1 to 1.9
- head_shifts: float32 [3, 88], replicated, may hold values from -1.75 to 1.75
- cotangent: bfloat16 [1024, 16, 1408], P('tensor', 'dp'), may hold values from -6 to 6
Outputs:
- block_out: float32 [1024, 16, 1408], P('tensor', 'dp')
- latent_grads: float32 [1024, 16, 1408], P('tensor', 'dp')
- skip_grads: float32 [1024, 16, 1408], P('tensor', 'dp')
- text_grads: float32 [16, 333, 1024], P('dp', None, 'tensor')
- time_grads: float32 [16, 1408], P('dp', 'tensor')
- merger_grads: float32 [2816, 1408], P(('dp', 'tensor'))
- modulator_grads: float32 [1408, 1408], P(('dp', 'tensor'))
- gain_grads: float32 [5, 1408], P(None, ('dp', 'tensor'))
- bias_grads: float32 [9, 1408], P(None, ('dp', 'tensor'))
- output_bias_grads: float32 [1408], P(('dp', 'tensor'))
- projector_grads: float32 [1408, 3, 1408], P('dp', None, 'tensor')
- combiner_grads: float32 [1408, 1408], P('tensor', 'dp')
- query_grads: float32 [1408, 1408], P('dp', 'tensor')
- memory_grads: float32 [1024, 2, 1408], P('dp', None, 'tensor')
- blender_grads: float32 [1408, 1408], P('tensor', 'dp')
- expander_grads: float32 [1408, 6144], P('dp', 'tensor')
- reducer_grads: float32 [6144, 1408], P('tensor', 'dp')
- column_grads: float32 [6, 1408], P(None, ('dp', 'tensor'))
- hidden_grads: float32 [6144], P(('dp', 'tensor'))
- scale_grads: float32 [4, 88], replicated
- shift_grads: float32 [3, 88], replicated
All inputs are finite; a program needn't handle non-finite values.
Results may differ from a plain program's by a relative error of at most 0.038.
Values may be sent and summed in bfloat16 or wider, within the bound.
A program may use at most 320 MiB of HBM per device.

v0:
```python
from functools import partial

import jax
import jax.numpy as jnp
from jax import lax
from jax.sharding import PartitionSpec as P

GRID_W = 32


EPSILON = 1e-06
THETA = 10000.0


def normalize(values):
    centred = values - jnp.mean(values, axis=-1, keepdims=True)
    inverse = lax.rsqrt(jnp.mean(centred * centred, axis=-1, keepdims=True) + EPSILON)
    return (centred * inverse, inverse)


def layer_norm_backward(grad_out, normed, inverse, gain):
    scaled = grad_out * gain
    first_mean = jnp.mean(scaled, axis=-1, keepdims=True)
    second_mean = jnp.mean(scaled * normed, axis=-1, keepdims=True)
    return inverse * (scaled - first_mean - normed * second_mean)


def contract_last(left, right):
    return lax.dot_general(
        left, right, (((1,), (1,)), ((), ())), preferred_element_type=jnp.float32
    )


def contract_first(left, right):
    return lax.dot_general(
        left, right, (((0,), (0,)), ((), ())), preferred_element_type=jnp.float32
    )


def rope_tables(length, head_size):
    quarter = head_size // 4
    position = jnp.arange(length)
    row_index = (position // GRID_W).astype(jnp.float32)
    col_index = (position % GRID_W).astype(jnp.float32)
    inverse = THETA ** (-2.0 * jnp.arange(quarter).astype(jnp.float32) / (head_size // 2))
    angles = jnp.stack([row_index[:, None] * inverse, col_index[:, None] * inverse], axis=1)
    return (jnp.cos(angles)[:, :, None, :], jnp.sin(angles)[:, :, None, :])


def apply_rotary_embedding(values, rotary_cosine_values, rotary_sine_values, direction):
    value_shape = values.shape
    quarter = value_shape[-1] // 4
    halves = values.reshape(value_shape[:-1] + (2, 2, quarter))
    spread = (value_shape[0],) + (1,) * (len(value_shape) - 2) + (2, 1, quarter)
    swapped = jnp.stack([-halves[..., 1, :], halves[..., 0, :]], axis=-2)
    turned = halves * rotary_cosine_values.reshape(
        spread
    ) + direction * swapped * rotary_sine_values.reshape(spread)
    return turned.reshape(value_shape)


def attend(query, keys, values, query_block):
    block_count = query.shape[0] // query_block
    query_parts = query.reshape((block_count, query_block) + query.shape[1:])

    def attend_one_block(query_part):
        scores = jnp.einsum("qshd,kshd->shqk", query_part, keys, preferred_element_type=jnp.float32)
        row_max = jnp.max(scores, axis=-1, keepdims=True)
        exponent = jnp.exp(scores - row_max)
        row_total = jnp.sum(exponent, axis=-1, keepdims=True)
        shares = (exponent / row_total).astype(jnp.bfloat16)
        mixture = jnp.einsum("shqk,kshd->qshd", shares, values, preferred_element_type=jnp.float32)
        return (mixture.astype(jnp.bfloat16), (row_max + jnp.log(row_total))[..., 0])

    mixture, log_sums = lax.map(attend_one_block, query_parts)
    return (mixture.reshape(query.shape), log_sums)


def attention_backward_pass(query, keys, values, log_sums, mixture_grad, query_block):
    block_count = query.shape[0] // query_block
    query_parts = query.reshape((block_count, query_block) + query.shape[1:])
    grad_parts = mixture_grad.reshape((block_count, query_block) + query.shape[1:])

    def attention_one_block(running, scan_items):
        keys_grad, values_grad = running
        query_part, grad_part, sums_part = scan_items
        scores = jnp.einsum("qshd,kshd->shqk", query_part, keys, preferred_element_type=jnp.float32)
        shares = jnp.exp(scores - sums_part[..., None])
        share_grad = jnp.einsum(
            "qshd,kshd->shqk", grad_part, values, preferred_element_type=jnp.float32
        )
        inner = jnp.sum(shares * share_grad, axis=-1, keepdims=True)
        score_grad = (shares * (share_grad - inner)).astype(jnp.bfloat16)
        query_grad = jnp.einsum(
            "shqk,kshd->qshd", score_grad, keys, preferred_element_type=jnp.float32
        )
        keys_grad = keys_grad + jnp.einsum(
            "shqk,qshd->kshd", score_grad, query_part, preferred_element_type=jnp.float32
        )
        values_grad = values_grad + jnp.einsum(
            "shqk,qshd->kshd",
            shares.astype(jnp.bfloat16),
            grad_part,
            preferred_element_type=jnp.float32,
        )
        return ((keys_grad, values_grad), query_grad)

    empty_grad = jnp.zeros(keys.shape, jnp.float32)
    (keys_grad, values_grad), query_grad = lax.scan(
        attention_one_block, (empty_grad, empty_grad), (query_parts, grad_parts, log_sums)
    )
    return (query_grad.reshape(query.shape), keys_grad, values_grad)


def body(
    latents,
    skips,
    text_states,
    time_embedding,
    merger,
    modulator,
    norm_gains,
    norm_biases,
    output_bias,
    projector,
    combiner,
    cross_query,
    cross_memory,
    blender,
    expander,
    reducer,
    column_biases,
    hidden_bias,
    per_head_norm_gains,
    head_shifts,
    cotangent,
):
    merger_all, modulator_all, gains, biases, output_bias_all, columns_all, hidden_all = (
        lax.all_gather(merger, ("dp", "tensor"), axis=0, tiled=True),
        lax.all_gather(modulator, ("dp", "tensor"), axis=0, tiled=True),
        lax.all_gather(
            norm_gains.astype(jnp.bfloat16), ("dp", "tensor"), axis=1, tiled=True
        ).astype(norm_gains.dtype),
        lax.all_gather(
            norm_biases.astype(jnp.bfloat16), ("dp", "tensor"), axis=1, tiled=True
        ).astype(norm_biases.dtype),
        lax.all_gather(
            output_bias.astype(jnp.bfloat16), ("dp", "tensor"), axis=0, tiled=True
        ).astype(output_bias.dtype),
        lax.all_gather(
            column_biases.astype(jnp.bfloat16), ("dp", "tensor"), axis=1, tiled=True
        ).astype(column_biases.dtype),
        lax.all_gather(
            hidden_bias.astype(jnp.bfloat16), ("dp", "tensor"), axis=0, tiled=True
        ).astype(hidden_bias.dtype),
    )
    projector_all, combiner_all, query_all, memory_all, blender_all, expander_all, reducer_all = (
        lax.all_gather(projector, "dp", axis=0, tiled=True),
        lax.all_gather(combiner, "dp", axis=1, tiled=True),
        lax.all_gather(cross_query, "dp", axis=0, tiled=True),
        lax.all_gather(cross_memory, "dp", axis=0, tiled=True),
        lax.all_gather(blender, "dp", axis=1, tiled=True),
        lax.all_gather(expander, "dp", axis=0, tiled=True),
        lax.all_gather(reducer, "dp", axis=1, tiled=True),
    )
    shard_len, sequences, model_width = latents.shape
    text_width = text_states.shape[2]
    head_size = per_head_norm_gains.shape[1]
    head_cols = projector.shape[2]
    local_heads = head_cols // head_size
    hidden_cols = expander.shape[1]
    tensor_rank = lax.axis_index("tensor")
    local_rows = shard_len * sequences
    seq_len = shard_len * lax.axis_size("tensor")
    total_rows = seq_len * sequences
    text_len = text_states.shape[1]
    memory_rows = text_len * sequences
    query_block = min(512, seq_len)
    softmax_scale = head_size ** (-0.5)
    head_shape = (seq_len, sequences, local_heads, head_size)
    memory_shape = (text_len, sequences, local_heads, head_size)
    local_shape = (shard_len, sequences, model_width)
    rotary_cosine_values, rotary_sine_values = rope_tables(seq_len, head_size)
    own_columns = lax.dynamic_slice_in_dim(columns_all, tensor_rank * head_cols, head_cols, 1)
    own_hidden = lax.dynamic_slice_in_dim(hidden_all, tensor_rank * hidden_cols, hidden_cols, 0)

    def gather_rows(local_part):
        return lax.all_gather(local_part, "tensor", axis=0, tiled=True)

    def rows_back(local_part):
        return lax.all_gather(local_part, "tensor", axis=0, tiled=True).reshape(
            total_rows, model_width
        )

    def scatter_rows(source, weight):

        def partial_term(row_start, row_count):
            return jnp.dot(source, weight, preferred_element_type=jnp.float32)

        return lax.psum_scatter(
            partial_term(jnp.int32(0), local_rows * lax.axis_size("tensor")).astype(jnp.bfloat16),
            "tensor",
            scatter_dimension=0,
            tiled=True,
        ).astype(jnp.float32)

    def gather_grads(local_part):
        return lax.all_gather(
            local_part.reshape(local_shape), "tensor", axis=0, tiled=True
        ).reshape(total_rows, model_width)

    def scatter_grads(source, weight):

        def partial_term(row_start, row_count):
            return contract_last(source, weight)

        return lax.psum_scatter(
            partial_term(jnp.int32(0), local_rows * lax.axis_size("tensor")).astype(jnp.bfloat16),
            "tensor",
            scatter_dimension=0,
            tiled=True,
        ).astype(jnp.float32)

    flat_latents = latents.reshape(local_rows, model_width).astype(jnp.float32)
    flat_skips = skips.reshape(local_rows, model_width).astype(jnp.float32)
    joined = jnp.concatenate([flat_latents, flat_skips], axis=1)
    join_gain = jnp.concatenate([gains[0], gains[1]])
    join_bias = jnp.concatenate([biases[0], biases[1]])
    join_hat, join_inv = normalize(joined)
    merge_in = (join_hat * join_gain + join_bias).astype(jnp.bfloat16)
    first = jnp.dot(merge_in, merger_all, preferred_element_type=jnp.float32) + biases[5]
    time_values = time_embedding.astype(jnp.float32)
    silu_time = jax.nn.silu(time_values).astype(jnp.bfloat16)
    modulation = jnp.dot(silu_time, modulator_all, preferred_element_type=jnp.float32) + biases[6]
    first_hat, first_inv = normalize(first)
    self_entry = (
        (first_hat * gains[2] + biases[2]).reshape(local_shape) + modulation[None]
    ).astype(jnp.bfloat16)
    self_all = gather_rows(self_entry)
    self_flat = self_all.reshape(total_rows, model_width)
    packed = (
        jnp.dot(
            self_flat,
            projector_all.reshape(model_width, 3 * head_cols),
            preferred_element_type=jnp.float32,
        ).reshape(total_rows, 3, head_cols)
        + own_columns[None, 0:3]
    )
    query_hat, query_inv = normalize(packed[:, 0].reshape(head_shape))
    normalized_key_rows, key_inverse_norm = normalize(packed[:, 1].reshape(head_shape))
    query_low = (
        apply_rotary_embedding(
            query_hat * per_head_norm_gains[0] + head_shifts[0],
            rotary_cosine_values,
            rotary_sine_values,
            1.0,
        )
        * softmax_scale
    ).astype(jnp.bfloat16)
    key_low = apply_rotary_embedding(
        normalized_key_rows * per_head_norm_gains[1] + head_shifts[1],
        rotary_cosine_values,
        rotary_sine_values,
        1.0,
    ).astype(jnp.bfloat16)
    value_low = packed[:, 2].reshape(head_shape).astype(jnp.bfloat16)
    attended, self_sums = attend(query_low, key_low, value_low, query_block)
    attended_flat = attended.reshape(total_rows, head_cols)
    second = first + (scatter_rows(attended_flat, combiner_all) + biases[7])
    cross_hat, cross_inv = normalize(second)
    cross_entry = (cross_hat * gains[3] + biases[3]).reshape(local_shape).astype(jnp.bfloat16)
    cross_all = gather_rows(cross_entry)
    cross_flat = cross_all.reshape(total_rows, model_width)
    cross_pre = jnp.dot(cross_flat, query_all, preferred_element_type=jnp.float32) + own_columns[3]
    cquery_hat, cquery_inv = normalize(cross_pre.reshape(head_shape))
    cross_qlow = ((cquery_hat * per_head_norm_gains[2] + head_shifts[2]) * softmax_scale).astype(
        jnp.bfloat16
    )
    text_flat = jnp.transpose(text_states, (1, 0, 2)).reshape(memory_rows, text_width)
    memory = (
        jnp.dot(
            text_flat,
            memory_all.reshape(text_width, 2 * head_cols),
            preferred_element_type=jnp.float32,
        ).reshape(memory_rows, 2, head_cols)
        + own_columns[None, 4:6]
    )
    mkey_hat, mkey_inv = normalize(memory[:, 0].reshape(memory_shape))
    memory_keys = (mkey_hat * per_head_norm_gains[3]).astype(jnp.bfloat16)
    memory_values = memory[:, 1].reshape(memory_shape).astype(jnp.bfloat16)
    crossed, cross_sums = attend(cross_qlow, memory_keys, memory_values, query_block)
    crossed_flat = crossed.reshape(total_rows, head_cols)
    third = second + (scatter_rows(crossed_flat, blender_all) + biases[8])
    ffn_hat, ffn_inv = normalize(third)
    ffn_entry = (ffn_hat * gains[4] + biases[4]).reshape(local_shape).astype(jnp.bfloat16)
    ffn_all = gather_rows(ffn_entry)
    hidden = (
        jnp.dot(
            ffn_all.reshape(total_rows, model_width),
            expander_all,
            preferred_element_type=jnp.float32,
        )
        + own_hidden
    )
    active = jax.nn.gelu(hidden, approximate=True).astype(jnp.bfloat16)
    block_out = third + scatter_rows(active, reducer_all) + output_bias_all
    grad_low = cotangent.reshape(local_rows, model_width)
    grad_top = grad_low.astype(jnp.float32)
    reducer_bias = jnp.sum(grad_top, axis=0)
    grad_all = gather_grads(grad_low)
    reducer_grad = contract_first(active, grad_all)
    active_grad = contract_last(grad_all, reducer_all)
    _, gelu_pull = jax.vjp(partial(jax.nn.gelu, approximate=True), hidden)
    hidden_grad = gelu_pull(active_grad)[0].astype(jnp.bfloat16)
    expander_grad = contract_first(rows_back(ffn_entry), hidden_grad)
    own_hidden_grad = jnp.sum(hidden_grad.astype(jnp.float32), axis=0)
    ffn_back = scatter_grads(hidden_grad, expander_all)
    ffn_gain = jnp.sum(ffn_back * ffn_hat, axis=0)
    ffn_bias = jnp.sum(ffn_back, axis=0)
    grad_third = grad_top + layer_norm_backward(ffn_back, ffn_hat, ffn_inv, gains[4])
    third_low = grad_third.astype(jnp.bfloat16)
    blender_bias = jnp.sum(third_low.astype(jnp.float32), axis=0)
    grad_all = gather_grads(third_low)
    blender_grad = contract_first(crossed_flat, grad_all)
    crossed_grad = contract_last(grad_all, blender_all).astype(jnp.bfloat16).reshape(head_shape)
    cquery_grad, mkey_grad, mvalue_grad = attention_backward_pass(
        cross_qlow, memory_keys, memory_values, cross_sums, crossed_grad, query_block
    )
    cquery_grad = cquery_grad * softmax_scale
    scale_two = jnp.sum(cquery_grad * cquery_hat, axis=(0, 1, 2))
    shift_two = jnp.sum(cquery_grad, axis=(0, 1, 2))
    cross_pre_grad = (
        layer_norm_backward(cquery_grad, cquery_hat, cquery_inv, per_head_norm_gains[2])
        .reshape(total_rows, head_cols)
        .astype(jnp.bfloat16)
    )
    scale_three = jnp.sum(mkey_grad * mkey_hat, axis=(0, 1, 2))
    mkey_pre = layer_norm_backward(mkey_grad, mkey_hat, mkey_inv, per_head_norm_gains[3]).reshape(
        memory_rows, head_cols
    )
    memory_grad = (
        jnp.stack([mkey_pre, mvalue_grad.reshape(memory_rows, head_cols)], axis=1)
        .astype(jnp.bfloat16)
        .reshape(memory_rows, 2 * head_cols)
    )
    memory_grad_w = contract_first(text_flat, memory_grad).reshape(text_width, 2, head_cols)
    memory_bias = jnp.sum(memory_grad.astype(jnp.float32), axis=0).reshape(2, head_cols)
    text_term = contract_last(memory_grad, memory_all.reshape(text_width, 2 * head_cols))
    text_term = jnp.transpose(text_term.reshape(text_len, sequences, text_width), (1, 0, 2))
    query_grad_w = contract_first(rows_back(cross_entry), cross_pre_grad)
    query_bias = jnp.sum(cross_pre_grad.astype(jnp.float32), axis=0)
    cross_back = scatter_grads(cross_pre_grad, query_all)
    cross_gain = jnp.sum(cross_back * cross_hat, axis=0)
    cross_bias = jnp.sum(cross_back, axis=0)
    grad_second = grad_third + layer_norm_backward(cross_back, cross_hat, cross_inv, gains[3])
    second_low = grad_second.astype(jnp.bfloat16)
    combiner_bias = jnp.sum(second_low.astype(jnp.float32), axis=0)
    grad_all = gather_grads(second_low)
    combiner_grad = contract_first(attended_flat, grad_all)
    attended_grad = contract_last(grad_all, combiner_all).astype(jnp.bfloat16).reshape(head_shape)
    self_query_gradient, self_key_gradient, self_value_gradient = attention_backward_pass(
        query_low, key_low, value_low, self_sums, attended_grad, query_block
    )
    self_query_gradient = apply_rotary_embedding(
        self_query_gradient * softmax_scale, rotary_cosine_values, rotary_sine_values, -1.0
    )
    self_key_gradient = apply_rotary_embedding(
        self_key_gradient, rotary_cosine_values, rotary_sine_values, -1.0
    )
    scale_zero = jnp.sum(self_query_gradient * query_hat, axis=(0, 1, 2))
    shift_zero = jnp.sum(self_query_gradient, axis=(0, 1, 2))
    attention_scale_factor = jnp.sum(self_key_gradient * normalized_key_rows, axis=(0, 1, 2))
    attention_shift_offset = jnp.sum(self_key_gradient, axis=(0, 1, 2))
    packed_grad = (
        jnp.stack(
            [
                layer_norm_backward(
                    self_query_gradient, query_hat, query_inv, per_head_norm_gains[0]
                ).reshape(total_rows, head_cols),
                layer_norm_backward(
                    self_key_gradient, normalized_key_rows, key_inverse_norm, per_head_norm_gains[1]
                ).reshape(total_rows, head_cols),
                self_value_gradient.reshape(total_rows, head_cols),
            ],
            axis=1,
        )
        .astype(jnp.bfloat16)
        .reshape(total_rows, 3 * head_cols)
    )
    projector_grad = contract_first(rows_back(self_entry), packed_grad).reshape(
        model_width, 3, head_cols
    )
    packed_bias = jnp.sum(packed_grad.astype(jnp.float32), axis=0).reshape(3, head_cols)
    self_back = scatter_grads(packed_grad, projector_all.reshape(model_width, 3 * head_cols))
    (
        projector_grads,
        combiner_grads,
        query_grads,
        memory_grads,
        blender_grads,
        expander_grads,
        reducer_grads,
    ) = (
        lax.psum_scatter(
            projector_grad.astype(jnp.bfloat16), "dp", scatter_dimension=0, tiled=True
        ).astype(jnp.float32),
        lax.psum_scatter(
            combiner_grad.astype(jnp.bfloat16), "dp", scatter_dimension=1, tiled=True
        ).astype(jnp.float32),
        lax.psum_scatter(
            query_grad_w.astype(jnp.bfloat16), "dp", scatter_dimension=0, tiled=True
        ).astype(jnp.float32),
        lax.psum_scatter(
            memory_grad_w.astype(jnp.bfloat16), "dp", scatter_dimension=0, tiled=True
        ).astype(jnp.float32),
        lax.psum_scatter(
            blender_grad.astype(jnp.bfloat16), "dp", scatter_dimension=1, tiled=True
        ).astype(jnp.float32),
        lax.psum_scatter(
            expander_grad.astype(jnp.bfloat16), "dp", scatter_dimension=0, tiled=True
        ).astype(jnp.float32),
        lax.psum_scatter(
            reducer_grad.astype(jnp.bfloat16), "dp", scatter_dimension=1, tiled=True
        ).astype(jnp.float32),
    )
    shift_grad = jnp.sum(self_back.reshape(local_shape), axis=0)
    self_gain = jnp.sum(self_back * first_hat, axis=0)
    self_bias = jnp.sum(self_back, axis=0)
    grad_first = grad_second + layer_norm_backward(self_back, first_hat, first_inv, gains[2])
    modulation_bias = jnp.sum(shift_grad, axis=0)
    modulator_grad = lax.dot_general(
        silu_time.astype(jnp.float32),
        shift_grad,
        (((0,), (0,)), ((), ())),
        precision=lax.Precision.HIGHEST,
    )
    silu_grad = lax.dot_general(
        shift_grad,
        modulator_all.astype(jnp.float32),
        (((1,), (1,)), ((), ())),
        precision=lax.Precision.HIGHEST,
    )
    _, silu_pull = jax.vjp(jax.nn.silu, time_values)
    time_term = silu_pull(silu_grad)[0]
    first_low = grad_first.astype(jnp.bfloat16)
    merger_bias = jnp.sum(first_low.astype(jnp.float32), axis=0)
    merger_grad = contract_first(merge_in, first_low)
    join_back = contract_last(first_low, merger_all)
    join_gain_grad = jnp.sum(join_back * join_hat, axis=0)
    join_bias_grad = jnp.sum(join_back, axis=0)
    joined_grad = layer_norm_backward(join_back, join_hat, join_inv, join_gain)
    latent_grads = joined_grad[:, :model_width].reshape(local_shape)
    skip_grads = joined_grad[:, model_width:].reshape(local_shape)
    gain_full = jnp.stack(
        [
            join_gain_grad[:model_width],
            join_gain_grad[model_width:],
            self_gain,
            cross_gain,
            ffn_gain,
        ]
    )
    bias_full = jnp.stack(
        [
            join_bias_grad[:model_width],
            join_bias_grad[model_width:],
            self_bias,
            cross_bias,
            ffn_bias,
            merger_bias,
            modulation_bias,
            combiner_bias,
            blender_bias,
        ]
    )
    own_column_grad = jnp.concatenate([packed_bias, query_bias[None], memory_bias], axis=0)
    column_full = lax.dynamic_update_slice_in_dim(
        jnp.zeros(columns_all.shape, jnp.float32), own_column_grad, tensor_rank * head_cols, 1
    )
    hidden_full = lax.dynamic_update_slice_in_dim(
        jnp.zeros(hidden_all.shape, jnp.float32), own_hidden_grad, tensor_rank * hidden_cols, 0
    )
    (
        merger_grads,
        modulator_grads,
        gain_grads,
        bias_grads,
        output_bias_grads,
        column_grads,
        hidden_grads,
    ) = (
        lax.psum_scatter(merger_grad, ("dp", "tensor"), scatter_dimension=0, tiled=True),
        lax.psum_scatter(modulator_grad, ("dp", "tensor"), scatter_dimension=0, tiled=True),
        lax.psum_scatter(gain_full, ("dp", "tensor"), scatter_dimension=1, tiled=True),
        lax.psum_scatter(bias_full, ("dp", "tensor"), scatter_dimension=1, tiled=True),
        lax.psum_scatter(reducer_bias, ("dp", "tensor"), scatter_dimension=0, tiled=True),
        lax.psum_scatter(column_full, ("dp", "tensor"), scatter_dimension=1, tiled=True),
        lax.psum_scatter(hidden_full, ("dp", "tensor"), scatter_dimension=0, tiled=True),
    )
    scale_grads, shift_grads = lax.psum(
        (
            jnp.stack([scale_zero, attention_scale_factor, scale_two, scale_three]),
            jnp.stack([shift_zero, attention_shift_offset, shift_two]),
        ),
        ("dp", "tensor"),
    )
    text_grads, time_grads = (
        lax.psum_scatter(
            text_term.astype(jnp.bfloat16), "tensor", scatter_dimension=2, tiled=True
        ).astype(jnp.float32),
        lax.psum_scatter(
            time_term.astype(jnp.bfloat16), "tensor", scatter_dimension=1, tiled=True
        ).astype(jnp.float32),
    )
    return (
        block_out.reshape(local_shape),
        latent_grads,
        skip_grads,
        text_grads,
        time_grads,
        merger_grads,
        modulator_grads,
        gain_grads,
        bias_grads,
        output_bias_grads,
        projector_grads,
        combiner_grads,
        query_grads,
        memory_grads,
        blender_grads,
        expander_grads,
        reducer_grads,
        column_grads,
        hidden_grads,
        scale_grads,
        shift_grads,
    )


def solution(mesh):
    return jax.shard_map(
        body,
        mesh=mesh,
        in_specs=(
            P("tensor", "dp", None),
            P("tensor", "dp", None),
            P("dp", None, None),
            P("dp", None),
            P(("dp", "tensor"), None),
            P(("dp", "tensor"), None),
            P(None, ("dp", "tensor")),
            P(None, ("dp", "tensor")),
            P(("dp", "tensor")),
            P("dp", None, "tensor"),
            P("tensor", "dp"),
            P("dp", "tensor"),
            P("dp", None, "tensor"),
            P("tensor", "dp"),
            P("dp", "tensor"),
            P("tensor", "dp"),
            P(None, ("dp", "tensor")),
            P(("dp", "tensor")),
            P(),
            P(),
            P("tensor", "dp", None),
        ),
        out_specs=(
            P("tensor", "dp", None),
            P("tensor", "dp", None),
            P("tensor", "dp", None),
            P("dp", None, "tensor"),
            P("dp", "tensor"),
            P(("dp", "tensor"), None),
            P(("dp", "tensor"), None),
            P(None, ("dp", "tensor")),
            P(None, ("dp", "tensor")),
            P(("dp", "tensor")),
            P("dp", None, "tensor"),
            P("tensor", "dp"),
            P("dp", "tensor"),
            P("dp", None, "tensor"),
            P("tensor", "dp"),
            P("dp", "tensor"),
            P("tensor", "dp"),
            P(None, ("dp", "tensor")),
            P(("dp", "tensor")),
            P(),
            P(),
        ),
        check_vma=False,
    )
```

profile of v0, /device:TPU:9, one launch (start us, length us, event | category | flops | bytes accessed | tf_op | source)
XLA Modules:
  0.0 3393.7 jit_solution(18230904354263417519)
XLA Ops:
  10.8 59.8 %all-gather = bf16[32,44,5]{1,2,0:T(8,128)(2,1)S(1)} all-gather(bf16[1,44,5]{1,2,0:T(8,128)(2,1)S(1)} %convert_bitcast_fusion.2), channel_id=1, replica_groups=mesh['dp'=8,'tensor'=4] {'dp','tensor'}, dimensions={0}, use_global_device_ids=true | all-gather | bytes 14520 | tf_op jit(solution)/shard_map/all_gather | solution.py:141
  70.6 71.0 %all-gather.1 = bf16[32,44,9]{1,2,0:T(8,128)(2,1)S(1)} all-gather(bf16[1,44,9]{1,2,0:T(8,128)(2,1)S(1)} %convert_bitcast_fusion), channel_id=1, replica_groups=mesh['dp'=8,'tensor'=4] {'dp','tensor'}, dimensions={0}, use_global_device_ids=true | all-gather | bytes 26136 | tf_op jit(solution)/shard_map/all_gather | solution.py:144
  187.4 72.1 %all-gather.3 = bf16[32,44,6]{1,2,0:T(8,128)(2,1)S(1)} all-gather(bf16[1,44,6]{1,2,0:T(8,128)(2,1)S(1)} %convert_bitcast_fusion.1), channel_id=1, replica_groups=mesh['dp'=8,'tensor'=4] {'dp','tensor'}, dimensions={0}, use_global_device_ids=true | all-gather | bytes 17424 | tf_op jit(solution)/shard_map/all_gather | solution.py:150
  262.6 13.4 all_gather.70
  334.0 30.9 multiply_reduce_fusion.9
  379.9 30.9 multiply_reduce_fusion.10
  416.5 27.9 reshape_squeeze.19
  444.4 28.2 reshape_squeeze.21
  492.0 22.4 copy.528
  526.3 22.5 copy.536
  582.7 22.3 while.54
  622.1 102.8 %reduce-scatter.29.cloned.1.call-done = bf16[512,1408]{1,0:T(8,128)(2,1)} async-done(((bf16[2048,1408]{1,0:T(8,128)(2,1)}), bf16[512,1408]{1,0:T(8,128)(2,1)}) %reduce-scatter.29.cloned.1.call-update) | async-done | bytes 1441808 | tf_op jit(solution)/shard_map/reduce_scatter | solution.py:200
  730.9 13.5 all_gather.72
  744.5 14.2 all_gather.74
  778.3 83.0 %all-gather.23.cloned.1.call-done = bf16[1024,2,1408]{2,1,0:T(2,128)(2,1)} async-done(((bf16[256,2,1408]{2,1,0:T(2,128)(2,1)}), bf16[1024,2,1408]{2,1,0:T(2,128)(2,1)}) %all-gather.23.cloned.1.call-update) | async-done | bytes 5767184 | tf_op jit(solution)/shard_map/all_gather | solution.py:188
  903.5 30.0 multiply_reduce_fusion.8
  972.3 102.7 %reduce-scatter.31.cloned.1.call-done = bf16[512,1408]{1,0:T(8,128)(2,1)} async-done(((bf16[2048,1408]{1,0:T(8,128)(2,1)}), bf16[512,1408]{1,0:T(8,128)(2,1)}) %reduce-scatter.31.cloned.1.call-update) | async-done | bytes 1441808 | tf_op jit(solution)/shard_map/reduce_scatter | solution.py:200
  1082.4 44.1 %all-reduce.11 = (bf16[6144]{0:T(1024)(128)(2,1)S(1)}, bf16[1408]{0:T(1024)(128)(2,1)S(1)}) all-reduce(bf16[6144]{0:T(1024)(128)(2,1)S(1)} %dynamic-update-slice, bf16[1408]{0:T(1024)(128)(2,1)S(1)} %dynamic-update-slice.1), channel_id=1, replica_groups=mesh['dp'=8,'tensor'=4] {'dp','tensor'}, use_global_device_ids=true, to_apply=%add | all-reduce | flops 7552 | bytes 30208
  1126.6 55.6 %all-gather.33.cloned.1.call-done = bf16[1024,2,1408]{2,1,0:T(2,128)(2,1)} async-done(((bf16[256,2,1408]{2,1,0:T(2,128)(2,1)}), bf16[1024,2,1408]{2,1,0:T(2,128)(2,1)}) %all-gather.33.cloned.1.call-update) | async-done | bytes 5767184 | tf_op jit(solution)/shard_map/all_gather | solution.py:208
  1194.8 94.2 %all-gather.27.cloned.1.call-done = bf16[1024,2,1408]{2,1,0:T(2,128)(2,1)} async-done(((bf16[256,2,1408]{2,1,0:T(2,128)(2,1)}), bf16[1024,2,1408]{2,1,0:T(2,128)(2,1)}) %all-gather.27.cloned.1.call-update) | async-done | bytes 5767184 | tf_op jit(solution)/shard_map/all_gather | solution.py:188
  1301.8 27.9 all-gather.29.cloned.1.call-done
  1329.6 15.8 fusion.143
  1345.4 23.1 all-gather.31.cloned.1.call-done
  1368.5 24.0 convert_reduce_fusion
  1406.8 17.2 convolution_convert_fusion.4
  1428.7 80.1 %reduce-scatter.35.cloned.1.call-done = bf16[512,1408]{1,0:T(8,128)(2,1)} async-done(((bf16[2048,1408]{1,0:T(8,128)(2,1)}), bf16[512,1408]{1,0:T(8,128)(2,1)}) %reduce-scatter.35.cloned.1.call-update) | async-done | bytes 1441808 | tf_op jit(solution)/shard_map/reduce_scatter | solution.py:217
  1512.0 101.8 %reduce-scatter.33.cloned.1.call-done = bf16[512,1408]{1,0:T(8,128)(2,1)} async-done(((bf16[2048,1408]{1,0:T(8,128)(2,1)}), bf16[512,1408]{1,0:T(8,128)(2,1)}) %reduce-scatter.33.cloned.1.call-update) | async-done | bytes 1441808 | tf_op jit(solution)/shard_map/reduce_scatter | solution.py:200
  1648.7 80.0 %all-gather.35.cloned.1.call-done = bf16[1024,2,1408]{2,1,0:T(2,128)(2,1)} async-done(((bf16[256,2,1408]{2,1,0:T(2,128)(2,1)}), bf16[1024,2,1408]{2,1,0:T(2,128)(2,1)}) %all-gather.35.cloned.1.call-update) | async-done | bytes 5767184 | tf_op jit(solution)/shard_map/all_gather | solution.py:208
  1754.6 19.6 while.56
  1826.2 103.4 %reduce-scatter.37.cloned.1.call-done = bf16[512,1408]{1,0:T(8,128)(2,1)} async-done(((bf16[2048,1408]{1,0:T(8,128)(2,1)}), bf16[512,1408]{1,0:T(8,128)(2,1)}) %reduce-scatter.37.cloned.1.call-update) | async-done | bytes 1441808 | tf_op jit(solution)/shard_map/reduce_scatter | solution.py:217
  1989.2 56.0 %all-gather.37.cloned.1.call-done = bf16[1024,2,1408]{2,1,0:T(2,128)(2,1)} async-done(((bf16[256,2,1408]{2,1,0:T(2,128)(2,1)}), bf16[1024,2,1408]{2,1,0:T(2,128)(2,1)}) %all-gather.37.cloned.1.call-update) | async-done | bytes 5767184 | tf_op jit(solution)/shard_map/all_gather | solution.py:208
  2074.0 83.1 %while.57 = (s32[]{:T(128)}, f32[1024,2,4,88]{0,3,2,1:T(8,128)}, f32[1024,2,4,88]{0,3,2,1:T(8,128)}, f32[2,512,2,4,88]{1,4,3,2,0:T(8,128)}, bf16[2,512,2,4,88]{1...) while((s32[]{:T(128)}, f32[1024,2,4,88]{0,3,2,1:T(8,128)}, ...), condition=%wide.region_41.42_spmd.clone, body=%wide.region_39.41_spmd.clone.sunk | while | flops 3731615744 | bytes 220053840 | solution.py:109
  2186.9 18.0 copy.577
  2243.1 34.8 %multiply_reduce_fusion.6 = (f32[88]{0:T(128)}, f32[1024,2,4]{2,1,0:T(2,128)}, f32[1024,2,4]{2,1,0:T(2,128)}, f32[88]{0:T(128)}, f32[1024,2,4,88]{3,2,1,0:T(4,128)}) fusion(f32[1024,2,4]{2,1,0:T(2,128)S(1)} %copy-done.37, f32[1024,2,4,88]{3,2,1,0:T(4,128)} %reshape_squeeze.20, f32[1024,2,4]{2,1,0:T(2,128)S(1)} %copy-done.31, f32[88]{0:T(128)S(1)} %copy-done.155, ...), kind=kLoop, calls=%fused_computation.115 | loop fusion | flops 8634192 | bytes 12387360 | tf_op jit(solution)/shard_map/reduce_sum | solution.py:372
  2321.9 22.2 stack.117
  2374.5 14.5 convolution_convert_fusion.6
  2389.6 16.6 convolution_convert_fusion.5
  2479.6 13.7 fusion.83
  2540.6 48.4 %reduce-scatter.53.cloned.1.call-done = bf16[1536,176]{0,1:T(8,128)(2,1)} async-done(((bf16[1536,1408]{0,1:T(8,128)(2,1)}), bf16[1536,176]{0,1:T(8,128)(2,1)}) %reduce-scatter.53.cloned.1.call-update) | async-done | bytes 540688 | tf_op jit(solution)/shard_map/reduce_scatter | solution.py:422
  2595.8 31.8 reduce-scatter.49.cloned.1.call-done
  2629.2 37.1 %reduce-scatter.47.cloned.1.call-done = bf16[176,352]{1,0:T(8,128)(2,1)} async-done(((bf16[1408,352]{1,0:T(8,128)(2,1)}), bf16[176,352]{1,0:T(8,128)(2,1)}) %reduce-scatter.47.cloned.1.call-update) | async-done | bytes 123920 | tf_op jit(solution)/shard_map/reduce_scatter | solution.py:410
  2668.0 40.1 %reduce-scatter.57.cloned.1.call-done = bf16[128,704]{1,0:T(8,128)(2,1)} async-done(((bf16[1024,704]{1,0:T(8,128)(2,1)}), bf16[128,704]{1,0:T(8,128)(2,1)}) %reduce-scatter.57.cloned.1.call-update) | async-done | bytes 180240
  2709.9 30.7 reduce-scatter.41.cloned.1.call-done
  2742.6 37.4 %reduce-scatter.45.cloned.1.call-done = bf16[352,176]{0,1:T(8,128)(2,1)} async-done(((bf16[352,1408]{0,1:T(8,128)(2,1)}), bf16[352,176]{0,1:T(8,128)(2,1)}) %reduce-scatter.45.cloned.1.call-update) | async-done | bytes 123920 | tf_op jit(solution)/shard_map/reduce_scatter | solution.py:407
  2781.6 47.7 %reduce-scatter.43.cloned.1.call-done = bf16[176,3,352]{2,0,1:T(8,128)(2,1)} async-done(((bf16[1408,3,352]{2,0,1:T(8,128)(2,1)}), bf16[176,3,352]{2,0,1:T(8,128)(2,1)}) %reduce-scatter.43.cloned.1.call-update) | async-done | bytes 371728 | tf_op jit(solution)/shard_map/reduce_scatter | solution.py:404
  2837.0 218.3 %fusion = f32[48,1408]{1,0:T(8,128)S(1)} fusion(f32[1408,1408]{1,0:T(8,128)} %fusion.125), kind=kCustom, calls=%all-reduce-scatter | all-reduce-scatter fusion | flops 2162689 | bytes 8200192
  3090.5 19.7 collective-permute-done.2
  3113.4 270.9 %reduce-scatter.59.cloned.1.call-done = f32[88,1408]{1,0:T(8,128)} async-done(((f32[2816,1408]{1,0:T(8,128)}), f32[88,1408]{1,0:T(8,128)}) %reduce-scatter.59.cloned.1.call-update) | async-done | bytes 495632
  (873 shorter events, 1034.6 us)
Async XLA Ops:
  7.2 149.0 %all-gather.39.cloned.1.call-start = ((), (), s32[]{:S(2)}) async-start(), calls=%async_computation.40 | async-start | bytes 4460544 | tf_op jit(solution)/shard_map/all_gather | solution.py:140
  7.9 157.6 %all-gather.17.cloned.1.call-start = ((), (), s32[]{:S(2)}) async-start(), calls=%async_computation.16 | async-start | bytes 8177664 | tf_op jit(solution)/shard_map/all_gather | solution.py:139
  8.7 267.4 %all-gather.21.cloned.1.call-start = ((), (), s32[]{:S(2)}) async-start(), calls=%async_computation.18 | async-start | bytes 3649536 | tf_op jit(solution)/shard_map/all_gather | solution.py:158
  9.4 282.3 %all-gather.19.cloned.1.call-start = ((), (), s32[]{:S(2)}) async-start(), calls=%async_computation.17 | async-start | bytes 7208960 | tf_op jit(solution)/shard_map/all_gather | solution.py:188
  183.0 541.9 %reduce-scatter.29.cloned.1.call-start = ((), (), s32[]{:S(2)}) async-start(), calls=%async_computation.19 | async-start | bytes 7208960 | tf_op jit(solution)/shard_map/reduce_scatter | solution.py:200
  184.9 77.7 %copy-start.113 = (bf16[352,176]{0,1:T(8,128)(2,1)S(1)}, bf16[352,176]{0,1:T(8,128)(2,1)}, u32[]{:S(2)}) copy-start(bf16[352,176]{0,1:T(8,128)(2,1)} %param.39) | copy-start | bytes 371716
  185.3 96.8 %copy-start.86 = (f32[2,512,88]{1,0,2:T(2,128)}, f32[2,512,88]{1,0,2:T(2,128)S(1)}, u32[]{:S(2)}) copy-start(f32[2,512,88]{1,0,2:T(2,128)S(1)} %mul.807) | copy-start | bytes 1081348
  186.7 374.9 %copy-start.154 = (f32[88]{0:T(128)}, f32[88]{0:T(128)S(1)}, u32[]{:S(2)}) copy-start(f32[88]{0:T(128)S(1)} %get-tuple-element.780) | copy-start | bytes 1060
  482.0 79.6 %copy-start.36 = (f32[1024,2,4]{2,1,0:T(2,128)}, f32[1024,2,4]{2,1,0:T(2,128)S(1)}, u32[]{:S(2)}) copy-start(f32[1024,2,4]{2,1,0:T(2,128)S(1)} %add_rsqrt_fusion.1) | copy-start | bytes 98308
  485.5 91.1 %copy-start.104 = (f32[2,512,2,4]{1,3,2,0:T(4,128)}, f32[2,512,2,4]{1,3,2,0:T(4,128)S(1)}, u32[]{:S(2)}) copy-start(f32[2,512,2,4]{1,3,2,0:T(4,128)S(1)} %copy.521) | copy-start | bytes 98308
  621.4 103.4 %copy-start.15 = (f32[512,1408]{1,0:T(8,128)S(1)}, f32[512,1408]{1,0:T(8,128)}, u32[]{:S(2)}) copy-start(f32[512,1408]{1,0:T(8,128)} %copy-done.14) | copy-start | bytes 8650756
  621.4 103.4 %copy-start.148 = (f32[1408]{0:T(1024)S(1)}, f32[1408]{0:T(1024)}, u32[]{:S(2)}) copy-start(f32[1408]{0:T(1024)} %get-tuple-element.646) | copy-start | bytes 16900
  621.4 137.2 %all-gather.25.cloned.1.call-start = ((), (), s32[]{:S(2)}) async-start(), calls=%async_computation.21 | async-start | bytes 1622016 | tf_op jit(solution)/shard_map/all_gather | solution.py:161
  622.0 239.2 %all-gather.23.cloned.1.call-start = ((), (), s32[]{:S(2)}) async-start(), calls=%async_computation.20 | async-start | bytes 7208960 | tf_op jit(solution)/shard_map/all_gather | solution.py:188
  730.3 344.7 %reduce-scatter.31.cloned.1.call-start = ((), (), s32[]{:S(2)}) async-start(), calls=%async_computation.22 | async-start | bytes 7208960 | tf_op jit(solution)/shard_map/reduce_scatter | solution.py:200
  971.5 103.5 %copy-start.12 = (f32[512,1408]{1,0:T(8,128)S(1)}, f32[512,1408]{1,0:T(8,128)}, u32[]{:S(2)}) copy-start(f32[512,1408]{1,0:T(8,128)} %copy-done.11) | copy-start | bytes 8650756
  971.5 103.5 %copy-start.146 = (f32[1408]{0:T(1024)S(1)}, f32[1408]{0:T(1024)}, u32[]{:S(2)}) copy-start(f32[1408]{0:T(1024)} %get-tuple-element.644) | copy-start | bytes 16900
  971.5 210.6 %all-gather.33.cloned.1.call-start = ((), (), s32[]{:S(2)}) async-start(), calls=%async_computation.27 | async-start | bytes 7208960 | tf_op jit(solution)/shard_map/all_gather | solution.py:208
  972.3 316.8 %all-gather.27.cloned.1.call-start = ((), (), s32[]{:S(2)}) async-start(), calls=%async_computation.23 | async-start | bytes 7208960 | tf_op jit(solution)/shard_map/all_gather | solution.py:188
  1080.5 249.2 %all-gather.29.cloned.1.call-start = ((), (), s32[]{:S(2)}) async-start(), calls=%async_computation.24 | async-start | bytes 4866048 | tf_op jit(solution)/shard_map/all_gather | solution.py:163
  1081.2 287.3 %all-gather.31.cloned.1.call-start = ((), (), s32[]{:S(2)}) async-start(), calls=%async_computation.25 | async-start | bytes 4866048 | tf_op jit(solution)/shard_map/all_gather | solution.py:164
  1081.8 427.0 %reduce-scatter.35.cloned.1.call-start = ((), (), s32[]{:S(2)}) async-start(), calls=%async_computation.28 | async-start | bytes 7208960 | tf_op jit(solution)/shard_map/reduce_scatter | solution.py:217
  1126.5 280.3 %copy-start.165 = (f32[1536]{0:T(1024)}, f32[1536]{0:T(1024)S(1)}, u32[]{:S(2)}) copy-start(f32[1536]{0:T(1024)S(1)} %dynamic-slice_convert_fusion) | copy-start | bytes 18436
  1406.8 206.9 %reduce-scatter.33.cloned.1.call-start = ((), (), s32[]{:S(2)}) async-start(), calls=%async_computation.26 | async-start | bytes 7208960 | tf_op jit(solution)/shard_map/reduce_scatter | solution.py:200
  1424.1 84.7 %copy-start.18 = (f32[512,1408]{1,0:T(8,128)S(1)}, f32[512,1408]{1,0:T(8,128)}, u32[]{:S(2)}) copy-start(f32[512,1408]{1,0:T(8,128)} %copy-done.17) | copy-start | bytes 8650756
  1424.1 304.6 %all-gather.35.cloned.1.call-start = ((), (), s32[]{:S(2)}) async-start(), calls=%async_computation.29 | async-start | bytes 7208960 | tf_op jit(solution)/shard_map/all_gather | solution.py:208
  1624.1 305.5 %reduce-scatter.37.cloned.1.call-start = ((), (), s32[]{:S(2)}) async-start(), calls=%async_computation.30 | async-start | bytes 7208960 | tf_op jit(solution)/shard_map/reduce_scatter | solution.py:217
  1648.7 92.7 %copy-start.98 = (bf16[352,1408]{0,1:T(8,128)(2,1)S(1)}, bf16[352,1408]{0,1:T(8,128)(2,1)}, u32[]{:S(2)}) copy-start(bf16[352,1408]{0,1:T(8,128)(2,1)} %all_gather.74) | copy-start | bytes 2973700
  1826.1 103.5 %copy-start.13 = (f32[512,1408]{1,0:T(8,128)S(1)}, f32[512,1408]{1,0:T(8,128)}, u32[]{:S(2)}) copy-start(f32[512,1408]{1,0:T(8,128)} %copy-done.11) | copy-start | bytes 8650756
  1826.1 103.5 %copy-start.119 = (f32[1408]{0:T(1024)S(1)}, f32[1408]{0:T(1024)}, u32[]{:S(2)}) copy-start(f32[1408]{0:T(1024)} %get-tuple-element.653) | copy-start | bytes 16900
  1826.1 103.5 %copy-start.130 = (f32[512]{0:T(512)S(1)}, f32[512]{0:T(512)}, u32[]{:S(2)}) copy-start(f32[512]{0:T(512)} %copy-done.129) | copy-start | bytes 6148
  1826.1 103.5 %copy-start.138 = (f32[512]{0:T(512)S(1)}, f32[512]{0:T(512)}, u32[]{:S(2)}) copy-start(f32[512]{0:T(512)} %copy-done.137) | copy-start | bytes 6148
  1826.2 219.1 %all-gather.37.cloned.1.call-start = ((), (), s32[]{:S(2)}) async-start(), calls=%async_computation.31 | async-start | bytes 7208960 | tf_op jit(solution)/shard_map/all_gather | solution.py:208
  1940.7 558.2 %reduce-scatter.39.cloned.1.call-start = ((), (), s32[]{:S(2)}) async-start(), calls=%async_computation.32 | async-start | bytes 7208960 | tf_op jit(solution)/shard_map/reduce_scatter | solution.py:217
  2374.4 164.0 %reduce-scatter.51.cloned.1.call-start = ((), (), s32[]{:S(2)}) async-start(), calls=%async_computation.38 | async-start | bytes 4866048 | tf_op jit(solution)/shard_map/reduce_scatter | solution.py:419
  2389.0 200.0 %reduce-scatter.53.cloned.1.call-start = ((), (), s32[]{:S(2)}) async-start(), calls=%async_computation.39 | async-start | bytes 4866048 | tf_op jit(solution)/shard_map/reduce_scatter | solution.py:422
  2406.3 221.3 %reduce-scatter.49.cloned.1.call-start = ((), (), s32[]{:S(2)}) async-start(), calls=%async_computation.37 | async-start | bytes 1216512 | tf_op jit(solution)/shard_map/reduce_scatter | solution.py:416
  2418.0 248.4 %reduce-scatter.47.cloned.1.call-start = ((), (), s32[]{:S(2)}) async-start(), calls=%async_computation.36 | async-start | bytes 1216512 | tf_op jit(solution)/shard_map/reduce_scatter | solution.py:410
  2437.4 270.6 %reduce-scatter.57.cloned.1.call-start = ((), (), s32[]{:S(2)}) async-start(), calls=%async_computation.42 | async-start | bytes 1769472
  2451.8 288.8 %reduce-scatter.41.cloned.1.call-start = ((), (), s32[]{:S(2)}) async-start(), calls=%async_computation.33 | async-start | bytes 1720320 | tf_op jit(solution)/shard_map/reduce_scatter | solution.py:508
  2459.4 320.6 %reduce-scatter.45.cloned.1.call-start = ((), (), s32[]{:S(2)}) async-start(), calls=%async_computation.35 | async-start | bytes 1216512 | tf_op jit(solution)/shard_map/reduce_scatter | solution.py:407
  2466.9 362.4 %reduce-scatter.43.cloned.1.call-start = ((), (), s32[]{:S(2)}) async-start(), calls=%async_computation.34 | async-start | bytes 3649536 | tf_op jit(solution)/shard_map/reduce_scatter | solution.py:404
  2493.5 588.7 %reduce-scatter.55.cloned.1.call-start = ((), (), s32[]{:S(2)}) async-start(), calls=%async_computation.41 | async-start | bytes 450560
  2525.7 558.0 %all-reduce.14.cloned.1.call-start = ((), (), s32[]{:S(2)}) async-start(), calls=%async_computation.44 | async-start | bytes 434176
  2527.9 856.4 %reduce-scatter.59.cloned.1.call-start = ((), (), s32[]{:S(2)}) async-start(), calls=%async_computation.43 | async-start | bytes 16355328
  3056.0 54.2 %collective-permute-start.1 = (f32[48,1408]{1,0:T(8,128)S(1)}, f32[48,1408]{1,0:T(8,128)S(1)}, u32[]{:S(2)}, u32[]{:S(2)}) collective-permute-start(f32[48,1408]{1,0:T(8,128)S(1)} %fusion), channel_id=1, source_target_pairs={{0,2},{1,3},{2,4},{3,5},{4,6},{5,7},{6,8},{7,9},{8,10},{9,11},{10,... | collective-permute-start | bytes 811016
  3062.6 48.5 %collective-permute-start = (f32[48,1408]{1,0:T(8,128)S(1)}, f32[48,1408]{1,0:T(8,128)}, u32[]{:S(2)}, u32[]{:S(2)}) collective-permute-start(f32[48,1408]{1,0:T(8,128)S(1)} %fusion), channel_id=1, source_target_pairs={{0,1},{1,2},{2,3},{3,4},{4,5},{5,6},{6,7},{7,8},{8,9},{9,10},{10,1... | collective-permute-start | bytes 811016
  3078.9 31.3 collective-permute-start.2
  (190 other events, 1234.1 us)
Sparse Core Ops, SparseCore 0:
  10.8 63.7 all-gather.38
  77.5 74.2 all-gather.16
  153.7 31.2 all-gather.20
  187.0 104.6 all-gather.18
  621.6 103.2 reduce-scatter.28
  726.6 28.8 all-gather.24
  757.7 103.5 all-gather.22
  971.7 103.3 reduce-scatter.30
  1076.6 105.4 all-gather.32
  1184.1 104.8 all-gather.26
  1290.9 38.6 all-gather.28
  1331.4 37.1 all-gather.30
  1406.9 101.8 reduce-scatter.34
  1510.9 102.7 reduce-scatter.32
  1624.3 104.3 all-gather.34
  1826.3 103.3 reduce-scatter.36
  1940.8 104.4 all-gather.36
  2374.6 103.3 reduce-scatter.38
  2481.3 52.3 reduce-scatter.50
  2537.0 51.9 reduce-scatter.52
  2592.2 35.3 reduce-scatter.48
  2630.9 35.4 reduce-scatter.46
  2669.6 38.3 reduce-scatter.56
  2710.2 30.3 reduce-scatter.40
  2743.8 36.1 reduce-scatter.44
  2783.3 45.9 reduce-scatter.42
  2831.4 17.4 reduce-scatter.54
  2855.9 137.1 all-reduce.13
  2996.0 388.1 reduce-scatter.58
where the time goes:
time: 3410 us; the launch traced here: 3390 us
  waiting for transfers between devices  1490 us (44%)
  local copies, waits for them, and re-layouts  669 us (20%)
  blocking collectives  506 us (15%)
  other arithmetic  367 us (11%)
  matrix products  329 us (10%)
    unnamed x36, waiting for transfers between devices  336 us
    reduce_scatter x3, waiting for transfers between devices, scatter_rows(): lax.psum_scatter(partial_term(jnp.int32(0), local_rows * lax.axis_size('t...  307 us
    unnamed x2, blocking collectives  262 us
    all_gather x3, waiting for transfers between devices, gather_grads(): lax.all_gather(local_part.reshape(local_shape), 'tensor', axis=0, tiled=T...  192 us
    all_gather x3, waiting for transfers between devices, gather_rows(): return lax.all_gather(local_part, 'tensor', axis=0, tiled=True)  187 us
    reduce_scatter x3, waiting for transfers between devices, scatter_grads(): lax.psum_scatter(partial_term(jnp.int32(0), local_rows * lax.axis_size('t...  183 us
    reduce_sum x8, other arithmetic, normalize(): jnp.mean(centred * centred, axis=-1, keepdims=True) + EPSILON  103 us
    dot_general x8, matrix products, contract_first(): lax.dot_general(left, right, (((0,), (0,)), ((), ())), preferred_element_...  79.7 us
  transfers between devices with their start and end apart: 32, of which 23 were waited for; matrix products, arithmetic and copies ran while one was open for 19% of the time, Pallas kernels for 0%

commit v1 on v0

v1 whole, which is shorter than its diff:
```python
import functools

import jax
import jax.numpy as jnp
from jax import lax
from jax.experimental import pallas as pl
from jax.experimental.pallas import tpu as pltpu
from jax.sharding import Mesh, PartitionSpec as P

GRID_W = 32
EPSILON = 1e-06
THETA = 10000.0
F32 = jnp.float32
BF16 = jnp.bfloat16
VMEM_LIMIT = 62 * 1024 * 1024
MLP_CHUNKS = 3
QUERY_BLOCK = 512


def bits_of(size):
    return [1 << i for i in range(size.bit_length() - 1)]


def swap(value, axis, size, mask):
    return lax.ppermute(value, axis, [(i, i ^ mask) for i in range(size)])


def dot(left, right, left_dim, right_dim):
    return lax.dot_general(
        left, right, (((left_dim,), (right_dim,)), ((), ())), preferred_element_type=F32
    )


def params(count=1):
    return pltpu.CompilerParams(
        dimension_semantics=("arbitrary",) * count, vmem_limit_bytes=VMEM_LIMIT
    )


def whole(shape):
    zeros = (0,) * len(shape)
    return pl.BlockSpec(shape, lambda *_: zeros, pipeline_mode=pl.Buffered(1))


def per_step(shape):
    rest = (0,) * (len(shape) - 1)
    return pl.BlockSpec((1,) + tuple(shape[1:]), lambda i, *_: (i,) + rest)


def shape_of(shape, dtype):
    return jax.ShapeDtypeStruct(shape, dtype)


def head_norm(values):
    width = values.shape[-1]
    centred = values - jnp.sum(values, axis=-1, keepdims=True) * (1.0 / width)
    inverse = lax.rsqrt(
        jnp.sum(centred * centred, axis=-1, keepdims=True) * (1.0 / width) + EPSILON
    )
    return centred * inverse, inverse


def head_norm_back(grad, hat, inverse, gain):
    scale = 1.0 / grad.shape[-1]
    scaled = grad * gain
    first = jnp.sum(scaled, axis=-1, keepdims=True) * scale
    second = jnp.sum(scaled * hat, axis=-1, keepdims=True) * scale
    return inverse * (scaled - first - hat * second)


def half_turn(values):
    quarter = values.shape[-1] // 4
    part = [values[:, i * quarter : (i + 1) * quarter] for i in range(4)]
    return jnp.concatenate([part[1], part[0], part[3], part[2]], axis=1)


def assemble(target, pieces, chip, rows):
    for k, piece in enumerate(pieces):
        start = pl.multiple_of((chip ^ k) * rows, 16)
        target[pl.ds(start, rows), :] = piece[0]


def scatter_pieces(source, pieces, chip, rows):
    for k, piece in enumerate(pieces):
        start = pl.multiple_of((chip ^ k) * rows, 16)
        piece[0] = source[pl.ds(start, rows), :]


def column_sum(values):
    return jnp.sum(values, axis=0, keepdims=True)


def self_forward_kernel(counts, chip_ref, *refs):
    chips, heads, size, own = counts
    refs = list(refs)
    take = lambda n: [refs.pop(0) for _ in range(n)]
    (x_ref,) = take(1)
    proj = take(chips)
    (bias_ref,) = take(1)
    comb = take(chips)
    gains, shifts, cosine, sine = take(4)
    low_ref, pre_ref, att_ref, lse_ref, own_ref, other_ref = take(6)
    wp, wc, acc = take(3)
    step = pl.program_id(0)
    chip = chip_ref[0]
    assemble(wp, proj, chip, proj[0].shape[1])
    assemble(wc, comb, chip, comb[0].shape[1])
    width = heads * size
    packed = dot(x_ref[...], wp[...], 1, 0) + bias_ref[0]
    pre_ref[0] = packed[:, : 2 * width].astype(BF16)
    value_low = packed[:, 2 * width :].astype(BF16)
    length = packed.shape[0]
    block = min(QUERY_BLOCK, length)
    cos, sin = cosine[...], sine[...]
    queries, keys, mixes, logs = [], [], [], []
    for h in range(heads):
        part = packed[:, h * size : (h + 1) * size]
        hat, _ = head_norm(part)
        turned = hat * gains[0:1, :] + shifts[0:1, :]
        query = ((turned * cos + half_turn(turned) * sin) * (size**-0.5)).astype(BF16)
        part = packed[:, width + h * size : width + (h + 1) * size]
        hat, _ = head_norm(part)
        turned = hat * gains[1:2, :] + shifts[1:2, :]
        key = (turned * cos + half_turn(turned) * sin).astype(BF16)
        value = value_low[:, h * size : (h + 1) * size]
        queries.append(query)
        keys.append(key)
        parts, sums = [], []
        for b in range(length // block):
            scores = dot(key, query[b * block : (b + 1) * block], 1, 1)
            top = jnp.max(scores, axis=0, keepdims=True)
            power = jnp.exp(scores - top)
            total = jnp.sum(power, axis=0, keepdims=True)
            shares = (power * (1.0 / total)).astype(BF16)
            parts.append(jnp.transpose(dot(value, shares, 0, 0)))
            sums.append(top + jnp.log(total))
        mixes.append(jnp.concatenate(parts, axis=0))
        logs.append(jnp.concatenate(sums, axis=1))
    low_ref[0] = jnp.concatenate(queries + keys + [value_low], axis=1)
    att = jnp.concatenate(mixes, axis=1).astype(BF16)
    att_ref[0] = att
    lse_ref[0] = jnp.concatenate(logs, axis=0)
    term = dot(att, wc[...], 1, 1)

    @pl.when(step == 0)
    def _():
        acc[...] = term

    @pl.when(step > 0)
    def _():
        acc[...] += term

    @pl.when(step == pl.num_programs(0) - 1)
    def _():
        own_ref[...] = acc[:own, :]
        other_ref[...] = acc[own:, :].astype(BF16)


def self_forward(chip, x, proj, bias, comb, gains, shifts, cosine, sine, own):
    length, width = x.shape
    groups, rows, cols = proj[0].shape
    size = gains.shape[1]
    heads = cols // (3 * size)
    chips = len(proj)
    small = heads * size
    return pl.pallas_call(
        functools.partial(self_forward_kernel, (chips, heads, size, own)),
        grid_spec=pltpu.PrefetchScalarGridSpec(
            num_scalar_prefetch=1,
            grid=(groups,),
            in_specs=[whole(x.shape)]
            + [per_step(p.shape) for p in proj]
            + [per_step(bias.shape)]
            + [per_step(p.shape) for p in comb]
            + [whole(gains.shape), whole(shifts.shape), whole(cosine.shape), whole(sine.shape)],
            out_specs=[
                per_step((groups, length, cols)),
                per_step((groups, length, 2 * small)),
                per_step((groups, length, small)),
                per_step((groups, heads, length)),
                whole((own, width)),
                whole((length - own, width)),
            ],
            scratch_shapes=[
                pltpu.VMEM((rows * chips, cols), BF16),
                pltpu.VMEM((rows * chips, small), BF16),
                pltpu.VMEM((length, width), F32),
            ],
        ),
        out_shape=[
            shape_of((groups, length, cols), BF16),
            shape_of((groups, length, 2 * small), BF16),
            shape_of((groups, length, small), BF16),
            shape_of((groups, heads, length), F32),
            shape_of((own, width), F32),
            shape_of((length - own, width), BF16),
        ],
        compiler_params=params(),
        name="self_forward",
    )(chip, x, *proj, bias, *comb, gains, shifts, cosine, sine)


def attention_back(query, key, value, out_grad, logs, block, limit=None):
    length = query.shape[0]
    key_grad, value_grad, query_parts = None, None, []
    for b in range(length // block):
        rows = slice(b * block, (b + 1) * block)
        query_part, grad_part = query[rows], out_grad[rows]
        scores = dot(key, query_part, 1, 1)
        shares = jnp.exp(scores - logs[:, rows])
        if limit is not None:
            index = lax.broadcasted_iota(jnp.int32, shares.shape, 0)
            shares = jnp.where(index < limit, shares, 0.0)
        share_grad = dot(value, grad_part, 1, 1)
        inner = jnp.sum(shares * share_grad, axis=0, keepdims=True)
        score_grad = (shares * (share_grad - inner)).astype(BF16)
        query_parts.append(jnp.transpose(dot(key, score_grad, 0, 0)))
        key_term = dot(score_grad, query_part, 1, 0)
        value_term = dot(shares.astype(BF16), grad_part, 1, 0)
        key_grad = key_term if b == 0 else key_grad + key_term
        value_grad = value_term if b == 0 else value_grad + value_term
    return jnp.concatenate(query_parts, axis=0), key_grad, value_grad


def self_backward_kernel(counts, chip_ref, *refs):
    chips, heads, size, own = counts
    refs = list(refs)
    take = lambda n: [refs.pop(0) for _ in range(n)]
    x_ref, grad_ref = take(2)
    proj = take(chips)
    comb = take(chips)
    low_ref, pre_ref, att_ref, lse_ref = take(4)
    gains, cosine, sine = take(3)
    proj_out = take(chips)
    comb_out = take(chips)
    own_ref, other_ref, column_ref, head_ref = take(4)
    wp, wc, acc, grad_t, x_t = take(5)
    step = pl.program_id(0)
    chip = chip_ref[0]
    rows = proj[0].shape[1]
    assemble(wp, proj, chip, rows)
    assemble(wc, comb, chip, rows)
    width = heads * size
    scale = size**-0.5

    @pl.when(step == 0)
    def _():
        grad_t[...] = jnp.transpose(grad_ref[...])
        x_t[...] = jnp.transpose(x_ref[...])

    out_grad = dot(grad_ref[...], wc[...], 1, 0).astype(BF16)
    wc[...] = dot(grad_t[...], att_ref[0], 1, 0).astype(BF16)
    scatter_pieces(wc, comb_out, chip, rows)
    cos, sin = cosine[...], sine[...]
    block = min(QUERY_BLOCK, out_grad.shape[0])
    query_grads, key_grads, value_grads = [], [], []
    sums = [None] * 4
    for h in range(heads):
        cut = lambda ref, part: ref[0, :, part * width + h * size : part * width + (h + 1) * size]
        query, key, value = cut(low_ref, 0), cut(low_ref, 1), cut(low_ref, 2)
        dq, dk, dv = attention_back(
            query, key, value, out_grad[:, h * size : (h + 1) * size], lse_ref[0, h : h + 1, :], block
        )
        dq = dq * scale
        dq = dq * cos - half_turn(dq) * sin
        dk = dk * cos - half_turn(dk) * sin
        q_hat, q_inverse = head_norm(cut(pre_ref, 0).astype(F32))
        k_hat, k_inverse = head_norm(cut(pre_ref, 1).astype(F32))
        terms = [column_sum(dq * q_hat), column_sum(dk * k_hat), column_sum(dq), column_sum(dk)]
        sums = terms if h == 0 else [s + t for s, t in zip(sums, terms)]
        query_grads.append(head_norm_back(dq, q_hat, q_inverse, gains[0:1, :]))
        key_grads.append(head_norm_back(dk, k_hat, k_inverse, gains[1:2, :]))
        value_grads.append(dv)
    packed = jnp.concatenate(query_grads + key_grads + value_grads, axis=1).astype(BF16)
    column_ref[0] = column_sum(packed.astype(F32))
    term = dot(packed, wp[...], 1, 1)
    wp[...] = dot(x_t[...], packed, 1, 0).astype(BF16)
    scatter_pieces(wp, proj_out, chip, rows)
    head_sums = jnp.concatenate(sums, axis=0)

    @pl.when(step == 0)
    def _():
        acc[...] = term
        head_ref[...] = head_sums

    @pl.when(step > 0)
    def _():
        acc[...] += term
        head_ref[...] += head_sums

    @pl.when(step == pl.num_programs(0) - 1)
    def _():
        own_ref[...] = acc[:own, :]
        other_ref[...] = acc[own:, :].astype(BF16)


def self_backward(chip, x, grad, proj, comb, low, pre, att, lse, gains, cosine, sine, own):
    length, width = x.shape
    groups, rows, cols = proj[0].shape
    size = gains.shape[1]
    heads = cols // (3 * size)
    chips = len(proj)
    small = heads * size
    out = pl.pallas_call(
        functools.partial(self_backward_kernel, (chips, heads, size, own)),
        grid_spec=pltpu.PrefetchScalarGridSpec(
            num_scalar_prefetch=1,
            grid=(groups,),
            in_specs=[whole(x.shape), whole(grad.shape)]
            + [per_step(p.shape) for p in proj]
            + [per_step(p.shape) for p in comb]
            + [per_step(v.shape) for v in (low, pre, att, lse)]
            + [whole(gains.shape), whole(cosine.shape), whole(sine.shape)],
            out_specs=[per_step(p.shape) for p in proj]
            + [per_step(p.shape) for p in comb]
            + [
                whole((own, width)),
                whole((length - own, width)),
                per_step((groups, 1, cols)),
                whole((4, size)),
            ],
            scratch_shapes=[
                pltpu.VMEM((rows * chips, cols), BF16),
                pltpu.VMEM((rows * chips, small), BF16),
                pltpu.VMEM((length, width), F32),
                pltpu.VMEM((width, length), BF16),
                pltpu.VMEM((width, length), BF16),
            ],
        ),
        out_shape=[shape_of(p.shape, BF16) for p in proj]
        + [shape_of(p.shape, BF16) for p in comb]
        + [
            shape_of((own, width), F32),
            shape_of((length - own, width), BF16),
            shape_of((groups, 1, cols), F32),
            shape_of((4, size), F32),
        ],
        compiler_params=params(),
        name="self_backward",
    )(chip, x, grad, *proj, *comb, low, pre, att, lse, gains, cosine, sine)
    return out[:chips], out[chips : 2 * chips], *out[2 * chips :]


def cross_forward_kernel(counts, chip_ref, *refs):
    chips, heads, size, own, limit = counts
    refs = list(refs)
    take = lambda n: [refs.pop(0) for _ in range(n)]
    x_ref, text_ref = take(2)
    query_w = take(chips)
    memory_w = take(chips)
    blend = take(chips)
    bias_ref, memory_bias, gains, shifts = take(4)
    low_ref, pre_ref, memory_ref, memory_pre, att_ref, lse_ref, own_ref, other_ref = take(8)
    wq, wm, wb, acc = take(4)
    step = pl.program_id(0)
    chip = chip_ref[0]
    assemble(wq, query_w, chip, query_w[0].shape[1])
    assemble(wm, memory_w, chip, memory_w[0].shape[1])
    assemble(wb, blend, chip, blend[0].shape[1])
    width = heads * size
    pre = dot(x_ref[...], wq[...], 1, 0) + bias_ref[0]
    memory = dot(text_ref[...], wm[...], 1, 0) + memory_bias[0]
    pre_ref[0] = pre.astype(BF16)
    memory_pre[0] = memory[:, :width].astype(BF16)
    value_low = memory[:, width:].astype(BF16)
    length = pre.shape[0]
    block = min(QUERY_BLOCK, length)
    queries, keys, mixes, logs = [], [], [], []
    for h in range(heads):
        cols = slice(h * size, (h + 1) * size)
        hat, _ = head_norm(pre[:, cols])
        query = ((hat * gains[2:3, :] + shifts[2:3, :]) * (size**-0.5)).astype(BF16)
        hat, _ = head_norm(memory[:, cols])
        key = (hat * gains[3:4, :]).astype(BF16)
        value = value_low[:, cols]
        queries.append(query)
        keys.append(key)
        parts, sums = [], []
        for b in range(length // block):
            scores = dot(key, query[b * block : (b + 1) * block], 1, 1)
            index = lax.broadcasted_iota(jnp.int32, scores.shape, 0)
            scores = jnp.where(index < limit, scores, -jnp.inf)
            top = jnp.max(scores, axis=0, keepdims=True)
            power = jnp.exp(scores - top)
            total = jnp.sum(power, axis=0, keepdims=True)
            shares = (power * (1.0 / total)).astype(BF16)
            parts.append(jnp.transpose(dot(value, shares, 0, 0)))
            sums.append(top + jnp.log(total))
        mixes.append(jnp.concatenate(parts, axis=0))
        logs.append(jnp.concatenate(sums, axis=1))
    low_ref[0] = jnp.concatenate(queries, axis=1)
    memory_ref[0] = jnp.concatenate(keys + [value_low], axis=1)
    att = jnp.concatenate(mixes, axis=1).astype(BF16)
    att_ref[0] = att
    lse_ref[0] = jnp.concatenate(logs, axis=0)
    term = dot(att, wb[...], 1, 1)

    @pl.when(step == 0)
    def _():
        acc[...] = term

    @pl.when(step > 0)
    def _():
        acc[...] += term

    @pl.when(step == pl.num_programs(0) - 1)
    def _():
        own_ref[...] = acc[:own, :]
        other_ref[...] = acc[own:, :].astype(BF16)


def cross_forward(chip, x, text, query_w, memory_w, blend, bias, memory_bias, gains, shifts, own, limit):
    length, width = x.shape
    groups, rows, small = query_w[0].shape
    text_rows = text.shape[0]
    memory_rows = memory_w[0].shape[1]
    size = gains.shape[1]
    heads = small // size
    chips = len(query_w)
    saved = [
        ((groups, length, small), BF16),
        ((groups, length, small), BF16),
        ((groups, text_rows, 2 * small), BF16),
        ((groups, text_rows, small), BF16),
        ((groups, length, small), BF16),
        ((groups, heads, length), F32),
    ]
    return pl.pallas_call(
        functools.partial(cross_forward_kernel, (chips, heads, size, own, limit)),
        grid_spec=pltpu.PrefetchScalarGridSpec(
            num_scalar_prefetch=1,
            grid=(groups,),
            in_specs=[whole(x.shape), whole(text.shape)]
            + [per_step(p.shape) for p in (*query_w, *memory_w, *blend)]
            + [per_step(bias.shape), per_step(memory_bias.shape), whole(gains.shape), whole(shifts.shape)],
            out_specs=[per_step(s) for s, _ in saved]
            + [whole((own, width)), whole((length - own, width))],
            scratch_shapes=[
                pltpu.VMEM((rows * chips, small), BF16),
                pltpu.VMEM((memory_rows * chips, 2 * small), BF16),
                pltpu.VMEM((rows * chips, small), BF16),
                pltpu.VMEM((length, width), F32),
            ],
        ),
        out_shape=[shape_of(*s) for s in saved]
        + [shape_of((own, width), F32), shape_of((length - own, width), BF16)],
        compiler_params=params(),
        name="cross_forward",
    )(chip, x, text, *query_w, *memory_w, *blend, bias, memory_bias, gains, shifts)


def cross_backward_kernel(counts, chip_ref, *refs):
    chips, heads, size, own, limit = counts
    refs = list(refs)
    take = lambda n: [refs.pop(0) for _ in range(n)]
    x_ref, grad_ref, text_ref = take(3)
    query_w = take(chips)
    memory_w = take(chips)
    blend = take(chips)
    low_ref, pre_ref, memory_ref, memory_pre, att_ref, lse_ref = take(6)
    (gains,) = take(1)
    query_out = take(chips)
    memory_out = take(chips)
    blend_out = take(chips)
    own_ref, other_ref, text_out, column_ref, memory_column, head_ref = take(6)
    wq, wm, wb, acc, grad_t, x_t, text_t = take(7)
    step = pl.program_id(0)
    chip = chip_ref[0]
    rows, memory_rows = query_w[0].shape[1], memory_w[0].shape[1]
    assemble(wq, query_w, chip, rows)
    assemble(wm, memory_w, chip, memory_rows)
    assemble(wb, blend, chip, rows)
    width = heads * size
    scale = size**-0.5

    @pl.when(step == 0)
    def _():
        grad_t[...] = jnp.transpose(grad_ref[...])
        x_t[...] = jnp.transpose(x_ref[...])
        text_t[...] = jnp.transpose(text_ref[...])

    out_grad = dot(grad_ref[...], wb[...], 1, 0).astype(BF16)
    wb[...] = dot(grad_t[...], att_ref[0], 1, 0).astype(BF16)
    scatter_pieces(wb, blend_out, chip, rows)
    block = min(QUERY_BLOCK, out_grad.shape[0])
    query_grads, key_grads, value_grads = [], [], []
    sums = [None] * 3
    for h in range(heads):
        cols = slice(h * size, (h + 1) * size)
        query = low_ref[0, :, cols]
        key = memory_ref[0, :, cols]
        value = memory_ref[0, :, width + h * size : width + (h + 1) * size]
        dq, dk, dv = attention_back(
            query, key, value, out_grad[:, cols], lse_ref[0, h : h + 1, :], block, limit
        )
        dq = dq * scale
        q_hat, q_inverse = head_norm(pre_ref[0, :, cols].astype(F32))
        k_hat, k_inverse = head_norm(memory_pre[0, :, cols].astype(F32))
        terms = [column_sum(dq * q_hat), column_sum(dk * k_hat), column_sum(dq)]
        sums = terms if h == 0 else [s + t for s, t in zip(sums, terms)]
        query_grads.append(head_norm_back(dq, q_hat, q_inverse, gains[2:3, :]))
        key_grads.append(head_norm_back(dk, k_hat, k_inverse, gains[3:4, :]))
        value_grads.append(dv)
    packed = jnp.concatenate(query_grads, axis=1).astype(BF16)
    memory_grad = jnp.concatenate(key_grads + value_grads, axis=1).astype(BF16)
    column_ref[0] = column_sum(packed.astype(F32))
    memory_column[0] = column_sum(memory_grad.astype(F32))
    term = dot(packed, wq[...], 1, 1)
    text_term = dot(memory_grad, wm[...], 1, 1)
    wq[...] = dot(x_t[...], packed, 1, 0).astype(BF16)
    scatter_pieces(wq, query_out, chip, rows)
    wm[...] = dot(text_t[...], memory_grad, 1, 0).astype(BF16)
    scatter_pieces(wm, memory_out, chip, memory_rows)
    head_sums = jnp.concatenate(sums, axis=0)

    @pl.when(step == 0)
    def _():
        acc[...] = term
        text_out[...] = text_term
        head_ref[...] = head_sums

    @pl.when(step > 0)
    def _():
        acc[...] += term
        text_out[...] += text_term
        head_ref[...] += head_sums

    @pl.when(step == pl.num_programs(0) - 1)
    def _():
        own_ref[...] = acc[:own, :]
        other_ref[...] = acc[own:, :].astype(BF16)


def cross_backward(
    chip, x, grad, text, query_w, memory_w, blend, low, pre, memory, memory_pre, att, lse, gains, own, limit
):
    length, width = x.shape
    groups, rows, small = query_w[0].shape
    memory_rows = memory_w[0].shape[1]
    size = gains.shape[1]
    heads = small // size
    chips = len(query_w)
    pieces = (*query_w, *memory_w, *blend)
    tail = [
        ((own, width), F32, False),
        ((length - own, width), BF16, False),
        (text.shape, F32, False),
        ((groups, 1, small), F32, True),
        ((groups, 1, 2 * small), F32, True),
        ((3, size), F32, False),
    ]
    out = pl.pallas_call(
        functools.partial(cross_backward_kernel, (chips, heads, size, own, limit)),
        grid_spec=pltpu.PrefetchScalarGridSpec(
            num_scalar_prefetch=1,
            grid=(groups,),
            in_specs=[whole(x.shape), whole(grad.shape), whole(text.shape)]
            + [per_step(p.shape) for p in pieces]
            + [per_step(v.shape) for v in (low, pre, memory, memory_pre, att, lse)]
            + [whole(gains.shape)],
            out_specs=[per_step(p.shape) for p in pieces]
            + [per_step(s) if stepped else whole(s) for s, _, stepped in tail],
            scratch_shapes=[
                pltpu.VMEM((rows * chips, small), BF16),
                pltpu.VMEM((memory_rows * chips, 2 * small), BF16),
                pltpu.VMEM((rows * chips, small), BF16),
                pltpu.VMEM((length, width), F32),
                pltpu.VMEM((width, length), BF16),
                pltpu.VMEM((width, length), BF16),
                pltpu.VMEM((text.shape[1], text.shape[0]), BF16),
            ],
        ),
        out_shape=[shape_of(p.shape, BF16) for p in pieces] + [shape_of(s, d) for s, d, _ in tail],
        compiler_params=params(),
        name="cross_backward",
    )(chip, x, grad, text, *pieces, low, pre, memory, memory_pre, att, lse, gains)
    return out[:chips], out[chips : 2 * chips], out[2 * chips : 3 * chips], *out[3 * chips :]


def mlp_kernel(counts, chip_ref, *refs):
    chips, own = counts
    refs = list(refs)
    take = lambda n: [refs.pop(0) for _ in range(n)]
    x_ref, cot_ref, x_t, cot_t = take(4)
    weights = take(chips)
    (bias_ref,) = take(1)
    grads = take(chips)
    out_own, out_other, back_own, back_other, hidden_ref = take(5)
    w, acc, back = take(3)
    step = pl.program_id(0)
    chip = chip_ref[0]
    rows = weights[0].shape[1]
    assemble(w, weights, chip, rows)
    tile = w.shape[1] // 2
    hidden = dot(x_ref[...], w[:, :tile], 1, 0) + bias_ref[0]
    square = hidden * hidden
    inner = 0.7978845608028654 * hidden * (1.0 + 0.044715 * square)
    curve = jnp.tanh(inner)
    active = (0.5 * hidden * (1.0 + curve)).astype(BF16)
    slope = 0.5 * (1.0 + curve) + 0.5 * hidden * (1.0 - curve * curve) * (
        0.7978845608028654 * (1.0 + 3 * 0.044715 * square)
    )
    hidden_grad = dot(cot_ref[...], w[:, tile:], 1, 0) * slope
    hidden_grad = hidden_grad.astype(BF16)
    hidden_ref[0] = column_sum(hidden_grad.astype(F32))
    out_term = dot(active, w[:, tile:], 1, 1)
    back_term = dot(hidden_grad, w[:, :tile], 1, 1)

    @pl.when(step == 0)
    def _():
        acc[...] = out_term
        back[...] = back_term

    @pl.when(step > 0)
    def _():
        acc[...] += out_term
        back[...] += back_term

    w[:, :tile] = dot(x_t[...], hidden_grad, 1, 0).astype(BF16)
    w[:, tile:] = dot(cot_t[...], active, 1, 0).astype(BF16)
    scatter_pieces(w, grads, chip, rows)

    @pl.when(step == pl.num_programs(0) - 1)
    def _():
        out_own[...] = acc[:own, :]
        out_other[...] = acc[own:, :].astype(BF16)
        back_own[...] = back[:own, :]
        back_other[...] = back[own:, :].astype(BF16)


def mlp(chip, x, cot, x_t, cot_t, weights, bias, own):
    length, width = x.shape
    groups, rows, cols = weights[0].shape
    chips = len(weights)
    tail = [((own, width), F32), ((length - own, width), BF16)] * 2
    out = pl.pallas_call(
        functools.partial(mlp_kernel, (chips, own)),
        grid_spec=pltpu.PrefetchScalarGridSpec(
            num_scalar_prefetch=1,
            grid=(groups,),
            in_specs=[whole(v.shape) for v in (x, cot, x_t, cot_t)]
            + [per_step(p.shape) for p in weights]
            + [per_step(bias.shape)],
            out_specs=[per_step(p.shape) for p in weights]
            + [whole(s) for s, _ in tail]
            + [per_step(bias.shape)],
            scratch_shapes=[
                pltpu.VMEM((rows * chips, cols), BF16),
                pltpu.VMEM((length, width), F32),
                pltpu.VMEM((length, width), F32),
            ],
        ),
        out_shape=[shape_of(p.shape, BF16) for p in weights]
        + [shape_of(*s) for s in tail]
        + [shape_of(bias.shape, F32)],
        compiler_params=params(),
        name="mlp",
    )(chip, x, cot, x_t, cot_t, *weights, bias)
    return out[:chips], *out[chips:]


def row_spec(block, width):
    return pl.BlockSpec((block, width), lambda i, *_: (i, 0))


def merge_kernel(count, index_ref, *refs):
    refs = list(refs)
    take = lambda n: [refs.pop(0) for _ in range(n)]
    latent_ref, skip_ref = take(2)
    pieces = take(count)
    gains, biases = take(2)
    out_ref, merger_ref = take(2)

    @pl.when(pl.program_id(0) == 0)
    def _():
        rows = pieces[0].shape[0]
        for k, piece in enumerate(pieces):
            start = pl.multiple_of((index_ref[0] ^ k) * rows, 16)
            merger_ref[pl.ds(start, rows), :] = piece[...]

    left, right, _ = joined_norm(latent_ref, skip_ref)
    width = left.shape[1]
    left = (left * gains[0:1, :] + biases[0:1, :]).astype(BF16)
    right = (right * gains[1:2, :] + biases[1:2, :]).astype(BF16)
    total = dot(left, merger_ref[:width, :], 1, 0) + dot(right, merger_ref[width:, :], 1, 0)
    out_ref[...] = (total + biases[5:6, :]).astype(BF16)


def joined_norm(latent_ref, skip_ref):
    left, right = latent_ref[...].astype(F32), skip_ref[...].astype(F32)
    scale = 0.5 / left.shape[1]
    mean = (jnp.sum(left, axis=-1, keepdims=True) + jnp.sum(right, axis=-1, keepdims=True)) * scale
    left, right = left - mean, right - mean
    spread = jnp.sum(left * left, axis=-1, keepdims=True) + jnp.sum(right * right, axis=-1, keepdims=True)
    inverse = lax.rsqrt(spread * scale + EPSILON)
    return left * inverse, right * inverse, inverse


def merge(index, latents, skips, pieces, gains, biases, block=128):
    rows, width = latents.shape
    return pl.pallas_call(
        functools.partial(merge_kernel, len(pieces)),
        grid_spec=pltpu.PrefetchScalarGridSpec(
            num_scalar_prefetch=1,
            grid=(rows // block,),
            in_specs=[row_spec(block, width)] * 2
            + [whole(p.shape) for p in pieces]
            + [whole(gains.shape), whole(biases.shape)],
            out_specs=[row_spec(block, width), whole((2 * width, width))],
        ),
        out_shape=[shape_of((rows, width), BF16), shape_of((2 * width, width), BF16)],
        compiler_params=params(),
        name="merge",
    )(index, latents, skips, *pieces, gains, biases)


def merge_back_kernel(latent_ref, skip_ref, low_ref, merger, gains, biases, left_out, right_out, merge_in, sums):
    left, right, inverse = joined_norm(latent_ref, skip_ref)
    width = left.shape[1]
    low = low_ref[...]
    scale = 0.5 / width
    left_grad = dot(low, merger[:width, :], 1, 1)
    right_grad = dot(low, merger[width:, :], 1, 1)
    merge_in[:, :width] = (left * gains[0:1, :] + biases[0:1, :]).astype(BF16)
    merge_in[:, width:] = (right * gains[1:2, :] + biases[1:2, :]).astype(BF16)
    terms = jnp.concatenate(
        [
            column_sum(left_grad * left),
            column_sum(right_grad * right),
            column_sum(left_grad),
            column_sum(right_grad),
            column_sum(low.astype(F32)),
        ],
        axis=0,
    )
    left_grad, right_grad = left_grad * gains[0:1, :], right_grad * gains[1:2, :]
    first = jnp.sum(left_grad, axis=-1, keepdims=True) + jnp.sum(right_grad, axis=-1, keepdims=True)
    second = jnp.sum(left_grad * left, axis=-1, keepdims=True) + jnp.sum(
        right_grad * right, axis=-1, keepdims=True
    )
    first, second = first * scale, second * scale
    left_out[...] = inverse * (left_grad - first - left * second)
    right_out[...] = inverse * (right_grad - first - right * second)

    @pl.when(pl.program_id(0) == 0)
    def _():
        sums[...] = terms

    @pl.when(pl.program_id(0) > 0)
    def _():
        sums[...] += terms


def merge_back(latents, skips, low, merger, gains, biases, block=128):
    rows, width = latents.shape
    return pl.pallas_call(
        merge_back_kernel,
        grid=(rows // block,),
        in_specs=[row_spec(block, width)] * 3
        + [whole(merger.shape), whole(gains.shape), whole(biases.shape)],
        out_specs=[row_spec(block, width)] * 2 + [row_spec(block, 2 * width), whole((5, width))],
        out_shape=[
            shape_of((rows, width), F32),
            shape_of((rows, width), F32),
            shape_of((rows, 2 * width), BF16),
            shape_of((5, width), F32),
        ],
        compiler_params=params(),
        name="merge_back",
    )(latents, skips, low, merger, gains, biases)


def norm_kernel(count, keep, *refs):
    parts, rows, outs = refs[:count], refs[count], refs[count + 1 :]
    total = parts[0][...].astype(F32)
    for part in parts[1:]:
        total = total + part[...].astype(F32)
    total = total + rows[0:1, :]
    hat, _ = head_norm(total)
    outs[0][...] = (hat * rows[1:2, :] + rows[2:3, :]).astype(BF16)
    if keep:
        outs[1][...] = total


def norm(parts, rows, keep=True, block=128):
    length, width = parts[0].shape
    out = pl.pallas_call(
        functools.partial(norm_kernel, len(parts), keep),
        grid=(length // block,),
        in_specs=[row_spec(block, width)] * len(parts) + [whole(rows.shape)],
        out_specs=[row_spec(block, width)] * (1 + keep),
        out_shape=[shape_of((length, width), BF16)] + [shape_of((length, width), F32)] * keep,
        compiler_params=params(),
        name="norm",
    )(*parts, rows)
    return out if keep else out[0]


def norm_back_kernel(count, keep, *refs):
    parts, value_ref, carried, gain = refs[:count], refs[count], refs[count + 1], refs[count + 2]
    outs = refs[count + 3 :]
    grad = parts[0][...].astype(F32)
    for part in parts[1:]:
        grad = grad + part[...].astype(F32)
    hat, inverse = head_norm(value_ref[...].astype(F32))
    total = carried[...].astype(F32) + head_norm_back(grad, hat, inverse, gain[...])
    low = total.astype(BF16)
    outs[0][...] = low
    if keep:
        outs[2][...] = total
    terms = jnp.concatenate(
        [column_sum(grad * hat), column_sum(grad), column_sum(low.astype(F32))], axis=0
    )
    sums = outs[1]

    @pl.when(pl.program_id(0) == 0)
    def _():
        sums[...] = terms

    @pl.when(pl.program_id(0) > 0)
    def _():
        sums[...] += terms


def norm_back(parts, value, carried, gain, keep=True, block=128):
    length, width = value.shape
    return pl.pallas_call(
        functools.partial(norm_back_kernel, len(parts), keep),
        grid=(length // block,),
        in_specs=[row_spec(block, width)] * (len(parts) + 2) + [whole(gain.shape)],
        out_specs=[row_spec(block, width), whole((3, width))] + [row_spec(block, width)] * keep,
        out_shape=[shape_of((length, width), BF16), shape_of((3, width), F32)]
        + [shape_of((length, width), F32)] * keep,
        compiler_params=params(),
        name="norm_back",
    )(*parts, value, carried, gain)


class Links:
    def __init__(self, depth):
        self.depth = depth
        self.sent = {}

    def swap(self, value, axis, size, mask):
        sent = self.sent.setdefault((axis, mask if axis == "chip" else 0), [])
        if len(sent) >= self.depth:
            value, _ = lax.optimization_barrier((value, sent[-self.depth]))
        value = swap(value, axis, size, mask)
        sent.append(value)
        return value


def body(sizes, latents, skips, text_states, time_embedding, merger, modulator, norm_gains, norm_biases,
         output_bias, projector, combiner, cross_query, cross_memory, blender, expander, reducer,
         column_biases, hidden_bias, per_head_norm_gains, head_shifts, cotangent):
    chips, wide, deep = sizes
    chip_index, core, lane, side = (lax.axis_index(n) for n in ("chip", "core", "ta", "tb"))
    shard_len, local, width = latents.shape
    size = per_head_norm_gains.shape[1]
    text_len, text_width = text_states.shape[1:]
    own_len = shard_len * local
    seq_len = shard_len * wide * deep
    devices = chips * 2 * wide * deep
    latent_total = chips * 2 * local
    half_len = shard_len // 2
    tensor_cols = projector.shape[2]
    head_cols = tensor_cols // 2
    hidden_cols = expander.shape[1] // 2
    links = Links(2)
    chip_bits, wide_bits, deep_bits = bits_of(chips), bits_of(wide)[::-1], bits_of(deep)
    chip = chip_index.astype(jnp.int32).reshape(1)

    everywhere = [("ta", wide, b) for b in bits_of(wide)] + [("tb", deep, b) for b in deep_bits]
    everywhere = [("core", 2, 1)] + everywhere + [("chip", chips, b) for b in chip_bits]
    index_of = {"chip": chip_index, "core": core, "ta": lane, "tb": side}

    def at(value, index, axis=0):
        return lax.dynamic_index_in_dim(value, index, axis, keepdims=False)

    def gather_all(value):
        value = value[None, None, None, None]
        dims = {"chip": 0, "core": 1, "ta": 2, "tb": 3}
        shape = [1, 1, 1, 1]
        for axis, extent, mask in everywhere:
            value = value.reshape((*shape, *value.shape[4:]))
            other = swap(value, axis, extent, mask)
            high = (index_of[axis] & mask) > 0
            low_part = jnp.where(high, other, value)
            high_part = jnp.where(high, value, other)
            value = jnp.concatenate([low_part, high_part], axis=dims[axis])
            shape[dims[axis]] *= 2
        return value

    def sum_scatter_all(value):
        dims = {"chip": 0, "core": 1, "ta": 2, "tb": 3}
        for axis, extent, mask in everywhere[::-1]:
            dim = dims[axis]
            rows = value.shape[dim] // 2
            high = (index_of[axis] & mask) > 0
            low_part = lax.slice_in_dim(value, 0, rows, axis=dim)
            high_part = lax.slice_in_dim(value, rows, 2 * rows, axis=dim)
            kept = jnp.where(high, high_part, low_part)
            value = kept + swap(jnp.where(high, low_part, high_part), axis, extent, mask)
        return value.reshape(value.shape[4:])

    def halves(value):
        mine, other = at(value, core, 1), at(value, 1 - core, 1)
        other = swap(other, "core", 2, 1)
        pair = jnp.where(core == 0, jnp.stack([mine, other]), jnp.stack([other, mine]))
        return pair.reshape((-1,) + pair.shape[2:])

    def unhalves(value):
        value = value.reshape((2, -1) + value.shape[1:])
        mine, other = at(value, core), at(value, 1 - core)
        other = swap(other, "core", 2, 1)
        return jnp.where(core == 0, jnp.stack([mine, other], 1), jnp.stack([other, mine], 1))

    def gather_weight(value, order):
        value = value[None]
        count = 1
        value = value.reshape((1,) + value.shape)
        for mask in wide_bits:
            other = links.swap(value, "ta", wide, mask)
            value = jnp.stack([value, other], axis=2)
            count *= 2
            value = value.reshape((1, count) + value.shape[3:])
        pieces = {0: value[0]}
        for mask in order:
            for k in list(pieces):
                pieces[k ^ mask] = links.swap(pieces[k], "chip", chips, mask)
        return [pieces[k] for k in range(chips)]

    def scatter_weight(pieces, order):
        pieces = dict(enumerate(pieces))
        for mask in order[::-1]:
            for k in [k for k in pieces if k & mask]:
                received = swap(pieces.pop(k), "chip", chips, mask).astype(F32)
                near = pieces[k ^ mask].astype(F32) + received
                pieces[k ^ mask] = near if k == mask else near.astype(BF16)
        value = pieces[0].astype(F32)
        for mask in wide_bits[::-1]:
            value = value.reshape((value.shape[0] // 2, 2) + value.shape[1:])
            value = value[:, 0] + swap(value[:, 1].astype(BF16), "ta", wide, mask).astype(F32)
        return value[0]

    forth, back = chip_bits, chip_bits[::-1]

    small = jnp.concatenate(
        [v.reshape(-1) for v in (norm_gains, norm_biases, output_bias, column_biases, hidden_bias)]
    )
    small_all = gather_all(small).reshape(devices, -1)
    part = norm_gains.shape[1]
    hidden_part = hidden_bias.shape[0]
    table = jnp.transpose(small_all[:, : 21 * part].reshape(devices, 21, part), (1, 0, 2)).reshape(21, width)
    gains, biases, out_bias, columns = table[:5], table[5:14], table[14:15], table[15:21]
    hidden_all = small_all[:, 21 * part :].reshape(wide, deep, 2, hidden_cols)

    def own_columns(value):
        value = value.reshape(value.shape[0], wide, deep, 2, -1)
        value = at(at(value, side, 2), core, 2)
        return jnp.stack([at(value, lane ^ i, 1) for i in range(wide)])

    def all_columns(value):
        value = jnp.stack([at(value, lane ^ i) for i in range(wide)], axis=1)
        there = (jnp.arange(deep) == side)[:, None] & (jnp.arange(2) == core)[None, :]
        value = jnp.where(there[None, None, :, :, None], value[:, :, None, None, :], 0.0)
        return value.reshape(value.shape[0], -1)

    own_biases = own_columns(columns)

    rows = projector.shape[0]
    merger_z = merger[None]
    for mask in bits_of(wide):
        other = links.swap(merger_z, "ta", wide, mask)
        high = (lane & mask) > 0
        merger_z = jnp.concatenate(
            [jnp.where(high, other, merger_z), jnp.where(high, merger_z, other)], axis=0
        )
    merger_z = merger_z.reshape(wide, 1, *merger.shape)
    for mask in deep_bits:
        other = swap(merger_z, "tb", deep, mask)
        high = (side & mask) > 0
        merger_z = jnp.concatenate(
            [jnp.where(high, other, merger_z), jnp.where(high, merger_z, other)], axis=1
        )
    merger_z = merger_z.reshape(-1, width)
    merger_pieces = {0: merger_z}
    for mask in forth:
        for k in list(merger_pieces):
            merger_pieces[k ^ mask] = links.swap(merger_pieces[k], "chip", chips, mask)
    merger_list = []
    for k in range(chips):
        merger_list += [merger_pieces[k], swap(merger_pieces[k], "core", 2, 1)]

    projector_in = halves(projector.reshape(rows, 3, 2, head_cols).transpose(0, 2, 1, 3))
    projector_w = gather_weight(projector_in.reshape(2 * rows, 3 * head_cols), back)
    combiner_w = gather_weight(halves(combiner.T.reshape(rows, 2, head_cols)), forth)
    text_rows_w = cross_memory.shape[0]
    memory_in = halves(cross_memory.reshape(text_rows_w, 2, 2, head_cols).transpose(0, 2, 1, 3))
    memory_w = gather_weight(memory_in.reshape(2 * text_rows_w, 2 * head_cols), back)
    query_w = gather_weight(halves(cross_query.reshape(rows, 2, head_cols)), forth)
    blender_w = gather_weight(halves(blender.T.reshape(rows, 2, head_cols)), back)
    tile = hidden_cols // MLP_CHUNKS
    mlp_in = jnp.stack(
        [
            halves(expander.reshape(rows, 2, hidden_cols)),
            halves(reducer.T.reshape(rows, 2, hidden_cols)),
        ],
        axis=1,
    ).reshape(2 * rows, 2, MLP_CHUNKS, tile)
    mlp_orders = [forth if j % 2 == 0 else back for j in range(MLP_CHUNKS)]

    times = time_embedding
    silu_own = jax.nn.silu(times.astype(F32)).astype(BF16)
    silu_all = silu_own[None, None]
    silu_all = jnp.concatenate([silu_all, swap(silu_all, "core", 2, 1)], axis=1)
    silu_all = jnp.where(core == 0, silu_all, silu_all[:, ::-1])
    for mask in chip_bits:
        other = swap(silu_all, "chip", chips, mask)
        high = (chip_index & mask) > 0
        silu_all = jnp.concatenate(
            [jnp.where(high, other, silu_all), jnp.where(high, silu_all, other)], axis=0
        )
    silu_all = silu_all.reshape(latent_total, width)
    mod_rows = modulator.shape[0]
    device = ((chip_index * 2 + core) * wide + lane) * deep + side
    silu_cols = at(silu_all.reshape(latent_total, devices, mod_rows), device, 1)
    mod = jnp.dot(silu_cols, modulator, preferred_element_type=F32).reshape(chips, wide, width)
    for axis, extent, mask in [("chip", chips, b) for b in chip_bits[::-1]]:
        high = (chip_index & mask) > 0
        low_part, high_part = jnp.split(mod, 2, axis=0)
        mod = jnp.where(high, high_part, low_part) + swap(
            jnp.where(high, low_part, high_part), axis, extent, mask
        )
    for axis, extent, mask in [("ta", wide, b) for b in bits_of(wide)[::-1]]:
        high = (lane & mask) > 0
        low_part, high_part = jnp.split(mod, 2, axis=1)
        mod = jnp.where(high, high_part, low_part) + swap(
            jnp.where(high, low_part, high_part), axis, extent, mask
        )
    mod = mod.reshape(1, width)
    for axis, extent, mask in [("tb", deep, b) for b in deep_bits] + [("core", 2, 1)]:
        mod = mod + swap(mod, axis, extent, mask)

    def to_latent(value):
        value = value.reshape(local, 2, half_len, width)
        mine, other = at(value, core, 1), at(value, 1 - core, 1)
        other = swap(other, "core", 2, 1)
        pair = jnp.where(core == 0, jnp.stack([mine, other]), jnp.stack([other, mine]))
        return exchange(pair.reshape(wide, half_len, width)).reshape(own_len, width)

    def from_latent(value):
        pair = exchange(value.reshape(wide, half_len, width)).reshape(2, local, half_len, width)
        mine, other = at(pair, core), at(pair, 1 - core)
        other = swap(other, "core", 2, 1)
        value = jnp.where(core == 0, jnp.stack([mine, other], 1), jnp.stack([other, mine], 1))
        return value.reshape(own_len, width)

    def exchange(value):
        own = at(value, lane)
        parts = [own] + [
            swap(at(value, lane ^ mask), "ta", wide, mask) for mask in range(1, wide)
        ]
        parts = jnp.stack(parts)
        return jnp.stack([at(parts, lane ^ i) for i in range(wide)])

    def gather_tokens(value):
        value = jnp.concatenate([value, swap(value, "core", 2, 1)], axis=0)
        for mask in deep_bits:
            value = jnp.concatenate([value, swap(value, "tb", deep, mask)], axis=0)
        return value

    def scatter_tokens(other):
        terms = []
        rest = other
        for mask in deep_bits[::-1]:
            rows_sent = (own_len * 2 * deep) // 2
            kept = rest.shape[0] - rows_sent
            received = swap(rest[kept:], "tb", deep, mask)
            terms.append(received[:own_len])
            rest = (rest[:kept].astype(F32) + received[own_len:].astype(F32)).astype(BF16)
        terms.append(swap(rest, "core", 2, 1))
        return terms

    latents_flat = jnp.transpose(latents, (1, 0, 2)).reshape(own_len, width)
    skips_flat = jnp.transpose(skips, (1, 0, 2)).reshape(own_len, width)
    merge_index = (chip_index * 2 + core).astype(jnp.int32).reshape(1)
    first_local, merger_full = merge(merge_index, latents_flat, skips_flat, merger_list, gains, biases)
    first = to_latent(first_local)
    cot = to_latent(jnp.transpose(cotangent, (1, 0, 2)))
    cot_all = gather_tokens(cot)

    block_index = jnp.arange(wide)[:, None]
    inside = jnp.arange(half_len)[None, :]
    places = []
    for b in range(deep):
        for c in range(2):
            slot = (block_index * deep + (side ^ b)) * 2 + (core ^ c)
            places.append((slot * half_len + inside).reshape(-1))
    places = jnp.concatenate(places)
    quarter = size // 4
    frequency = THETA ** (-2.0 * jnp.arange(quarter).astype(F32) / (size // 2))
    row_angle = (places // GRID_W).astype(F32)[:, None] * frequency
    column_angle = (places % GRID_W).astype(F32)[:, None] * frequency
    angles = jnp.concatenate([row_angle, row_angle, column_angle, column_angle], axis=1)
    sign = jnp.where((jnp.arange(size) // quarter) % 2 == 0, -1.0, 1.0)
    cosine, sine = jnp.cos(angles), jnp.sin(angles) * sign

    zero_row = jnp.zeros((1, width), F32)
    rows_of = lambda *parts: jnp.concatenate(parts, axis=0)
    x_self = gather_tokens(
        norm([first], rows_of(zero_row, gains[2:3], biases[2:3] + biases[6:7] + mod), keep=False)
    )
    self_bias = own_biases[:, 0:3].reshape(wide, 1, 3 * head_cols)
    self_low, self_pre, self_att, self_lse, part_own, part_other = self_forward(
        chip, x_self, projector_w, self_bias, combiner_w, per_head_norm_gains, head_shifts, cosine, sine, own_len
    )
    x_cross, second = norm(
        [first, part_own, *scatter_tokens(part_other)], rows_of(biases[7:8], gains[3:4], biases[3:4])
    )
    x_cross = gather_tokens(x_cross)

    text_pad = -text_len % 16
    text_mine = at(text_states, lane % local)
    text_other = swap(text_mine, "core", 2, 1)
    text = jnp.where(core == lane // local, text_mine, text_other)
    text = jnp.pad(text, ((0, text_pad), (0, 0)))
    cross_bias = own_biases[:, 3:4]
    memory_bias = own_biases[:, 4:6].reshape(wide, 1, 2 * head_cols)
    cross_low, cross_pre, memory_low, memory_pre, cross_att, cross_lse, part_own, part_other = cross_forward(
        chip, x_cross, text, query_w, memory_w, blender_w, cross_bias, memory_bias,
        per_head_norm_gains, head_shifts, own_len, text_len,
    )
    x_mlp, third = norm(
        [second, part_own, *scatter_tokens(part_other)], rows_of(biases[8:9], gains[4:5], biases[4:5])
    )
    x_mlp = gather_tokens(x_mlp)

    own_hidden = at(at(hidden_all, side, 1), core, 1)
    own_hidden = jnp.stack([at(own_hidden, lane ^ i) for i in range(wide)]).reshape(wide, 1, MLP_CHUNKS, tile)
    x_t, cot_t = x_mlp.T, cot_all.T
    outs, backs, hidden_sums, mlp_grads = [third], [], [], []
    for j in range(MLP_CHUNKS):
        weights = gather_weight(mlp_in[:, :, j].reshape(2 * rows, 2 * tile), mlp_orders[j])
        grads, out_own, out_other, back_own, back_other, hidden_sum = mlp(
            chip, x_mlp, cot_all, x_t, cot_t, weights, own_hidden[:, :, j], own_len
        )
        mlp_grads.append(scatter_weight(grads, mlp_orders[j]))
        outs += [out_own, *scatter_tokens(out_other)]
        backs += [back_own, *scatter_tokens(back_other)]
        hidden_sums.append(hidden_sum)
    block_total = sum(v.astype(F32) for v in outs) + out_bias
    block_out = from_latent(block_total.astype(BF16))

    third_low, mlp_sums, third_grad = norm_back(backs, third, cot, gains[4:5])
    blender_g_in = gather_tokens(third_low)
    query_g, memory_g, blender_g, part_own, part_other, text_part, query_col, memory_col, cross_heads = (
        cross_backward(
            chip, x_cross, blender_g_in, text, query_w, memory_w, blender_w, cross_low, cross_pre,
            memory_low, memory_pre, cross_att, cross_lse, per_head_norm_gains, own_len, text_len,
        )
    )
    blender_grads = unhalves(scatter_weight(blender_g, back)).reshape(rows, tensor_cols).T
    query_grads = unhalves(scatter_weight(query_g, forth)).reshape(rows, tensor_cols)
    memory_grads = unhalves(
        scatter_weight(memory_g, back).reshape(2 * text_rows_w, 2, head_cols)
    )
    memory_grads = memory_grads.transpose(0, 2, 1, 3).reshape(text_rows_w, 2, tensor_cols)
    second_low, cross_sums, second_grad = norm_back(
        [part_own, *scatter_tokens(part_other)], second, third_grad, gains[3:4]
    )
    proj_g, comb_g, part_own, part_other, self_col, self_heads = self_backward(
        chip, x_self, gather_tokens(second_low), projector_w, combiner_w, self_low, self_pre, self_att,
        self_lse, per_head_norm_gains, cosine, sine, own_len,
    )
    first_low, self_sums = norm_back(
        [part_own, *scatter_tokens(part_other)], first, second_grad, gains[2:3], keep=False
    )
    low_local = from_latent(first_low)
    projector_grads = unhalves(scatter_weight(proj_g, back).reshape(2 * rows, 3, head_cols))
    projector_grads = projector_grads.transpose(0, 2, 1, 3).reshape(rows, 3, tensor_cols)
    combiner_grads = unhalves(scatter_weight(comb_g, forth)).reshape(rows, tensor_cols).T
    left, right, merge_in, merge_sums = merge_back(
        latents_flat, skips_flat, low_local, merger_full, gains, biases
    )
    merger_g = dot(merge_in, low_local, 0, 0).astype(BF16).reshape(chips, 2, -1, width)
    mine, other = [], []
    for k in range(chips):
        block = at(merger_g, chip_index ^ k)
        mine.append(at(block, core))
        other.append(at(block, 1 - core))
    received = [swap(o, "core", 2, 1) for o in other]
    merger_p = {
        k: (m.astype(F32) + r.astype(F32)).astype(BF16) for k, (m, r) in enumerate(zip(mine, received))
    }
    for mask in forth[::-1]:
        for k in [k for k in merger_p if k & mask]:
            received = swap(merger_p.pop(k), "chip", chips, mask)
            merger_p[k ^ mask] = (merger_p[k ^ mask].astype(F32) + received.astype(F32)).astype(BF16)
    value = merger_p[0].reshape(wide, deep, -1, width).astype(F32)
    for axis, dim, extent, index, mask in [("tb", 1, deep, side, b) for b in deep_bits[::-1]] + [
        ("ta", 0, wide, lane, b) for b in bits_of(wide)[::-1]
    ]:
        low_part, high_part = jnp.split(value, 2, axis=dim)
        high = (index & mask) > 0
        sent = jnp.where(high, low_part, high_part).astype(BF16)
        value = jnp.where(high, high_part, low_part) + swap(sent, axis, extent, mask).astype(F32)
    merger_grads = value.reshape(merger.shape)

    mlp_grad = jnp.stack([g.reshape(2 * rows, 2, tile) for g in mlp_grads], axis=2)
    expander_grads = unhalves(mlp_grad[:, 0].reshape(2 * rows, hidden_cols)).reshape(rows, 2 * hidden_cols)
    reducer_grads = unhalves(mlp_grad[:, 1].reshape(2 * rows, hidden_cols)).reshape(rows, 2 * hidden_cols).T

    text_sum = text_part
    for axis, extent, mask in [("core", 2, 1)] + [("tb", deep, b) for b in deep_bits]:
        text_sum = text_sum + swap(text_sum.astype(BF16), axis, extent, mask).astype(F32)
    text_sum = text_sum[:text_len].astype(BF16).reshape(text_len, wide, deep, -1)
    text_sum = at(text_sum, side, 2).transpose(1, 0, 2)
    text_got = exchange(text_sum)
    text_grads = lax.dynamic_slice_in_dim(text_got, core * local, local, 0).astype(F32)

    mod_grad = self_sums[1:2]
    for axis, extent, mask in [("core", 2, 1)] + [("tb", deep, b) for b in deep_bits]:
        mod_grad = mod_grad + swap(mod_grad, axis, extent, mask)
    mod_all = mod_grad[None]
    for mask in bits_of(wide):
        other = swap(mod_all, "ta", wide, mask)
        high = (lane & mask) > 0
        mod_all = jnp.concatenate([jnp.where(high, other, mod_all), jnp.where(high, mod_all, other)], axis=1)
    for mask in chip_bits:
        other = swap(mod_all, "chip", chips, mask)
        high = (chip_index & mask) > 0
        mod_all = jnp.concatenate([jnp.where(high, other, mod_all), jnp.where(high, mod_all, other)], axis=0)
    mod_all = mod_all.reshape(latent_total, width)
    exact = lax.Precision.HIGHEST
    modulator_grads = lax.dot_general(
        silu_cols.astype(F32), mod_all, (((0,), (0,)), ((), ())), precision=exact
    )
    time_part = lax.dot_general(
        mod_all, modulator.astype(F32), (((1,), (1,)), ((), ())), precision=exact
    )
    time_all = gather_all(time_part)
    time_all = jnp.moveaxis(time_all.reshape(devices, latent_total, mod_rows), 0, 1)
    time_all = time_all.reshape(chips * 2, local, wide * deep, -1)
    time_own = at(at(time_all, chip_index * 2 + core), lane * deep + side, 1)
    times_own = at(times.reshape(local, wide * deep, -1), lane * deep + side, 1).astype(F32)
    _, silu_pull = jax.vjp(jax.nn.silu, times_own)
    time_grads = silu_pull(time_own)[0]

    output_sum = jnp.sum(cotangent.astype(F32), axis=(0, 1))[None]
    columns_own = jnp.concatenate(
        [self_col.reshape(wide, 3, head_cols), query_col, memory_col.reshape(wide, 2, head_cols)], axis=1
    )
    sums = jnp.concatenate(
        [
            merge_sums[0:2], self_sums[0:1], cross_sums[0:1], mlp_sums[0:1],
            merge_sums[2:4], self_sums[1:2], cross_sums[1:2], mlp_sums[1:2],
            merge_sums[4:5], self_sums[1:2], cross_sums[2:3], mlp_sums[2:3],
            output_sum, all_columns(columns_own),
        ],
        axis=0,
    )
    hidden_sum = jnp.stack(hidden_sums, axis=2).reshape(wide, 1, hidden_cols)
    hidden_sum = all_columns(hidden_sum)
    sums = jnp.transpose(sums.reshape(21, devices, part), (1, 0, 2)).reshape(devices, -1)
    both = jnp.concatenate([sums, hidden_sum.reshape(devices, hidden_part)], axis=1)
    both = sum_scatter_all(both.reshape(chips, 2, wide, deep, -1))
    table = both[: 21 * part].reshape(21, part)
    hidden_grads = both[21 * part :]
    head_sums = jnp.concatenate(
        [self_heads[0:2], cross_heads[0:2], self_heads[2:4], cross_heads[2:3]], axis=0
    )
    for axis, extent, mask in everywhere:
        head_sums = head_sums + swap(head_sums, axis, extent, mask)

    def to_local(value):
        return jnp.transpose(value.reshape(local, shard_len, width), (1, 0, 2)).astype(F32)

    return (
        to_local(block_out), to_local(left), to_local(right), text_grads, time_grads, merger_grads,
        modulator_grads, table[0:5], table[5:14], table[14], projector_grads, combiner_grads, query_grads,
        memory_grads, blender_grads, expander_grads, reducer_grads, table[15:21], hidden_grads,
        head_sums[0:4], head_sums[4:7],
    )


def solution(mesh):
    data, tensor = mesh.shape["dp"], mesh.shape["tensor"]

    def run(*arrays):
        local = arrays[0].shape[1] // data
        wide = min(tensor, 2 * local)
        deep = tensor // wide
        grid = Mesh(
            mesh.devices.reshape(data // 2, 2, wide, deep), ("chip", "core", "ta", "tb")
        )
        dp, tp = ("chip", "core"), ("ta", "tb")
        both = dp + tp
        tokens = P(tp, dp, None)
        in_specs = (
            tokens, tokens, P(dp, None, None), P(dp, None), P(both, None), P(both, None), P(None, both),
            P(None, both), P(both), P(dp, None, tp), P(tp, dp), P(dp, tp), P(dp, None, tp), P(tp, dp),
            P(dp, tp), P(tp, dp), P(None, both), P(both), P(), P(), tokens,
        )
        out_specs = (
            tokens, tokens, tokens, P(dp, None, tp), P(dp, tp), P(both, None), P(both, None),
            P(None, both), P(None, both), P(both), P(dp, None, tp), P(tp, dp), P(dp, tp),
            P(dp, None, tp), P(tp, dp), P(dp, tp), P(tp, dp), P(None, both), P(both), P(), P(),
        )
        return jax.shard_map(
            functools.partial(body, (data // 2, wide, deep)),
            mesh=grid, in_specs=in_specs, out_specs=out_specs, check_vma=False,
        )(*arrays)

    return run
```

time: 3410 us -> 1670 us (0.49)
  waiting for transfers between devices: 1490 us -> 518 us
  blocking collectives: 506 us -> 0 us
  Pallas kernels: 0 us -> 465 us
  local copies, waits for them, and re-layouts: 669 us -> 295 us
  matrix products: 329 us -> 8.09 us
  other arithmetic: 367 us -> 159 us
  starting transfers between devices: 14.3 us -> 206 us
    reduce_scatter x13 -> x0, waiting for transfers between devices: 724 us -> none  [the longest x3 307 us: scatter_rows(): lax.psum_scatter(partial_term(jnp.int32(0), local_rows * lax.axis_size('t...]
    ppermute x0 -> x182, waiting for transfers between devices: none -> 518 us  [swap(): return lax.ppermute(value, axis, [(i, i ^ mask) for i in range(size)])]
    pallas_call x0 -> x15, Pallas kernels: none -> 465 us  [the longest x3 110 us: mlp(): pl.pallas_call(functools.partial(mlp_kernel, (chips, own)), grid_spec=plt...]
    all_gather x12 -> x0, waiting for transfers between devices: 429 us -> none  [the longest x3 192 us: gather_grads(): lax.all_gather(local_part.reshape(local_shape), 'tensor', axis=0, tiled=T...]
    unnamed x36 -> x0, waiting for transfers between devices: 336 us -> none
    dot_general x55 -> x4, matrix products: 329 us -> 8.09 us  [the longest x1 6.73 us: dot(): lax.dot_general(left, right, (((left_dim,), (right_dim,)), ((), ())), pre...]
    unnamed x2 -> x0, blocking collectives: 262 us -> none
    all_gather x6 -> x0, blocking collectives: 244 us -> none  [the longest x1 72.1 us: body(): lax.all_gather(column_biases.astype(jnp.bfloat16), ('dp', 'tensor'), axis...]
  transfers between devices with their start and end apart: 32 -> 182, of which waited for: 23 -> 55; matrix products, arithmetic and copies ran while one was open for 19% -> 27% of each run, Pallas kernels for 0% -> 28%
where the time goes in v1:
time: 1670 us; the launch traced here: 1650 us
  waiting for transfers between devices  518 us (31%)
  Pallas kernels  465 us (28%)
  local copies, waits for them, and re-layouts  295 us (18%)
  starting transfers between devices  206 us (12%)
  other arithmetic  159 us (10%)
    ppermute x182, waiting for transfers between devices, swap(): return lax.ppermute(value, axis, [(i, i ^ mask) for i in range(size)])  518 us
    ppermute x182, starting transfers between devices, swap(): return lax.ppermute(value, axis, [(i, i ^ mask) for i in range(size)])  206 us
    pallas_call x3, Pallas kernels, mlp(): pl.pallas_call(functools.partial(mlp_kernel, (chips, own)), grid_spec=plt...  110 us
    pallas_call x1, Pallas kernels, self_backward(): pl.pallas_call(functools.partial(self_backward_kernel, (chips, heads, siz...  107 us
    pallas_call x1, Pallas kernels, self_forward(): pl.pallas_call(functools.partial(self_forward_kernel, (chips, heads, size...  76.8 us
    ppermute x30, local copies, waits for them, and re-layouts, swap(): return lax.ppermute(value, axis, [(i, i ^ mask) for i in range(size)])  68.5 us
    pallas_call x1, Pallas kernels, cross_backward(): pl.pallas_call(functools.partial(cross_backward_kernel, (chips, heads, si...  61.2 us
    pallas_call x1, Pallas kernels, cross_forward(): pl.pallas_call(functools.partial(cross_forward_kernel, (chips, heads, siz...  40.5 us
  transfers between devices with their start and end apart: 182, of which 55 were waited for; matrix products, arithmetic and copies ran while one was open for 27% of the time, Pallas kernels for 28%

profile of v1, /device:TPU:9, one launch (start us, length us, event | category | flops | bytes accessed | tf_op | source)
XLA Modules:
  0.0 1654.3 jit_solution(16281667461919060862)
XLA Ops:
  70.3 19.3 %collective-permute-done.1 = bf16[2,88,1408]{2,1,0:T(8,128)(2,1)S(1)} collective-permute-done((bf16[2,88,1408]{2,1,0:T(8,128)(2,1)S(1)}, bf16[2,88,1408]{2,1,0:T(8,128)(2,1)S(1)}, u32[]{:S(2)}, u32[]{:S(2)}) %collective-permute-start.1) | collective-permute-done | bytes 495648 | tf_op jit(solution)/shard_map/ppermute | solution.py:25
  91.1 5.4 collective-permute-start.24
  101.7 11.2 collective-permute-done.3.refs_4_
  128.2 17.2 %collective-permute-done.7.refs_8_ = bf16[352,1408]{1,0:T(8,128)(2,1)} collective-permute-done((bf16[352,1408]{1,0:T(8,128)(2,1)}, bf16[352,1408]{1,0:T(8,128)(2,1)}, u32[]{:S(2)}, u32[]{:S(2)}) %collective-permute-start.7) | collective-permute-done | bytes 991264 | tf_op jit(solution)/shard_map/ppermute | solution.py:25
  150.2 17.7 %collective-permute-done.29 = bf16[1,2,352,528]{2,3,1,0:T(8,128)(2,1)S(1)} collective-permute-done((bf16[1,2,352,528]{2,3,1,0:T(8,128)(2,1)S(1)}, bf16[1,2,352,528]{2,3,1,0:T(8,128)(2,1)S(1)}, u32[]{:S(2)}, u32[]{:S(2)}) %collective-permute-start.29) | collective-permute-done | bytes 743456 | tf_op jit(solution)/shard_map/ppermute | solution.py:25
  176.9 13.4 merge.1
  196.2 6.9 collective-permute-done.34
  227.5 11.3 collective-permute-done.35
  249.0 8.8 collective-permute-done.16
  285.0 20.6 %collective-permute-done.36 = bf16[4,352,176]{1,2,0:T(8,128)(2,1)} collective-permute-done((bf16[4,352,176]{1,2,0:T(8,128)(2,1)}, bf16[4,352,176]{1,2,0:T(8,128)(2,1)}, u32[]{:S(2)}, u32[]{:S(2)}) %collective-permute-start.36) | collective-permute-done | bytes 495648 | tf_op jit(solution)/shard_map/ppermute | solution.py:25
  348.2 76.8 %self_forward.1 = (bf16[4,1024,528]{2,1,0:T(8,128)(2,1)}, bf16[4,1024,352]{2,1,0:T(8,128)(2,1)}, bf16[4,1024,176]{2,1,0:T(8,128)(2,1)}, f32[4,2,1024]{2,1,0:T(2,...) custom-call(s32[1]{0:T(128)} %bitcast.20.chip_ref, bf16[1024,1408]{1,0:T(8,128)(2,1)} %pad_maximum_fusion.refs_0_, ...), custom_call_target="tpu_custom_call" | custom-call | tf_op jit(solution)/shard_map/self_forward/pallas_call | solution.py:166
  449.0 9.1 collective-permute-done.49
  464.3 5.5 collective-permute-done.57
  525.0 40.5 %cross_forward.1 = (bf16[4,1024,176]{2,1,0:T(8,128)(2,1)}, bf16[4,1024,176]{2,1,0:T(8,128)(2,1)}, bf16[4,336,352]{2,1,0:T(8,128)(2,1)}, bf16[4,336,176]{2,1,0:T(...) custom-call(s32[1]{0:T(128)} %bitcast.20.chip_ref, ...), custom_call_target="tpu_custom_call" | custom-call | tf_op jit(solution)/shard_map/cross_forward/pallas_call | solution.py:428
  576.3 5.8 norm.5
  583.9 19.4 %collective-permute-done.73.refs_7_ = bf16[4,352,512]{2,1,0:T(8,128)(2,1)} collective-permute-done((bf16[4,352,512]{2,1,0:T(8,128)(2,1)}, bf16[4,352,512]{2,1,0:T(8,128)(2,1)}, u32[]{:S(2)}, u32[]{:S(2)}) %collective-permute-start.73) | collective-permute-done | bytes 1441824 | tf_op jit(solution)/shard_map/ppermute | solution.py:25
  603.6 30.6 %collective-permute-done.78.refs_6_ = bf16[4,352,512]{2,1,0:T(8,128)(2,1)} collective-permute-done((bf16[4,352,512]{2,1,0:T(8,128)(2,1)}, bf16[4,352,512]{2,1,0:T(8,128)(2,1)}, u32[]{:S(2)}, u32[]{:S(2)}) %collective-permute-start.78) | collective-permute-done | bytes 1441824 | tf_op jit(solution)/shard_map/ppermute | solution.py:25
  654.9 10.2 collective-permute-done.84.refs_6_
  665.1 30.9 %collective-permute-done.85.refs_7_ = bf16[4,352,512]{2,1,0:T(8,128)(2,1)} collective-permute-done((bf16[4,352,512]{2,1,0:T(8,128)(2,1)}, bf16[4,352,512]{2,1,0:T(8,128)(2,1)}, u32[]{:S(2)}, u32[]{:S(2)}) %collective-permute-start.85) | collective-permute-done | bytes 1441824 | tf_op jit(solution)/shard_map/ppermute | solution.py:25
  696.0 36.7 %mlp.5 = (bf16[4,352,512]{2,1,0:T(8,128)(2,1)}, bf16[4,352,512]{2,1,0:T(8,128)(2,1)}, bf16[4,352,512]{2,1,0:T(8,128)(2,1)}, bf16[4,352,512]{2,1,0:T(8,128)(2,1)}...) custom-call(s32[1]{0:T(128)} %bitcast.20.chip_ref, ...), custom_call_target="tpu_custom_call" | custom-call | tf_op jit(solution)/shard_map/mlp/pallas_call | solution.py:636
  733.7 36.5 %mlp.4 = (bf16[4,352,512]{2,1,0:T(8,128)(2,1)}, bf16[4,352,512]{2,1,0:T(8,128)(2,1)}, bf16[4,352,512]{2,1,0:T(8,128)(2,1)}, bf16[4,352,512]{2,1,0:T(8,128)(2,1)}...) custom-call(s32[1]{0:T(128)} %bitcast.20.chip_ref, ...), custom_call_target="tpu_custom_call" | custom-call | tf_op jit(solution)/shard_map/mlp/pallas_call | solution.py:636
  770.3 36.9 %mlp.3 = (bf16[4,352,512]{2,1,0:T(8,128)(2,1)}, bf16[4,352,512]{2,1,0:T(8,128)(2,1)}, bf16[4,352,512]{2,1,0:T(8,128)(2,1)}, bf16[4,352,512]{2,1,0:T(8,128)(2,1)}...) custom-call(s32[1]{0:T(128)} %bitcast.20.chip_ref, ...), custom_call_target="tpu_custom_call" | custom-call | tf_op jit(solution)/shard_map/mlp/pallas_call | solution.py:636
  813.4 6.3 add_convert_fusion.4
  821.6 23.0 %collective-permute-done.171 = bf16[4,352,512]{2,1,0:T(8,128)(2,1)} collective-permute-done((bf16[4,352,512]{2,1,0:T(8,128)(2,1)}, bf16[4,352,512]{2,1,0:T(8,128)(2,1)}, u32[]{:S(2)}, u32[]{:S(2)}) %collective-permute-start.171) | collective-permute-done | bytes 1441824 | tf_op jit(solution)/shard_map/ppermute | solution.py:25
  851.4 9.7 norm_back.3
  871.8 8.0 collective-permute-done.161
  883.1 27.6 %collective-permute-done.170 = bf16[4,352,512]{2,1,0:T(8,128)(2,1)} collective-permute-done((bf16[4,352,512]{2,1,0:T(8,128)(2,1)}, bf16[4,352,512]{2,1,0:T(8,128)(2,1)}, u32[]{:S(2)}, u32[]{:S(2)}) %collective-permute-start.170) | collective-permute-done | bytes 1441824 | tf_op jit(solution)/shard_map/ppermute | solution.py:25
  920.0 61.2 %cross_backward.1 = (bf16[4,352,176]{2,1,0:T(8,128)(2,1)}, bf16[4,352,176]{2,1,0:T(8,128)(2,1)}, bf16[4,352,176]{2,1,0:T(8,128)(2,1)}, bf16[4,352,176]{2,1,0:T(8...) custom-call(s32[1]{0:T(128)} %bitcast.20.chip_ref, ...), custom_call_target="tpu_custom_call" | custom-call | tf_op jit(solution)/shard_map/cross_backward/pallas_call | solution.py:552
  1038.3 9.3 collective-permute-done.168
  1050.7 12.4 collective-permute-done.163
  1067.5 5.7 collective-permute-start.95
  1098.3 11.5 collective-permute-done.174
  1146.9 5.6 collective-permute-done.158
  1157.1 6.6 collective-permute-done.146
  1172.8 7.5 norm_back.4
  1202.2 107.0 %self_backward.1 = (bf16[4,352,528]{2,1,0:T(8,128)(2,1)}, bf16[4,352,528]{2,1,0:T(8,128)(2,1)}, bf16[4,352,528]{2,1,0:T(8,128)(2,1)}, bf16[4,352,528]{2,1,0:T(8,...) custom-call(s32[1]{0:T(128)} %bitcast.20.chip_ref, ...), custom_call_target="tpu_custom_call" | custom-call | tf_op jit(solution)/shard_map/self_backward/pallas_call | solution.py:304
  1314.6 10.7 collective-permute-done.137
  1344.8 6.4 norm_back.5
  1373.3 6.1 collective-permute-done.140
  1379.4 56.3 %collective-permute-done.109 = f32[1,4,1408]{2,1,0:T(4,128)S(1)} collective-permute-done((f32[1,4,1408]{2,1,0:T(4,128)S(1)}, f32[1,4,1408]{2,1,0:T(4,128)S(1)}, u32[]{:S(2)}, u32[]{:S(2)}) %collective-permute-start.109) | collective-permute-done | bytes 22560 | tf_op jit(solution)/shard_map/ppermute | solution.py:25
  1452.1 8.3 collective-permute-done.112
  1469.0 5.5 collective-permute-done.113
  1480.5 22.9 %collective-permute-done.115 = f32[2,2,4,1,16,44]{5,4,3,2,1,0:T(8,128)S(1)} collective-permute-done((f32[2,2,4,1,16,44]{5,4,3,2,1,0:T(8,128)S(1)}, f32[2,2,4,1,16,44]{5,4,3,2,1,0:T(8,128)S(1)}, u32[]{:S(2)}, u32[]{:S(2)}) %collective-permute-start.115) | collective-permute-done | bytes 45088 | tf_op jit(solution)/shard_map/ppermute | solution.py:25
  1504.8 17.1 %merge_back.1 = (f32[512,1408]{1,0:T(8,128)}, f32[512,1408]{1,0:T(8,128)}, bf16[512,2816]{1,0:T(8,128)(2,1)}, f32[5,1408]{1,0:T(8,128)}) custom-call(bf16[512,1408]{1,0:T(8,128)(2,1)} %bitcast.579, bf16[512,1408]{1,0:T(8,128)(2,1)} %bitcast.581, bf16[512,1408]{1,0:T(8,128)(2,1)} %bitcast.597, bf16[2816,1408]{1,0:T(8,128)(2,1)} %get-tuple-element.228.merger, ...), custom_call_target="tpu_custom_call" | custom-call | tf_op jit(solution)/shard_map/merge_back/pallas_call | solution.py:756
  1533.3 6.7 convolution_convert_fusion
  1581.2 5.6 collective-permute-done.121
  1595.1 15.1 collective-permute-done.134
  1621.6 21.0 %collective-permute-done.123 = bf16[2,1,88,1408]{3,2,1,0:T(8,128)(2,1)S(1)} collective-permute-done((bf16[2,1,88,1408]{3,2,1,0:T(8,128)(2,1)S(1)}, bf16[2,1,88,1408]{3,2,1,0:T(8,128)(2,1)S(1)}, u32[]{:S(2)}, u32[]{:S(2)}) %collective-permute-start.123) | collective-permute-done | bytes 495648 | tf_op jit(solution)/shard_map/ppermute | solution.py:25
  (1089 shorter events, 696.6 us)
Async XLA Ops:
  8.7 46.7 %collective-permute-start.33 = (bf16[176,176]{1,0:T(8,128)(2,1)}, bf16[176,176]{1,0:T(8,128)(2,1)}, u32[]{:S(2)}, u32[]{:S(2)}) collective-permute-start(bf16[176,176]{1,0:T(8,128)(2,1)} %bitcast.552), channel_id=1, source_target_pairs={{0,4},{4,0},{1,5},{5,1},{2,6},{6,2},{3,7},{7,3},{8,12},{12,8},{9,1... | collective-permute-start | bytes 185864 | tf_op jit(solution)/shard_map/ppermute | solution.py:25
  9.9 86.7 %collective-permute-start.43 = (bf16[128,2,176]{0,2,1:T(8,128)(2,1)}, bf16[128,2,176]{0,2,1:T(8,128)(2,1)}, u32[]{:S(2)}, u32[]{:S(2)}) collective-permute-start(bf16[128,2,176]{0,2,1:T(8,128)(2,1)} %get-tuple-element.490), channel_id=1, source_target_pairs={{0,4},{4,0},{1,5},{5,1},{2,6},{6,2},{3,7},{7,3},{8,12},{12,8},{9,1... | collective-permute-start | bytes 270344 | tf_op jit(solution)/shard_map/ppermute | solution.py:25
  10.0 57.7 %collective-permute-start = (bf16[1,88,1408]{2,1,0:T(8,128)(2,1)}, bf16[1,88,1408]{2,1,0:T(8,128)(2,1)}, u32[]{:S(2)}, u32[]{:S(2)}) collective-permute-start(bf16[1,88,1408]{2,1,0:T(8,128)(2,1)} %bitcast.5), channel_id=1, source_target_pairs={{0,1},{1,0},{2,3},{3,2},{4,5},{5,4},{6,7},{7,6},{8,9},{9,8},{10,11... | collective-permute-start | bytes 743432 | tf_op jit(solution)/shard_map/ppermute | solution.py:25
  55.5 63.1 %collective-permute-start.27 = (bf16[176,3,176]{2,0,1:T(8,128)(2,1)S(1)}, bf16[176,3,176]{2,0,1:T(8,128)(2,1)}, u32[]{:S(2)}, u32[]{:S(2)}) collective-permute-start(bf16[176,3,176]{2,0,1:T(8,128)(2,1)S(1)} %bitcast.669), channel_id=1, source_target_pairs={{0,4},{4,0},{1,5},{5,1},{2,6},{6,2},{3,7},{7,3},{8,12},{12,8},{9,1... | collective-permute-start | bytes 557576 | tf_op jit(solution)/shard_map/ppermute | solution.py:25
  124.5 51.1 %collective-permute-start.2 = (bf16[352,1408]{1,0:T(8,128)(2,1)}, bf16[352,1408]{1,0:T(8,128)(2,1)}, u32[]{:S(2)}, u32[]{:S(2)}) collective-permute-start(bf16[352,1408]{1,0:T(8,128)(2,1)} %bitcast.6.refs_2_), channel_id=1, source_target_pairs={{0,4},{4,0},{1,5},{5,1},{2,6},{6,2},{3,7},{7,3},{8,12},{12,8},{9,1... | collective-permute-start | bytes 2973704 | tf_op jit(solution)/shard_map/ppermute | solution.py:25
  127.7 49.3 %collective-permute-start.4 = (bf16[352,1408]{1,0:T(8,128)(2,1)}, bf16[352,1408]{1,0:T(8,128)(2,1)}, u32[]{:S(2)}, u32[]{:S(2)}) collective-permute-start(bf16[352,1408]{1,0:T(8,128)(2,1)} %collective-permute-done.3.refs_4_), channel_id=1, source_target_pairs={{0,4},{4,0},{1,5},{5,1},{2,6},{6,2},{3,7},{7,3},{8,12},{12,8},{9,1... | collective-permute-start | bytes 2973704 | tf_op jit(solution)/shard_map/ppermute | solution.py:25
  127.7 47.8 %collective-permute-start.6 = (bf16[352,1408]{1,0:T(8,128)(2,1)}, bf16[352,1408]{1,0:T(8,128)(2,1)}, u32[]{:S(2)}, u32[]{:S(2)}) collective-permute-start(bf16[352,1408]{1,0:T(8,128)(2,1)} %collective-permute-done.5.refs_6_), channel_id=1, source_target_pairs={{0,4},{4,0},{1,5},{5,1},{2,6},{6,2},{3,7},{7,3},{8,12},{12,8},{9,1... | collective-permute-start | bytes 2973704 | tf_op jit(solution)/shard_map/ppermute | solution.py:25
  175.5 70.3 %collective-permute-start.31 = (bf16[4,352,528]{1,2,0:T(8,128)(2,1)}, bf16[4,352,528]{1,2,0:T(8,128)(2,1)}, u32[]{:S(2)}, u32[]{:S(2)}) collective-permute-start(bf16[4,352,528]{1,2,0:T(8,128)(2,1)} %copy.309), channel_id=1, source_target_pairs={{0,16},{8,24},{16,0},{24,8},{1,17},{9,25},{17,1},{25,9},{2,18},{10... | collective-permute-start | bytes 4460552 | tf_op jit(solution)/shard_map/ppermute | solution.py:25
  219.9 52.9 %collective-permute-start.30 = (bf16[4,352,528]{1,2,0:T(8,128)(2,1)}, bf16[4,352,528]{1,2,0:T(8,128)(2,1)}, u32[]{:S(2)}, u32[]{:S(2)}) collective-permute-start(bf16[4,352,528]{1,2,0:T(8,128)(2,1)} %copy.308), channel_id=1, source_target_pairs={{0,8},{8,0},{16,24},{24,16},{1,9},{9,1},{17,25},{25,17},{2,10},{10... | collective-permute-start | bytes 4460552 | tf_op jit(solution)/shard_map/ppermute | solution.py:25
  257.7 79.0 %collective-permute-start.32 = (bf16[4,352,528]{1,2,0:T(8,128)(2,1)}, bf16[4,352,528]{1,2,0:T(8,128)(2,1)}, u32[]{:S(2)}, u32[]{:S(2)}) collective-permute-start(bf16[4,352,528]{1,2,0:T(8,128)(2,1)} %collective-permute-done.31), channel_id=1, source_target_pairs={{0,8},{8,0},{16,24},{24,16},{1,9},{9,1},{17,25},{25,17},{2,10},{10... | collective-permute-start | bytes 4460552 | tf_op jit(solution)/shard_map/ppermute | solution.py:25
  265.8 76.3 %collective-permute-start.26 = (bf16[512,1408]{1,0:T(8,128)(2,1)}, bf16[512,1408]{1,0:T(8,128)(2,1)}, u32[]{:S(2)}, u32[]{:S(2)}) collective-permute-start(bf16[512,1408]{1,0:T(8,128)(2,1)} %norm.3), channel_id=1, source_target_pairs={{0,4},{4,0},{1,5},{5,1},{2,6},{6,2},{3,7},{7,3},{8,12},{12,8},{9,1... | collective-permute-start | bytes 4325384 | tf_op jit(solution)/shard_map/ppermute | solution.py:25
  313.2 111.9 %collective-permute-start.51 = (bf16[4,256,352]{1,2,0:T(8,128)(2,1)}, bf16[4,256,352]{1,2,0:T(8,128)(2,1)}, u32[]{:S(2)}, u32[]{:S(2)}) collective-permute-start(bf16[4,256,352]{1,2,0:T(8,128)(2,1)} %copy.333), channel_id=1, source_target_pairs={{0,16},{8,24},{16,0},{24,8},{1,17},{9,25},{17,1},{25,9},{2,18},{10... | collective-permute-start | bytes 2162696 | tf_op jit(solution)/shard_map/ppermute | solution.py:25
  316.6 114.2 %collective-permute-start.70 = (bf16[1,2,352,512]{3,2,1,0:T(8,128)(2,1)}, bf16[1,2,352,512]{3,2,1,0:T(8,128)(2,1)}, u32[]{:S(2)}, u32[]{:S(2)}) collective-permute-start(bf16[1,2,352,512]{3,2,1,0:T(8,128)(2,1)} %get-tuple-element.183), channel_id=1, source_target_pairs={{0,1},{1,0},{2,3},{3,2},{4,5},{5,4},{6,7},{7,6},{8,9},{9,8},{10,11... | collective-permute-start | bytes 2162696 | tf_op jit(solution)/shard_map/ppermute | solution.py:25
  333.5 95.0 %collective-permute-start.75 = (bf16[1,1,352,512]{3,2,1,0:T(8,128)(2,1)}, bf16[1,1,352,512]{3,2,1,0:T(8,128)(2,1)}, u32[]{:S(2)}, u32[]{:S(2)}) collective-permute-start(bf16[1,1,352,512]{3,2,1,0:T(8,128)(2,1)} %reshape_broadcast_in_dim_reshape_squeeze.10), channel_id=1, source_target_pairs={{0,2},{1,3},{2,0},{3,1},{4,6},{5,7},{6,4},{7,5},{8,10},{9,11},{10,... | collective-permute-start | bytes 1081352 | tf_op jit(solution)/shard_map/ppermute | solution.py:25
  336.8 96.2 %collective-permute-start.50 = (bf16[4,352,176]{1,2,0:T(8,128)(2,1)}, bf16[4,352,176]{1,2,0:T(8,128)(2,1)}, u32[]{:S(2)}, u32[]{:S(2)}) collective-permute-start(bf16[4,352,176]{1,2,0:T(8,128)(2,1)} %copy.332), channel_id=1, source_target_pairs={{0,16},{8,24},{16,0},{24,8},{1,17},{9,25},{17,1},{25,9},{2,18},{10... | collective-permute-start | bytes 1486856 | tf_op jit(solution)/shard_map/ppermute | solution.py:25
  342.1 93.0 %collective-permute-start.48 = (bf16[4,256,352]{1,2,0:T(8,128)(2,1)}, bf16[4,256,352]{1,2,0:T(8,128)(2,1)}, u32[]{:S(2)}, u32[]{:S(2)}) collective-permute-start(bf16[4,256,352]{1,2,0:T(8,128)(2,1)} %copy.330), channel_id=1, source_target_pairs={{0,8},{8,0},{16,24},{24,16},{1,9},{9,1},{17,25},{25,17},{2,10},{10... | collective-permute-start | bytes 2162696 | tf_op jit(solution)/shard_map/ppermute | solution.py:25
  425.0 46.1 %collective-permute-start.39 = (bf16[512,1408]{1,0:T(8,128)(2,1)}, bf16[512,1408]{1,0:T(8,128)(2,1)}, u32[]{:S(2)}, u32[]{:S(2)}) collective-permute-start(bf16[512,1408]{1,0:T(8,128)(2,1)} %get-tuple-element.160), channel_id=1, source_target_pairs={{0,4},{4,0},{1,5},{5,1},{2,6},{6,2},{3,7},{7,3},{8,12},{12,8},{9,1... | collective-permute-start | bytes 4325384 | tf_op jit(solution)/shard_map/ppermute | solution.py:25
  488.9 76.6 %collective-permute-start.77 = (bf16[4,352,512]{2,1,0:T(8,128)(2,1)}, bf16[4,352,512]{2,1,0:T(8,128)(2,1)}, u32[]{:S(2)}, u32[]{:S(2)}) collective-permute-start(bf16[4,352,512]{2,1,0:T(8,128)(2,1)} %bitcast.107.refs_4_), channel_id=1, source_target_pairs={{0,8},{8,0},{16,24},{24,16},{1,9},{9,1},{17,25},{25,17},{2,10},{10... | collective-permute-start | bytes 4325384 | tf_op jit(solution)/shard_map/ppermute | solution.py:25
  490.3 79.6 %collective-permute-start.72 = (bf16[4,352,512]{2,1,0:T(8,128)(2,1)}, bf16[4,352,512]{2,1,0:T(8,128)(2,1)}, u32[]{:S(2)}, u32[]{:S(2)}) collective-permute-start(bf16[4,352,512]{2,1,0:T(8,128)(2,1)} %bitcast.97.refs_4_), channel_id=1, source_target_pairs={{0,16},{8,24},{16,0},{24,8},{1,17},{9,25},{17,1},{25,9},{2,18},{10... | collective-permute-start | bytes 4325384 | tf_op jit(solution)/shard_map/ppermute | solution.py:25
  519.2 51.0 %collective-permute-start.65 = (bf16[128,1408]{1,0:T(8,128)(2,1)}, bf16[128,1408]{1,0:T(8,128)(2,1)S(1)}, u32[]{:S(2)}, u32[]{:S(2)}) collective-permute-start(bf16[128,1408]{1,0:T(8,128)(2,1)} %get-tuple-element.418), channel_id=1, source_target_pairs={{0,3},{1,2},{2,1},{3,0},{4,7},{5,6},{6,5},{7,4},{8,11},{9,10},{10,... | collective-permute-start | bytes 1081352 | tf_op jit(solution)/shard_map/ppermute | solution.py:25
  520.4 50.0 %collective-permute-start.64 = (bf16[128,1408]{1,0:T(8,128)(2,1)}, bf16[128,1408]{1,0:T(8,128)(2,1)}, u32[]{:S(2)}, u32[]{:S(2)}) collective-permute-start(bf16[128,1408]{1,0:T(8,128)(2,1)} %get-tuple-element.419), channel_id=1, source_target_pairs={{0,2},{1,3},{2,0},{3,1},{4,6},{5,7},{6,4},{7,5},{8,10},{9,11},{10,... | collective-permute-start | bytes 1081352 | tf_op jit(solution)/shard_map/ppermute | solution.py:25
  522.5 49.2 %collective-permute-start.63 = (bf16[128,1408]{1,0:T(8,128)(2,1)}, bf16[128,1408]{1,0:T(8,128)(2,1)}, u32[]{:S(2)}, u32[]{:S(2)}) collective-permute-start(bf16[128,1408]{1,0:T(8,128)(2,1)} %get-tuple-element.420), channel_id=1, source_target_pairs={{0,1},{1,0},{2,3},{3,2},{4,5},{5,4},{6,7},{7,6},{8,9},{9,8},{10,11... | collective-permute-start | bytes 1081352 | tf_op jit(solution)/shard_map/ppermute | solution.py:25
  570.4 63.8 %collective-permute-start.78 = (bf16[4,352,512]{2,1,0:T(8,128)(2,1)}, bf16[4,352,512]{2,1,0:T(8,128)(2,1)}, u32[]{:S(2)}, u32[]{:S(2)}) collective-permute-start(bf16[4,352,512]{2,1,0:T(8,128)(2,1)} %bitcast.107.refs_4_), channel_id=1, source_target_pairs={{0,16},{8,24},{16,0},{24,8},{1,17},{9,25},{17,1},{25,9},{2,18},{10... | collective-permute-start | bytes 4325384 | tf_op jit(solution)/shard_map/ppermute | solution.py:25
  574.5 61.9 %collective-permute-start.66 = (bf16[512,1408]{1,0:T(8,128)(2,1)}, bf16[512,1408]{1,0:T(8,128)(2,1)}, u32[]{:S(2)}, u32[]{:S(2)}) collective-permute-start(bf16[512,1408]{1,0:T(8,128)(2,1)} %bitcast.87.refs_7_), channel_id=1, source_target_pairs={{0,4},{4,0},{1,5},{5,1},{2,6},{6,2},{3,7},{7,3},{8,12},{12,8},{9,1... | collective-permute-start | bytes 4325384 | tf_op jit(solution)/shard_map/ppermute | solution.py:25
  583.8 61.9 %collective-permute-start.61 = (bf16[512,1408]{0,1:T(8,128)(2,1)S(1)}, bf16[512,1408]{0,1:T(8,128)(2,1)}, u32[]{:S(2)}, u32[]{:S(2)}) collective-permute-start(bf16[512,1408]{0,1:T(8,128)(2,1)S(1)} %copy.347), channel_id=1, source_target_pairs={{0,4},{4,0},{1,5},{5,1},{2,6},{6,2},{3,7},{7,3},{8,12},{12,8},{9,1... | collective-permute-start | bytes 4325384 | tf_op jit(solution)/shard_map/ppermute | solution.py:25
  603.3 61.8 %collective-permute-start.84 = (bf16[4,352,512]{2,1,0:T(8,128)(2,1)}, bf16[4,352,512]{2,1,0:T(8,128)(2,1)}, u32[]{:S(2)}, u32[]{:S(2)}) collective-permute-start(bf16[4,352,512]{2,1,0:T(8,128)(2,1)} %bitcast.113.refs_4_), channel_id=1, source_target_pairs={{0,16},{8,24},{16,0},{24,8},{1,17},{9,25},{17,1},{25,9},{2,18},{10... | collective-permute-start | bytes 4325384 | tf_op jit(solution)/shard_map/ppermute | solution.py:25
  634.2 61.8 %collective-permute-start.85 = (bf16[4,352,512]{2,1,0:T(8,128)(2,1)}, bf16[4,352,512]{2,1,0:T(8,128)(2,1)}, u32[]{:S(2)}, u32[]{:S(2)}) collective-permute-start(bf16[4,352,512]{2,1,0:T(8,128)(2,1)} %collective-permute-done.83.refs_5_), channel_id=1, source_target_pairs={{0,16},{8,24},{16,0},{24,8},{1,17},{9,25},{17,1},{25,9},{2,18},{10... | collective-permute-start | bytes 4325384 | tf_op jit(solution)/shard_map/ppermute | solution.py:25
  634.5 99.2 %collective-permute-start.79 = (bf16[4,352,512]{2,1,0:T(8,128)(2,1)}, bf16[4,352,512]{2,1,0:T(8,128)(2,1)}, u32[]{:S(2)}, u32[]{:S(2)}) collective-permute-start(bf16[4,352,512]{2,1,0:T(8,128)(2,1)} %collective-permute-done.78.refs_6_), channel_id=1, source_target_pairs={{0,8},{8,0},{16,24},{24,16},{1,9},{9,1},{17,25},{25,17},{2,10},{10... | collective-permute-start | bytes 4325384 | tf_op jit(solution)/shard_map/ppermute | solution.py:25
  732.7 79.2 %collective-permute-start.86 = (bf16[512,1408]{1,0:T(8,128)(2,1)}, bf16[512,1408]{1,0:T(8,128)(2,1)}, u32[]{:S(2)}, u32[]{:S(2)}) collective-permute-start(bf16[512,1408]{1,0:T(8,128)(2,1)} %get-tuple-element.202), channel_id=1, source_target_pairs={{0,4},{4,0},{1,5},{5,1},{2,6},{6,2},{3,7},{7,3},{8,12},{12,8},{9,1... | collective-permute-start | bytes 4325384 | tf_op jit(solution)/shard_map/ppermute | solution.py:25
  812.7 55.4 %collective-permute-start.166 = (bf16[4,352,512]{2,1,0:T(8,128)(2,1)}, bf16[4,352,512]{2,1,0:T(8,128)(2,1)}, u32[]{:S(2)}, u32[]{:S(2)}) collective-permute-start(bf16[4,352,512]{2,1,0:T(8,128)(2,1)} %get-tuple-element.270), channel_id=1, source_target_pairs={{0,8},{8,0},{16,24},{24,16},{1,9},{9,1},{17,25},{25,17},{2,10},{10... | collective-permute-start | bytes 4325384 | tf_op jit(solution)/shard_map/ppermute | solution.py:25
  861.1 49.6 %collective-permute-start.170 = (bf16[4,352,512]{2,1,0:T(8,128)(2,1)}, bf16[4,352,512]{2,1,0:T(8,128)(2,1)}, u32[]{:S(2)}, u32[]{:S(2)}) collective-permute-start(bf16[4,352,512]{2,1,0:T(8,128)(2,1)} %get-tuple-element.272), channel_id=1, source_target_pairs={{0,16},{8,24},{16,0},{24,8},{1,17},{9,25},{17,1},{25,9},{2,18},{10... | collective-permute-start | bytes 4325384 | tf_op jit(solution)/shard_map/ppermute | solution.py:25
  862.4 127.0 %collective-permute-start.172 = (bf16[4,352,512]{2,1,0:T(8,128)(2,1)}, bf16[4,352,512]{2,1,0:T(8,128)(2,1)}, u32[]{:S(2)}, u32[]{:S(2)}) collective-permute-start(bf16[4,352,512]{2,1,0:T(8,128)(2,1)} %add_convert_fusion.1), channel_id=1, source_target_pairs={{0,8},{8,0},{16,24},{24,16},{1,9},{9,1},{17,25},{25,17},{2,10},{10... | collective-permute-start | bytes 4325384 | tf_op jit(solution)/shard_map/ppermute | solution.py:25
  862.7 51.0 %collective-permute-start.94 = (bf16[512,1408]{1,0:T(8,128)(2,1)}, bf16[512,1408]{1,0:T(8,128)(2,1)S(1)}, u32[]{:S(2)}, u32[]{:S(2)}) collective-permute-start(bf16[512,1408]{1,0:T(8,128)(2,1)} %get-tuple-element.209), channel_id=1, source_target_pairs={{0,4},{4,0},{1,5},{5,1},{2,6},{6,2},{3,7},{7,3},{8,12},{12,8},{9,1... | collective-permute-start | bytes 4325384 | tf_op jit(solution)/shard_map/ppermute | solution.py:25
  879.8 114.1 %collective-permute-start.165 = (bf16[4,352,512]{2,1,0:T(8,128)(2,1)}, bf16[4,352,512]{2,1,0:T(8,128)(2,1)}, u32[]{:S(2)}, u32[]{:S(2)}) collective-permute-start(bf16[4,352,512]{2,1,0:T(8,128)(2,1)} %get-tuple-element.268), channel_id=1, source_target_pairs={{0,8},{8,0},{16,24},{24,16},{1,9},{9,1},{17,25},{25,17},{2,10},{10... | collective-permute-start | bytes 4325384 | tf_op jit(solution)/shard_map/ppermute | solution.py:25
  910.7 83.8 %collective-permute-start.167 = (bf16[4,352,512]{2,1,0:T(8,128)(2,1)}, bf16[4,352,512]{2,1,0:T(8,128)(2,1)}, u32[]{:S(2)}, u32[]{:S(2)}) collective-permute-start(bf16[4,352,512]{2,1,0:T(8,128)(2,1)} %add_convert_fusion.2), channel_id=1, source_target_pairs={{0,16},{8,24},{16,0},{24,8},{1,17},{9,25},{17,1},{25,9},{2,18},{10... | collective-permute-start | bytes 4325384 | tf_op jit(solution)/shard_map/ppermute | solution.py:25
  912.5 85.2 %collective-permute-start.160 = (bf16[4,352,512]{2,1,0:T(8,128)(2,1)}, bf16[4,352,512]{2,1,0:T(8,128)(2,1)}, u32[]{:S(2)}, u32[]{:S(2)}) collective-permute-start(bf16[4,352,512]{2,1,0:T(8,128)(2,1)} %get-tuple-element.264), channel_id=1, source_target_pairs={{0,16},{8,24},{16,0},{24,8},{1,17},{9,25},{17,1},{25,9},{2,18},{10... | collective-permute-start | bytes 4325384 | tf_op jit(solution)/shard_map/ppermute | solution.py:25
  913.7 84.8 %collective-permute-start.162 = (bf16[4,352,512]{2,1,0:T(8,128)(2,1)}, bf16[4,352,512]{2,1,0:T(8,128)(2,1)}, u32[]{:S(2)}, u32[]{:S(2)}) collective-permute-start(bf16[4,352,512]{2,1,0:T(8,128)(2,1)} %add_convert_fusion.3), channel_id=1, source_target_pairs={{0,8},{8,0},{16,24},{24,16},{1,9},{9,1},{17,25},{25,17},{2,10},{10... | collective-permute-start | bytes 4325384 | tf_op jit(solution)/shard_map/ppermute | solution.py:25
  1021.8 45.7 %collective-permute-start.148 = (bf16[4,256,352]{1,2,0:T(8,128)(2,1)}, bf16[4,256,352]{1,2,0:T(8,128)(2,1)}, u32[]{:S(2)}, u32[]{:S(2)}) collective-permute-start(bf16[4,256,352]{1,2,0:T(8,128)(2,1)} %copy.416), channel_id=1, source_target_pairs={{0,8},{8,0},{16,24},{24,16},{1,9},{9,1},{17,25},{25,17},{2,10},{10... | collective-permute-start | bytes 2162696 | tf_op jit(solution)/shard_map/ppermute | solution.py:25
  1032.2 49.5 %collective-permute-start.156 = (bf16[4,352,176]{1,2,0:T(8,128)(2,1)}, bf16[4,352,176]{1,2,0:T(8,128)(2,1)}, u32[]{:S(2)}, u32[]{:S(2)}) collective-permute-start(bf16[4,352,176]{1,2,0:T(8,128)(2,1)} %copy.431), channel_id=1, source_target_pairs={{0,16},{8,24},{16,0},{24,8},{1,17},{9,25},{17,1},{25,9},{2,18},{10... | collective-permute-start | bytes 1486856 | tf_op jit(solution)/shard_map/ppermute | solution.py:25
  1067.5 103.3 %collective-permute-start.95 = (bf16[512,1408]{1,0:T(8,128)(2,1)}, bf16[512,1408]{1,0:T(8,128)(2,1)}, u32[]{:S(2)}, u32[]{:S(2)}) collective-permute-start(bf16[512,1408]{1,0:T(8,128)(2,1)} %get-tuple-element.217), channel_id=1, source_target_pairs={{0,4},{4,0},{1,5},{5,1},{2,6},{6,2},{3,7},{7,3},{8,12},{12,8},{9,1... | collective-permute-start | bytes 4325384 | tf_op jit(solution)/shard_map/ppermute | solution.py:25
  1081.7 84.1 %collective-permute-start.150 = (bf16[4,256,352]{1,2,0:T(8,128)(2,1)}, bf16[4,256,352]{1,2,0:T(8,128)(2,1)}, u32[]{:S(2)}, u32[]{:S(2)}) collective-permute-start(bf16[4,256,352]{1,2,0:T(8,128)(2,1)} %copy.420), channel_id=1, source_target_pairs={{0,16},{8,24},{16,0},{24,8},{1,17},{9,25},{17,1},{25,9},{2,18},{10... | collective-permute-start | bytes 2162696 | tf_op jit(solution)/shard_map/ppermute | solution.py:25
  1134.4 54.3 %collective-permute-start.176 = (f32[176,768]{1,0:T(8,128)}, f32[176,768]{1,0:T(8,128)}, u32[]{:S(2)}, u32[]{:S(2)}) collective-permute-start(f32[176,768]{1,0:T(8,128)} %get-tuple-element.435), channel_id=1, source_target_pairs={{0,4},{4,0},{1,5},{5,1},{2,6},{6,2},{3,7},{7,3},{8,12},{12,8},{9,1... | collective-permute-start | bytes 1622024 | tf_op jit(solution)/shard_map/ppermute | solution.py:25
  1141.6 50.0 %collective-permute-start.175 = (f32[176,768]{1,0:T(8,128)}, f32[176,768]{1,0:T(8,128)}, u32[]{:S(2)}, u32[]{:S(2)}) collective-permute-start(f32[176,768]{1,0:T(8,128)} %get-tuple-element.437), channel_id=1, source_target_pairs={{0,4},{4,0},{1,5},{5,1},{2,6},{6,2},{3,7},{7,3},{8,12},{12,8},{9,1... | collective-permute-start | bytes 1622024 | tf_op jit(solution)/shard_map/ppermute | solution.py:25
  1199.4 112.9 %collective-permute-start.152 = (bf16[1,256,352]{1,2,0:T(8,128)(2,1)S(1)}, bf16[1,256,352]{1,2,0:T(8,128)(2,1)S(1)}, u32[]{:S(2)}, u32[]{:S(2)}) collective-permute-start(bf16[1,256,352]{1,2,0:T(8,128)(2,1)S(1)} %fusion.62), channel_id=1, source_target_pairs={{0,2},{1,3},{2,0},{3,1},{4,6},{5,7},{6,4},{7,5},{8,10},{9,11},{10,... | collective-permute-start | bytes 540680 | tf_op jit(solution)/shard_map/ppermute | solution.py:25
  1363.1 79.1 %collective-permute-start.131 = (bf16[4,352,528]{1,2,0:T(8,128)(2,1)}, bf16[4,352,528]{1,2,0:T(8,128)(2,1)}, u32[]{:S(2)}, u32[]{:S(2)}) collective-permute-start(bf16[4,352,528]{1,2,0:T(8,128)(2,1)} %copy.393), channel_id=1, source_target_pairs={{0,8},{8,0},{16,24},{24,16},{1,9},{9,1},{17,25},{25,17},{2,10},{10... | collective-permute-start | bytes 4460552 | tf_op jit(solution)/shard_map/ppermute | solution.py:25
  1364.0 100.5 %collective-permute-start.130 = (bf16[4,352,528]{1,2,0:T(8,128)(2,1)}, bf16[4,352,528]{1,2,0:T(8,128)(2,1)}, u32[]{:S(2)}, u32[]{:S(2)}) collective-permute-start(bf16[4,352,528]{1,2,0:T(8,128)(2,1)} %copy.391), channel_id=1, source_target_pairs={{0,8},{8,0},{16,24},{24,16},{1,9},{9,1},{17,25},{25,17},{2,10},{10... | collective-permute-start | bytes 4460552 | tf_op jit(solution)/shard_map/ppermute | solution.py:25
  1372.3 63.3 %collective-permute-start.109 = (f32[1,4,1408]{2,1,0:T(4,128)S(1)}, f32[1,4,1408]{2,1,0:T(4,128)S(1)}, u32[]{:S(2)}, u32[]{:S(2)}) collective-permute-start(f32[1,4,1408]{2,1,0:T(4,128)S(1)} %pad_maximum_fusion.53), channel_id=1, source_target_pairs={{0,8},{8,0},{16,24},{24,16},{1,9},{9,1},{17,25},{25,17},{2,10},{10... | collective-permute-start | bytes 67592 | tf_op jit(solution)/shard_map/ppermute | solution.py:25
  1464.6 85.2 %collective-permute-start.132 = (bf16[4,352,528]{1,2,0:T(8,128)(2,1)}, bf16[4,352,528]{1,2,0:T(8,128)(2,1)}, u32[]{:S(2)}, u32[]{:S(2)}) collective-permute-start(bf16[4,352,528]{1,2,0:T(8,128)(2,1)} %copy.395), channel_id=1, source_target_pairs={{0,16},{8,24},{16,0},{24,8},{1,17},{9,25},{17,1},{25,9},{2,18},{10... | collective-permute-start | bytes 4460552 | tf_op jit(solution)/shard_map/ppermute | solution.py:25
  (263 other events, 4405.1 us)

commit v2 on v1

--- a/solution.py
+++ b/solution.py
@@ -15,6 +15,7 @@
 VMEM_LIMIT = 62 * 1024 * 1024
 MLP_CHUNKS = 3
 QUERY_BLOCK = 512
+MESH = pl.DeviceIdType.MESH
 
 
 def bits_of(size):
@@ -74,39 +75,246 @@
     return jnp.concatenate([part[1], part[0], part[3], part[2]], axis=1)
 
 
-def assemble(target, pieces, chip, rows):
-    for k, piece in enumerate(pieces):
-        start = pl.multiple_of((chip ^ k) * rows, 16)
-        target[pl.ds(start, rows), :] = piece[0]
-
-
-def scatter_pieces(source, pieces, chip, rows):
-    for k, piece in enumerate(pieces):
-        start = pl.multiple_of((chip ^ k) * rows, 16)
-        piece[0] = source[pl.ds(start, rows), :]
+def of_chips(width, shape):
+    return pl.BlockSpec(shape[:1] + (1,) + shape[2:3] + (width,), lambda i, *_: (0, i, 0, 0))
+
+
+def flat(ref):
+    chips, _, rows, cols = ref.shape
+    return ref[...].reshape(chips * rows, cols)
+
+
+def flip(index, mask):
+    for bit in bits_of(2 * mask + 1):
+        if mask & bit:
+            index = index + bit - 2 * bit * (index // bit % 2)
+    return index
+
+
+def link_of(k, slot):
+    bits = [b for b in bits_of(2 * k + 1) if k & b]
+    return bits[-1] if slot % 2 == 0 else bits[0]
+
+
+def by_distance(chips):
+    return sorted(range(1, chips), key=lambda k: (bin(k).count("1"), k))
+
+
+def greet(chips, wide, with_core):
+    chip, core, lane = (lax.axis_index(n) for n in ("chip", "core", "ta"))
+    barrier = pltpu.get_barrier_semaphore()
+    partners = [{"ta": flip(lane, i)} for i in range(1, wide)]
+    partners += [{"chip": flip(chip, b)} for b in bits_of(chips)]
+    if with_core:
+        partners.append({"core": 1 - core})
+    for partner in partners:
+        pl.semaphore_signal(barrier, inc=1, device_id=partner, device_id_type=MESH)
+    pl.semaphore_wait(barrier, len(partners))
+
+
+def gather_kernel(sizes, full, *refs):
+    chips, wide = sizes
+    n = len(full)
+    shards, outs = refs[:n], refs[n : 2 * n]
+    local_sem, z_send, z_recv, x_send, x_recv, c_send, c_recv = refs[2 * n :]
+    chip, core, lane = (lax.axis_index(name) for name in ("chip", "core", "ta"))
+    greet(chips, wide, any(full))
+    sends, arrived = [], set()
+
+    def place(w, k, i):
+        if full[w]:
+            return outs[w].at[flip(chip, k), core, flip(lane, i)]
+        return outs[w].at[flip(chip, k), i]
+
+    def send(source, target, device, send_sem, recv_sem):
+        copy = pltpu.make_async_remote_copy(
+            src_ref=source, dst_ref=target, send_sem=send_sem, recv_sem=recv_sem,
+            device_id=device, device_id_type=MESH,
+        )
+        copy.start()
+        sends.append(copy)
+
+    def take(w, k, i):
+        if k == 0 and i == 0 or (w, k, i) in arrived:
+            return
+        arrived.add((w, k, i))
+        piece = place(w, k, i)
+        sem = z_recv.at[w, i - 1] if k == 0 else x_recv.at[w, i, k - 1]
+        pltpu.make_async_copy(piece, piece, sem).wait()
+
+    def near(w, i):
+        take(w, 0, i)
+        source = shards[w] if i == 0 else place(w, 0, i)
+        for bit in bits_of(chips):
+            send(source, place(w, 0, i), {"chip": flip(chip, bit)},
+                 x_send.at[w, i, bit - 1], x_recv.at[w, i, bit - 1])
+
+    def far(w, i):
+        for k in by_distance(chips):
+            bit = link_of(k, i)
+            held = k ^ bit
+            if held:
+                take(w, held, i)
+                piece = place(w, held, i)
+                send(piece, piece, {"chip": flip(chip, bit)}, x_send.at[w, i, k - 1], x_recv.at[w, i, k - 1])
+
+    locals_ = []
+    for w in range(n):
+        copy = pltpu.make_async_copy(shards[w], place(w, 0, 0), local_sem.at[w])
+        copy.start()
+        locals_.append(copy)
+        for i in range(1, wide):
+            target = outs[w].at[chip, core, lane] if full[w] else outs[w].at[chip, i]
+            send(shards[w], target, {"ta": flip(lane, i)}, z_send.at[w, i - 1], z_recv.at[w, i - 1])
+    order = [(w, 0) for w in range(n)] + [(w, i) for w in range(n) for i in range(1, wide)]
+    for t, (w, i) in enumerate(order):
+        near(w, i)
+        if t >= 2:
+            far(*order[t - 2])
+    for w, i in order[-2:]:
+        far(w, i)
+    for copy in locals_:
+        copy.wait()
+    for w in range(n):
+        if full[w]:
+            for k in range(chips):
+                for i in range(wide):
+                    take(w, k, i)
+                send(outs[w].at[flip(chip, k), core], outs[w].at[flip(chip, k), core], {"core": 1 - core},
+                     c_send.at[w, k], c_recv.at[w, k])
+    for w in range(n):
+        for i in range(wide):
+            for k in range(chips):
+                take(w, k, i)
+        if full[w]:
+            for k in range(chips):
+                piece = outs[w].at[flip(chip, k), 1 - core]
+                pltpu.make_async_copy(piece, piece, c_recv.at[w, k]).wait()
+    for copy in sends:
+        copy.wait_send()
+
+
+def gather(sizes, shards, full, number):
+    chips, wide = sizes
+    n = len(shards)
+    shapes = [
+        ((chips, 2, wide) if f else (chips, wide)) + tuple(s.shape) for s, f in zip(shards, full)
+    ]
+    dma = pltpu.SemaphoreType.DMA
+    return pl.pallas_call(
+        functools.partial(gather_kernel, sizes, full),
+        in_specs=[pl.BlockSpec(memory_space=pltpu.VMEM)] * n,
+        out_specs=[pl.BlockSpec(memory_space=pl.ANY)] * n,
+        out_shape=[shape_of(shape, s.dtype) for shape, s in zip(shapes, shards)],
+        scratch_shapes=[
+            dma((n,)), dma((n, wide - 1)), dma((n, wide - 1)), dma((n, wide, chips - 1)),
+            dma((n, wide, chips - 1)), dma((n, chips)), dma((n, chips)),
+        ],
+        compiler_params=pltpu.CompilerParams(
+            collective_id=number, has_side_effects=True, vmem_limit_bytes=VMEM_LIMIT
+        ),
+        name="gather",
+    )(*shards)
+
+
+def scatter_kernel(sizes, absolute, *refs):
+    chips, wide = sizes
+    n = len(absolute)
+    sources, outs, nearby, along = (refs[j * n : (j + 1) * n] for j in range(4))
+    x_send, x_recv, z_send, z_recv = refs[4 * n :]
+    chip, lane = lax.axis_index("chip"), lax.axis_index("ta")
+    greet(chips, wide, False)
+    sends = []
+
+    def send(source, target, device, send_sem, recv_sem):
+        copy = pltpu.make_async_remote_copy(
+            src_ref=source, dst_ref=target, send_sem=send_sem, recv_sem=recv_sem,
+            device_id=device, device_id_type=MESH,
+        )
+        copy.start()
+        sends.append(copy)
+
+    def own(w, k, i):
+        return sources[w].at[flip(chip, k), flip(lane, i) if absolute[w] else i]
+
+    def children(q, i):
+        return [k for k in by_distance(chips) if k ^ link_of(k, i) == q]
+
+    def total(w, q, i):
+        value = own(w, q, i)[...].astype(F32)
+        for k in children(q, i):
+            piece = nearby[w].at[i, k - 1]
+            pltpu.make_async_copy(piece, piece, x_recv.at[w, i, k - 1]).wait()
+            value = value + piece[...].astype(F32)
+        return value
+
+    def pass_on(source, w, k, i):
+        send(source, nearby[w].at[i, k - 1], {"chip": flip(chip, link_of(k, i))},
+             x_send.at[w, i, k - 1], x_recv.at[w, i, k - 1])
+
+    order = [(w, i) for w in range(n) for i in (*range(1, wide), 0)]
+    for w, i in order:
+        for k in by_distance(chips)[::-1]:
+            if not children(k, i):
+                pass_on(own(w, k, i), w, k, i)
+    for w, i in order:
+        for k in by_distance(chips)[::-1]:
+            if children(k, i):
+                place = nearby[w].at[i, children(k, i)[0] - 1]
+                place[...] = total(w, k, i).astype(BF16)
+                pass_on(place, w, k, i)
+    for w, i in order:
+        value = total(w, 0, i)
+        if i == 0:
+            outs[w][...] = value
+        else:
+            place = nearby[w].at[i, children(0, i)[0] - 1]
+            place[...] = value.astype(BF16)
+            send(place, along[w].at[i - 1], {"ta": flip(lane, i)}, z_send.at[w, i - 1], z_recv.at[w, i - 1])
+    for w in range(n):
+        value = outs[w][...]
+        for i in range(1, wide):
+            piece = along[w].at[i - 1]
+            pltpu.make_async_copy(piece, piece, z_recv.at[w, i - 1]).wait()
+            value = value + piece[...].astype(F32)
+        outs[w][...] = value
+    for copy in sends:
+        copy.wait_send()
+
+
+def scatter(sizes, parts, absolute, number):
+    chips, wide = sizes
+    n = len(parts)
+    ends = [tuple(p.shape[2:]) for p in parts]
+    dma = pltpu.SemaphoreType.DMA
+    return pl.pallas_call(
+        functools.partial(scatter_kernel, sizes, absolute),
+        in_specs=[pl.BlockSpec(memory_space=pltpu.VMEM)] * n,
+        out_specs=[pl.BlockSpec(memory_space=pltpu.VMEM)] * n,
+        out_shape=[shape_of(e, F32) for e in ends],
+        scratch_shapes=[pltpu.VMEM((wide, chips - 1) + e, BF16) for e in ends]
+        + [pltpu.VMEM((wide - 1,) + e, BF16) for e in ends]
+        + [
+            dma((n, wide, chips - 1)), dma((n, wide, chips - 1)), dma((n, wide - 1)), dma((n, wide - 1)),
+        ],
+        compiler_params=pltpu.CompilerParams(
+            collective_id=number, has_side_effects=True, vmem_limit_bytes=VMEM_LIMIT
+        ),
+        name="scatter",
+    )(*parts)
 
 
 def column_sum(values):
     return jnp.sum(values, axis=0, keepdims=True)
 
 
-def self_forward_kernel(counts, chip_ref, *refs):
-    chips, heads, size, own = counts
-    refs = list(refs)
-    take = lambda n: [refs.pop(0) for _ in range(n)]
-    (x_ref,) = take(1)
-    proj = take(chips)
-    (bias_ref,) = take(1)
-    comb = take(chips)
-    gains, shifts, cosine, sine = take(4)
-    low_ref, pre_ref, att_ref, lse_ref, own_ref, other_ref = take(6)
-    wp, wc, acc = take(3)
+def self_forward_kernel(counts, x_ref, w_ref, bias_ref, gains, shifts, cosine, sine, low_ref, pre_ref, att_ref,
+                        lse_ref, own_ref, other_ref, acc):
+    heads, size, own = counts
     step = pl.program_id(0)
-    chip = chip_ref[0]
-    assemble(wp, proj, chip, proj[0].shape[1])
-    assemble(wc, comb, chip, comb[0].shape[1])
     width = heads * size
-    packed = dot(x_ref[...], wp[...], 1, 0) + bias_ref[0]
+    weights = flat(w_ref)
+    packed = dot(x_ref[...], weights[:, : 3 * width], 1, 0) + bias_ref[0]
     pre_ref[0] = packed[:, : 2 * width].astype(BF16)
     value_low = packed[:, 2 * width :].astype(BF16)
     length = packed.shape[0]
@@ -140,7 +348,7 @@
     att = jnp.concatenate(mixes, axis=1).astype(BF16)
     att_ref[0] = att
     lse_ref[0] = jnp.concatenate(logs, axis=0)
-    term = dot(att, wc[...], 1, 1)
+    term = dot(att, weights[:, 3 * width :], 1, 1)
 
     @pl.when(step == 0)
     def _():
@@ -156,37 +364,27 @@
         other_ref[...] = acc[own:, :].astype(BF16)
 
 
-def self_forward(chip, x, proj, bias, comb, gains, shifts, cosine, sine, own):
+def self_forward(x, weights, bias, gains, shifts, cosine, sine, own):
     length, width = x.shape
-    groups, rows, cols = proj[0].shape
+    chips, groups, rows, all_cols = weights.shape
     size = gains.shape[1]
-    heads = cols // (3 * size)
-    chips = len(proj)
-    small = heads * size
+    small = all_cols // 4
+    cols = 3 * small
+    heads = small // size
     return pl.pallas_call(
-        functools.partial(self_forward_kernel, (chips, heads, size, own)),
-        grid_spec=pltpu.PrefetchScalarGridSpec(
-            num_scalar_prefetch=1,
-            grid=(groups,),
-            in_specs=[whole(x.shape)]
-            + [per_step(p.shape) for p in proj]
-            + [per_step(bias.shape)]
-            + [per_step(p.shape) for p in comb]
-            + [whole(gains.shape), whole(shifts.shape), whole(cosine.shape), whole(sine.shape)],
-            out_specs=[
-                per_step((groups, length, cols)),
-                per_step((groups, length, 2 * small)),
-                per_step((groups, length, small)),
-                per_step((groups, heads, length)),
-                whole((own, width)),
-                whole((length - own, width)),
-            ],
-            scratch_shapes=[
-                pltpu.VMEM((rows * chips, cols), BF16),
-                pltpu.VMEM((rows * chips, small), BF16),
-                pltpu.VMEM((length, width), F32),
-            ],
-        ),
+        functools.partial(self_forward_kernel, (heads, size, own)),
+        grid=(groups,),
+        in_specs=[whole(x.shape), of_chips(all_cols, weights.shape), per_step(bias.shape)]
+        + [whole(gains.shape), whole(shifts.shape), whole(cosine.shape), whole(sine.shape)],
+        out_specs=[
+            per_step((groups, length, cols)),
+            per_step((groups, length, 2 * small)),
+            per_step((groups, length, small)),
+            per_step((groups, heads, length)),
+            whole((own, width)),
+            whole((length - own, width)),
+        ],
+        scratch_shapes=[pltpu.VMEM((length, width), F32)],
         out_shape=[
             shape_of((groups, length, cols), BF16),
             shape_of((groups, length, 2 * small), BF16),
@@ -197,7 +395,7 @@
         ],
         compiler_params=params(),
         name="self_forward",
-    )(chip, x, *proj, bias, *comb, gains, shifts, cosine, sine)
+    )(x, weights, bias, gains, shifts, cosine, sine)
 
 
 def attention_back(query, key, value, out_grad, logs, block, limit=None):
@@ -222,35 +420,22 @@
     return jnp.concatenate(query_parts, axis=0), key_grad, value_grad
 
 
-def self_backward_kernel(counts, chip_ref, *refs):
-    chips, heads, size, own = counts
-    refs = list(refs)
-    take = lambda n: [refs.pop(0) for _ in range(n)]
-    x_ref, grad_ref = take(2)
-    proj = take(chips)
-    comb = take(chips)
-    low_ref, pre_ref, att_ref, lse_ref = take(4)
-    gains, cosine, sine = take(3)
-    proj_out = take(chips)
-    comb_out = take(chips)
-    own_ref, other_ref, column_ref, head_ref = take(4)
-    wp, wc, acc, grad_t, x_t = take(5)
+def self_backward_kernel(counts, x_ref, grad_ref, w_ref, low_ref, pre_ref, att_ref, lse_ref, gains, cosine, sine,
+                         w_out, own_ref, other_ref, column_ref, head_ref, acc, grad_t, x_t):
+    heads, size, own = counts
     step = pl.program_id(0)
-    chip = chip_ref[0]
-    rows = proj[0].shape[1]
-    assemble(wp, proj, chip, rows)
-    assemble(wc, comb, chip, rows)
     width = heads * size
     scale = size**-0.5
+    weights = flat(w_ref)
+    chips, _, rows, _ = w_ref.shape
 
     @pl.when(step == 0)
     def _():
         grad_t[...] = jnp.transpose(grad_ref[...])
         x_t[...] = jnp.transpose(x_ref[...])
 
-    out_grad = dot(grad_ref[...], wc[...], 1, 0).astype(BF16)
-    wc[...] = dot(grad_t[...], att_ref[0], 1, 0).astype(BF16)
-    scatter_pieces(wc, comb_out, chip, rows)
+    out_grad = dot(grad_ref[...], weights[:, 3 * width :], 1, 0).astype(BF16)
+    comb_grad = dot(grad_t[...], att_ref[0], 1, 0).astype(BF16)
     cos, sin = cosine[...], sine[...]
     block = min(QUERY_BLOCK, out_grad.shape[0])
     query_grads, key_grads, value_grads = [], [], []
@@ -273,9 +458,9 @@
         value_grads.append(dv)
     packed = jnp.concatenate(query_grads + key_grads + value_grads, axis=1).astype(BF16)
     column_ref[0] = column_sum(packed.astype(F32))
-    term = dot(packed, wp[...], 1, 1)
-    wp[...] = dot(x_t[...], packed, 1, 0).astype(BF16)
-    scatter_pieces(wp, proj_out, chip, rows)
+    term = dot(packed, weights[:, : 3 * width], 1, 1)
+    proj_grad = dot(x_t[...], packed, 1, 0).astype(BF16)
+    w_out[:, 0] = jnp.concatenate([proj_grad, comb_grad], axis=1).reshape(chips, rows, 4 * width)
     head_sums = jnp.concatenate(sums, axis=0)
 
     @pl.when(step == 0)
@@ -294,42 +479,33 @@
         other_ref[...] = acc[own:, :].astype(BF16)
 
 
-def self_backward(chip, x, grad, proj, comb, low, pre, att, lse, gains, cosine, sine, own):
+def self_backward(x, grad, weights, low, pre, att, lse, gains, cosine, sine, own):
     length, width = x.shape
-    groups, rows, cols = proj[0].shape
+    chips, groups, rows, all_cols = weights.shape
     size = gains.shape[1]
-    heads = cols // (3 * size)
-    chips = len(proj)
-    small = heads * size
-    out = pl.pallas_call(
-        functools.partial(self_backward_kernel, (chips, heads, size, own)),
-        grid_spec=pltpu.PrefetchScalarGridSpec(
-            num_scalar_prefetch=1,
-            grid=(groups,),
-            in_specs=[whole(x.shape), whole(grad.shape)]
-            + [per_step(p.shape) for p in proj]
-            + [per_step(p.shape) for p in comb]
-            + [per_step(v.shape) for v in (low, pre, att, lse)]
-            + [whole(gains.shape), whole(cosine.shape), whole(sine.shape)],
-            out_specs=[per_step(p.shape) for p in proj]
-            + [per_step(p.shape) for p in comb]
-            + [
-                whole((own, width)),
-                whole((length - own, width)),
-                per_step((groups, 1, cols)),
-                whole((4, size)),
-            ],
-            scratch_shapes=[
-                pltpu.VMEM((rows * chips, cols), BF16),
-                pltpu.VMEM((rows * chips, small), BF16),
-                pltpu.VMEM((length, width), F32),
-                pltpu.VMEM((width, length), BF16),
-                pltpu.VMEM((width, length), BF16),
-            ],
-        ),
-        out_shape=[shape_of(p.shape, BF16) for p in proj]
-        + [shape_of(p.shape, BF16) for p in comb]
-        + [
+    small = all_cols // 4
+    cols = 3 * small
+    heads = small // size
+    return pl.pallas_call(
+        functools.partial(self_backward_kernel, (heads, size, own)),
+        grid=(groups,),
+        in_specs=[whole(x.shape), whole(grad.shape), of_chips(all_cols, weights.shape)]
+        + [per_step(v.shape) for v in (low, pre, att, lse)]
+        + [whole(gains.shape), whole(cosine.shape), whole(sine.shape)],
+        out_specs=[
+            of_chips(all_cols, weights.shape),
+            whole((own, width)),
+            whole((length - own, width)),
+            per_step((groups, 1, cols)),
+            whole((4, size)),
+        ],
+        scratch_shapes=[
+            pltpu.VMEM((length, width), F32),
+            pltpu.VMEM((width, length), BF16),
+            pltpu.VMEM((width, length), BF16),
+        ],
+        out_shape=[
+            shape_of(weights.shape, BF16),
             shape_of((own, width), F32),
             shape_of((length - own, width), BF16),
             shape_of((groups, 1, cols), F32),
@@ -337,29 +513,17 @@
         ],
         compiler_params=params(),
         name="self_backward",
-    )(chip, x, grad, *proj, *comb, low, pre, att, lse, gains, cosine, sine)
-    return out[:chips], out[chips : 2 * chips], *out[2 * chips :]
-
-
-def cross_forward_kernel(counts, chip_ref, *refs):
-    chips, heads, size, own, limit = counts
-    refs = list(refs)
-    take = lambda n: [refs.pop(0) for _ in range(n)]
-    x_ref, text_ref = take(2)
-    query_w = take(chips)
-    memory_w = take(chips)
-    blend = take(chips)
-    bias_ref, memory_bias, gains, shifts = take(4)
-    low_ref, pre_ref, memory_ref, memory_pre, att_ref, lse_ref, own_ref, other_ref = take(8)
-    wq, wm, wb, acc = take(4)
+    )(x, grad, weights, low, pre, att, lse, gains, cosine, sine)
+
+
+def cross_forward_kernel(counts, x_ref, text_ref, w_ref, memory_w, bias_ref, memory_bias, gains, shifts, low_ref,
+                         pre_ref, memory_ref, memory_pre, att_ref, lse_ref, own_ref, other_ref, acc):
+    heads, size, own, limit = counts
     step = pl.program_id(0)
-    chip = chip_ref[0]
-    assemble(wq, query_w, chip, query_w[0].shape[1])
-    assemble(wm, memory_w, chip, memory_w[0].shape[1])
-    assemble(wb, blend, chip, blend[0].shape[1])
     width = heads * size
-    pre = dot(x_ref[...], wq[...], 1, 0) + bias_ref[0]
-    memory = dot(text_ref[...], wm[...], 1, 0) + memory_bias[0]
+    weights = flat(w_ref)
+    pre = dot(x_ref[...], weights[:, :width], 1, 0) + bias_ref[0]
+    memory = dot(text_ref[...], flat(memory_w), 1, 0) + memory_bias[0]
     pre_ref[0] = pre.astype(BF16)
     memory_pre[0] = memory[:, :width].astype(BF16)
     value_low = memory[:, width:].astype(BF16)
@@ -393,7 +557,7 @@
     att = jnp.concatenate(mixes, axis=1).astype(BF16)
     att_ref[0] = att
     lse_ref[0] = jnp.concatenate(logs, axis=0)
-    term = dot(att, wb[...], 1, 1)
+    term = dot(att, weights[:, width:], 1, 1)
 
     @pl.when(step == 0)
     def _():
@@ -409,14 +573,12 @@
         other_ref[...] = acc[own:, :].astype(BF16)
 
 
-def cross_forward(chip, x, text, query_w, memory_w, blend, bias, memory_bias, gains, shifts, own, limit):
+def cross_forward(x, text, weights, memory_w, bias, memory_bias, gains, shifts, own, limit):
     length, width = x.shape
-    groups, rows, small = query_w[0].shape
+    groups, small = weights.shape[1], weights.shape[3] // 2
     text_rows = text.shape[0]
-    memory_rows = memory_w[0].shape[1]
     size = gains.shape[1]
     heads = small // size
-    chips = len(query_w)
     saved = [
         ((groups, length, small), BF16),
         ((groups, length, small), BF16),
@@ -426,52 +588,29 @@
         ((groups, heads, length), F32),
     ]
     return pl.pallas_call(
-        functools.partial(cross_forward_kernel, (chips, heads, size, own, limit)),
-        grid_spec=pltpu.PrefetchScalarGridSpec(
-            num_scalar_prefetch=1,
-            grid=(groups,),
-            in_specs=[whole(x.shape), whole(text.shape)]
-            + [per_step(p.shape) for p in (*query_w, *memory_w, *blend)]
-            + [per_step(bias.shape), per_step(memory_bias.shape), whole(gains.shape), whole(shifts.shape)],
-            out_specs=[per_step(s) for s, _ in saved]
-            + [whole((own, width)), whole((length - own, width))],
-            scratch_shapes=[
-                pltpu.VMEM((rows * chips, small), BF16),
-                pltpu.VMEM((memory_rows * chips, 2 * small), BF16),
-                pltpu.VMEM((rows * chips, small), BF16),
-                pltpu.VMEM((length, width), F32),
-            ],
-        ),
+        functools.partial(cross_forward_kernel, (heads, size, own, limit)),
+        grid=(groups,),
+        in_specs=[whole(x.shape), whole(text.shape)]
+        + [of_chips(v.shape[3], v.shape) for v in (weights, memory_w)]
+        + [per_step(bias.shape), per_step(memory_bias.shape), whole(gains.shape), whole(shifts.shape)],
+        out_specs=[per_step(s) for s, _ in saved] + [whole((own, width)), whole((length - own, width))],
+        scratch_shapes=[pltpu.VMEM((length, width), F32)],
         out_shape=[shape_of(*s) for s in saved]
         + [shape_of((own, width), F32), shape_of((length - own, width), BF16)],
         compiler_params=params(),
         name="cross_forward",
-    )(chip, x, text, *query_w, *memory_w, *blend, bias, memory_bias, gains, shifts)
-
-
-def cross_backward_kernel(counts, chip_ref, *refs):
-    chips, heads, size, own, limit = counts
-    refs = list(refs)
-    take = lambda n: [refs.pop(0) for _ in range(n)]
-    x_ref, grad_ref, text_ref = take(3)
-    query_w = take(chips)
-    memory_w = take(chips)
-    blend = take(chips)
-    low_ref, pre_ref, memory_ref, memory_pre, att_ref, lse_ref = take(6)
-    (gains,) = take(1)
-    query_out = take(chips)
-    memory_out = take(chips)
-    blend_out = take(chips)
-    own_ref, other_ref, text_out, column_ref, memory_column, head_ref = take(6)
-    wq, wm, wb, acc, grad_t, x_t, text_t = take(7)
+    )(x, text, weights, memory_w, bias, memory_bias, gains, shifts)
+
+
+def cross_backward_kernel(counts, x_ref, grad_ref, text_ref, w_ref, memory_w, low_ref, pre_ref, memory_ref,
+                          memory_pre, att_ref, lse_ref, gains, w_out, memory_out, own_ref, other_ref, text_out,
+                          column_ref, memory_column, head_ref, acc, grad_t, x_t, text_t):
+    heads, size, own, limit = counts
     step = pl.program_id(0)
-    chip = chip_ref[0]
-    rows, memory_rows = query_w[0].shape[1], memory_w[0].shape[1]
-    assemble(wq, query_w, chip, rows)
-    assemble(wm, memory_w, chip, memory_rows)
-    assemble(wb, blend, chip, rows)
     width = heads * size
     scale = size**-0.5
+    weights = flat(w_ref)
+    chips, _, rows, _ = w_ref.shape
 
     @pl.when(step == 0)
     def _():
@@ -479,9 +618,8 @@
         x_t[...] = jnp.transpose(x_ref[...])
         text_t[...] = jnp.transpose(text_ref[...])
 
-    out_grad = dot(grad_ref[...], wb[...], 1, 0).astype(BF16)
-    wb[...] = dot(grad_t[...], att_ref[0], 1, 0).astype(BF16)
-    scatter_pieces(wb, blend_out, chip, rows)
+    out_grad = dot(grad_ref[...], weights[:, width:], 1, 0).astype(BF16)
+    blend_grad = dot(grad_t[...], att_ref[0], 1, 0).astype(BF16)
     block = min(QUERY_BLOCK, out_grad.shape[0])
     query_grads, key_grads, value_grads = [], [], []
     sums = [None] * 3
@@ -505,12 +643,11 @@
     memory_grad = jnp.concatenate(key_grads + value_grads, axis=1).astype(BF16)
     column_ref[0] = column_sum(packed.astype(F32))
     memory_column[0] = column_sum(memory_grad.astype(F32))
-    term = dot(packed, wq[...], 1, 1)
-    text_term = dot(memory_grad, wm[...], 1, 1)
-    wq[...] = dot(x_t[...], packed, 1, 0).astype(BF16)
-    scatter_pieces(wq, query_out, chip, rows)
-    wm[...] = dot(text_t[...], memory_grad, 1, 0).astype(BF16)
-    scatter_pieces(wm, memory_out, chip, memory_rows)
+    term = dot(packed, weights[:, :width], 1, 1)
+    text_term = dot(memory_grad, flat(memory_w), 1, 1)
+    query_grad = dot(x_t[...], packed, 1, 0).astype(BF16)
+    w_out[:, 0] = jnp.concatenate([query_grad, blend_grad], axis=1).reshape(chips, rows, 2 * width)
+    memory_out[:, 0] = dot(text_t[...], memory_grad, 1, 0).astype(BF16).reshape(chips, -1, 2 * width)
     head_sums = jnp.concatenate(sums, axis=0)
 
     @pl.when(step == 0)
@@ -531,16 +668,12 @@
         other_ref[...] = acc[own:, :].astype(BF16)
 
 
-def cross_backward(
-    chip, x, grad, text, query_w, memory_w, blend, low, pre, memory, memory_pre, att, lse, gains, own, limit
-):
+def cross_backward(x, grad, text, weights, memory_w, low, pre, memory, memory_pre, att, lse, gains, own, limit):
     length, width = x.shape
-    groups, rows, small = query_w[0].shape
-    memory_rows = memory_w[0].shape[1]
+    groups, small = weights.shape[1], weights.shape[3] // 2
     size = gains.shape[1]
     heads = small // size
-    chips = len(query_w)
-    pieces = (*query_w, *memory_w, *blend)
+    pieces = (weights, memory_w)
     tail = [
         ((own, width), F32, False),
         ((length - own, width), BF16, False),
@@ -549,49 +682,33 @@
         ((groups, 1, 2 * small), F32, True),
         ((3, size), F32, False),
     ]
-    out = pl.pallas_call(
-        functools.partial(cross_backward_kernel, (chips, heads, size, own, limit)),
-        grid_spec=pltpu.PrefetchScalarGridSpec(
-            num_scalar_prefetch=1,
-            grid=(groups,),
-            in_specs=[whole(x.shape), whole(grad.shape), whole(text.shape)]
-            + [per_step(p.shape) for p in pieces]
-            + [per_step(v.shape) for v in (low, pre, memory, memory_pre, att, lse)]
-            + [whole(gains.shape)],
-            out_specs=[per_step(p.shape) for p in pieces]
-            + [per_step(s) if stepped else whole(s) for s, _, stepped in tail],
-            scratch_shapes=[
-                pltpu.VMEM((rows * chips, small), BF16),
-                pltpu.VMEM((memory_rows * chips, 2 * small), BF16),
-                pltpu.VMEM((rows * chips, small), BF16),
-                pltpu.VMEM((length, width), F32),
-                pltpu.VMEM((width, length), BF16),
-                pltpu.VMEM((width, length), BF16),
-                pltpu.VMEM((text.shape[1], text.shape[0]), BF16),
-            ],
-        ),
+    return pl.pallas_call(
+        functools.partial(cross_backward_kernel, (heads, size, own, limit)),
+        grid=(groups,),
+        in_specs=[whole(x.shape), whole(grad.shape), whole(text.shape)]
+        + [of_chips(p.shape[3], p.shape) for p in pieces]
+        + [per_step(v.shape) for v in (low, pre, memory, memory_pre, att, lse)]
+        + [whole(gains.shape)],
+        out_specs=[of_chips(p.shape[3], p.shape) for p in pieces]
+        + [per_step(s) if stepped else whole(s) for s, _, stepped in tail],
+        scratch_shapes=[
+            pltpu.VMEM((length, width), F32),
+            pltpu.VMEM((width, length), BF16),
+            pltpu.VMEM((width, length), BF16),
+            pltpu.VMEM((text.shape[1], text.shape[0]), BF16),
+        ],
         out_shape=[shape_of(p.shape, BF16) for p in pieces] + [shape_of(s, d) for s, d, _ in tail],
         compiler_params=params(),
         name="cross_backward",
-    )(chip, x, grad, text, *pieces, low, pre, memory, memory_pre, att, lse, gains)
-    return out[:chips], out[chips : 2 * chips], out[2 * chips : 3 * chips], *out[3 * chips :]
-
-
-def mlp_kernel(counts, chip_ref, *refs):
-    chips, own = counts
-    refs = list(refs)
-    take = lambda n: [refs.pop(0) for _ in range(n)]
-    x_ref, cot_ref, x_t, cot_t = take(4)
-    weights = take(chips)
-    (bias_ref,) = take(1)
-    grads = take(chips)
-    out_own, out_other, back_own, back_other, hidden_ref = take(5)
-    w, acc, back = take(3)
+    )(x, grad, text, *pieces, low, pre, memory, memory_pre, att, lse, gains)
+
+
+def mlp_kernel(own, x_ref, cot_ref, x_t, cot_t, w_ref, bias_ref, w_out, out_own, out_other, back_own, back_other,
+               hidden_ref, acc, back):
     step = pl.program_id(0)
-    chip = chip_ref[0]
-    rows = weights[0].shape[1]
-    assemble(w, weights, chip, rows)
-    tile = w.shape[1] // 2
+    chips, _, rows, cols = w_ref.shape
+    tile = cols // 2
+    w = flat(w_ref)
     hidden = dot(x_ref[...], w[:, :tile], 1, 0) + bias_ref[0]
     square = hidden * hidden
     inner = 0.7978845608028654 * hidden * (1.0 + 0.044715 * square)
@@ -616,9 +733,8 @@
         acc[...] += out_term
         back[...] += back_term
 
-    w[:, :tile] = dot(x_t[...], hidden_grad, 1, 0).astype(BF16)
-    w[:, tile:] = dot(cot_t[...], active, 1, 0).astype(BF16)
-    scatter_pieces(w, grads, chip, rows)
+    w_out[:, 0, :, :tile] = dot(x_t[...], hidden_grad, 1, 0).astype(BF16).reshape(chips, rows, tile)
+    w_out[:, 0, :, tile:] = dot(cot_t[...], active, 1, 0).astype(BF16).reshape(chips, rows, tile)
 
     @pl.when(step == pl.num_programs(0) - 1)
     def _():
@@ -628,56 +744,32 @@
         back_other[...] = back[own:, :].astype(BF16)
 
 
-def mlp(chip, x, cot, x_t, cot_t, weights, bias, own):
+def mlp(x, cot, x_t, cot_t, weights, bias, own):
     length, width = x.shape
-    groups, rows, cols = weights[0].shape
-    chips = len(weights)
+    chips, groups, rows, cols = weights.shape
+    part = pl.BlockSpec(
+        (chips, 1, rows, cols // MLP_CHUNKS), lambda i: (0, i // MLP_CHUNKS, 0, i % MLP_CHUNKS)
+    )
     tail = [((own, width), F32), ((length - own, width), BF16)] * 2
-    out = pl.pallas_call(
-        functools.partial(mlp_kernel, (chips, own)),
-        grid_spec=pltpu.PrefetchScalarGridSpec(
-            num_scalar_prefetch=1,
-            grid=(groups,),
-            in_specs=[whole(v.shape) for v in (x, cot, x_t, cot_t)]
-            + [per_step(p.shape) for p in weights]
-            + [per_step(bias.shape)],
-            out_specs=[per_step(p.shape) for p in weights]
-            + [whole(s) for s, _ in tail]
-            + [per_step(bias.shape)],
-            scratch_shapes=[
-                pltpu.VMEM((rows * chips, cols), BF16),
-                pltpu.VMEM((length, width), F32),
-                pltpu.VMEM((length, width), F32),
-            ],
-        ),
-        out_shape=[shape_of(p.shape, BF16) for p in weights]
+    return pl.pallas_call(
+        functools.partial(mlp_kernel, own),
+        grid=(groups * MLP_CHUNKS,),
+        in_specs=[whole(v.shape) for v in (x, cot, x_t, cot_t)] + [part, per_step(bias.shape)],
+        out_specs=[part] + [whole(s) for s, _ in tail] + [per_step(bias.shape)],
+        scratch_shapes=[pltpu.VMEM((length, width), F32), pltpu.VMEM((length, width), F32)],
+        out_shape=[shape_of(weights.shape, BF16)]
         + [shape_of(*s) for s in tail]
         + [shape_of(bias.shape, F32)],
         compiler_params=params(),
         name="mlp",
-    )(chip, x, cot, x_t, cot_t, *weights, bias)
-    return out[:chips], *out[chips:]
+    )(x, cot, x_t, cot_t, weights, bias)
 
 
 def row_spec(block, width):
     return pl.BlockSpec((block, width), lambda i, *_: (i, 0))
 
 
-def merge_kernel(count, index_ref, *refs):
-    refs = list(refs)
-    take = lambda n: [refs.pop(0) for _ in range(n)]
-    latent_ref, skip_ref = take(2)
-    pieces = take(count)
-    gains, biases = take(2)
-    out_ref, merger_ref = take(2)
-
-    @pl.when(pl.program_id(0) == 0)
-    def _():
-        rows = pieces[0].shape[0]
-        for k, piece in enumerate(pieces):
-            start = pl.multiple_of((index_ref[0] ^ k) * rows, 16)
-            merger_ref[pl.ds(start, rows), :] = piece[...]
-
+def merge_kernel(latent_ref, skip_ref, merger_ref, gains, biases, out_ref):
     left, right, _ = joined_norm(latent_ref, skip_ref)
     width = left.shape[1]
     left = (left * gains[0:1, :] + biases[0:1, :]).astype(BF16)
@@ -696,22 +788,18 @@
     return left * inverse, right * inverse, inverse
 
 
-def merge(index, latents, skips, pieces, gains, biases, block=128):
+def merge(latents, skips, merger, gains, biases, block=128):
     rows, width = latents.shape
     return pl.pallas_call(
-        functools.partial(merge_kernel, len(pieces)),
-        grid_spec=pltpu.PrefetchScalarGridSpec(
-            num_scalar_prefetch=1,
-            grid=(rows // block,),
-            in_specs=[row_spec(block, width)] * 2
-            + [whole(p.shape) for p in pieces]
-            + [whole(gains.shape), whole(biases.shape)],
-            out_specs=[row_spec(block, width), whole((2 * width, width))],
-        ),
-        out_shape=[shape_of((rows, width), BF16), shape_of((2 * width, width), BF16)],
+        merge_kernel,
+        grid=(rows // block,),
+        in_specs=[row_spec(block, width)] * 2
+        + [whole(merger.shape), whole(gains.shape), whole(biases.shape)],
+        out_specs=row_spec(block, width),
+        out_shape=shape_of((rows, width), BF16),
         compiler_params=params(),
         name="merge",
-    )(index, latents, skips, *pieces, gains, biases)
+    )(latents, skips, merger, gains, biases)
 
 
 def merge_back_kernel(latent_ref, skip_ref, low_ref, merger, gains, biases, left_out, right_out, merge_in, sums):
@@ -836,20 +924,6 @@
     )(*parts, value, carried, gain)
 
 
-class Links:
-    def __init__(self, depth):
-        self.depth = depth
-        self.sent = {}
-
-    def swap(self, value, axis, size, mask):
-        sent = self.sent.setdefault((axis, mask if axis == "chip" else 0), [])
-        if len(sent) >= self.depth:
-            value, _ = lax.optimization_barrier((value, sent[-self.depth]))
-        value = swap(value, axis, size, mask)
-        sent.append(value)
-        return value
-
-
 def body(sizes, latents, skips, text_states, time_embedding, merger, modulator, norm_gains, norm_biases,
          output_bias, projector, combiner, cross_query, cross_memory, blender, expander, reducer,
          column_biases, hidden_bias, per_head_norm_gains, head_shifts, cotangent):
@@ -866,9 +940,7 @@
     tensor_cols = projector.shape[2]
     head_cols = tensor_cols // 2
     hidden_cols = expander.shape[1] // 2
-    links = Links(2)
     chip_bits, wide_bits, deep_bits = bits_of(chips), bits_of(wide)[::-1], bits_of(deep)
-    chip = chip_index.astype(jnp.int32).reshape(1)
 
     everywhere = [("ta", wide, b) for b in bits_of(wide)] + [("tb", deep, b) for b in deep_bits]
     everywhere = [("core", 2, 1)] + everywhere + [("chip", chips, b) for b in chip_bits]
@@ -915,45 +987,40 @@
         other = swap(other, "core", 2, 1)
         return jnp.where(core == 0, jnp.stack([mine, other], 1), jnp.stack([other, mine], 1))
 
-    def gather_weight(value, order):
-        value = value[None]
-        count = 1
-        value = value.reshape((1,) + value.shape)
-        for mask in wide_bits:
-            other = links.swap(value, "ta", wide, mask)
-            value = jnp.stack([value, other], axis=2)
-            count *= 2
-            value = value.reshape((1, count) + value.shape[3:])
-        pieces = {0: value[0]}
-        for mask in order:
-            for k in list(pieces):
-                pieces[k ^ mask] = links.swap(pieces[k], "chip", chips, mask)
-        return [pieces[k] for k in range(chips)]
-
-    def scatter_weight(pieces, order):
-        pieces = dict(enumerate(pieces))
-        for mask in order[::-1]:
-            for k in [k for k in pieces if k & mask]:
-                received = swap(pieces.pop(k), "chip", chips, mask).astype(F32)
-                near = pieces[k ^ mask].astype(F32) + received
-                pieces[k ^ mask] = near if k == mask else near.astype(BF16)
-        value = pieces[0].astype(F32)
-        for mask in wide_bits[::-1]:
-            value = value.reshape((value.shape[0] // 2, 2) + value.shape[1:])
-            value = value[:, 0] + swap(value[:, 1].astype(BF16), "ta", wide, mask).astype(F32)
-        return value[0]
-
-    forth, back = chip_bits, chip_bits[::-1]
-
     small = jnp.concatenate(
         [v.reshape(-1) for v in (norm_gains, norm_biases, output_bias, column_biases, hidden_bias)]
     )
-    small_all = gather_all(small).reshape(devices, -1)
+    times = time_embedding
+    silu_own = jax.nn.silu(times.astype(F32)).astype(BF16)
+    small = jnp.concatenate([small, silu_own.astype(F32).reshape(-1)])[None]
+    rows, tile = projector.shape[0], hidden_cols // MLP_CHUNKS
+
+    def with_tb(value):
+        value = value[None]
+        for mask in deep_bits:
+            other = swap(value, "tb", deep, mask)
+            high = (side & mask) > 0
+            value = jnp.concatenate(
+                [jnp.where(high, other, value), jnp.where(high, value, other)], axis=0
+            )
+        return value.reshape((-1,) + value.shape[2:])
+
+    self_in = jnp.concatenate([projector, combiner.T[:, None]], axis=1)
+    self_in = halves(self_in.reshape(rows, 4, 2, head_cols).transpose(0, 2, 1, 3)).reshape(2 * rows, -1)
+    small_all, merger_full, modulator_full, self_w = gather(
+        (chips, wide), [with_tb(small), with_tb(merger), with_tb(modulator), self_in], (True, True, True, False), 1
+    )
+    merger_full = merger_full.reshape(2 * width, width)
+    modulator_full = modulator_full.reshape(width, width)
+    small_all = small_all.reshape(devices, -1)
     part = norm_gains.shape[1]
     hidden_part = hidden_bias.shape[0]
     table = jnp.transpose(small_all[:, : 21 * part].reshape(devices, 21, part), (1, 0, 2)).reshape(21, width)
     gains, biases, out_bias, columns = table[:5], table[5:14], table[14:15], table[15:21]
-    hidden_all = small_all[:, 21 * part :].reshape(wide, deep, 2, hidden_cols)
+    silu_at = 21 * part + hidden_part
+    hidden_all = small_all[:, 21 * part : silu_at].reshape(wide, deep, 2, hidden_cols)
+    silu_all = small_all[:, silu_at:].reshape(chips * 2, wide * deep, local, width)[:, 0]
+    silu_all = silu_all.reshape(latent_total, width).astype(BF16)
 
     def own_columns(value):
         value = value.reshape(value.shape[0], wide, deep, 2, -1)
@@ -968,79 +1035,20 @@
 
     own_biases = own_columns(columns)
 
-    rows = projector.shape[0]
-    merger_z = merger[None]
-    for mask in bits_of(wide):
-        other = links.swap(merger_z, "ta", wide, mask)
-        high = (lane & mask) > 0
-        merger_z = jnp.concatenate(
-            [jnp.where(high, other, merger_z), jnp.where(high, merger_z, other)], axis=0
-        )
-    merger_z = merger_z.reshape(wide, 1, *merger.shape)
-    for mask in deep_bits:
-        other = swap(merger_z, "tb", deep, mask)
-        high = (side & mask) > 0
-        merger_z = jnp.concatenate(
-            [jnp.where(high, other, merger_z), jnp.where(high, merger_z, other)], axis=1
-        )
-    merger_z = merger_z.reshape(-1, width)
-    merger_pieces = {0: merger_z}
-    for mask in forth:
-        for k in list(merger_pieces):
-            merger_pieces[k ^ mask] = links.swap(merger_pieces[k], "chip", chips, mask)
-    merger_list = []
-    for k in range(chips):
-        merger_list += [merger_pieces[k], swap(merger_pieces[k], "core", 2, 1)]
-
-    projector_in = halves(projector.reshape(rows, 3, 2, head_cols).transpose(0, 2, 1, 3))
-    projector_w = gather_weight(projector_in.reshape(2 * rows, 3 * head_cols), back)
-    combiner_w = gather_weight(halves(combiner.T.reshape(rows, 2, head_cols)), forth)
     text_rows_w = cross_memory.shape[0]
+    cross_in = jnp.stack([cross_query, blender.T], axis=1)
+    cross_in = halves(cross_in.reshape(rows, 2, 2, head_cols).transpose(0, 2, 1, 3)).reshape(2 * rows, -1)
     memory_in = halves(cross_memory.reshape(text_rows_w, 2, 2, head_cols).transpose(0, 2, 1, 3))
-    memory_w = gather_weight(memory_in.reshape(2 * text_rows_w, 2 * head_cols), back)
-    query_w = gather_weight(halves(cross_query.reshape(rows, 2, head_cols)), forth)
-    blender_w = gather_weight(halves(blender.T.reshape(rows, 2, head_cols)), back)
-    tile = hidden_cols // MLP_CHUNKS
-    mlp_in = jnp.stack(
-        [
-            halves(expander.reshape(rows, 2, hidden_cols)),
-            halves(reducer.T.reshape(rows, 2, hidden_cols)),
-        ],
-        axis=1,
-    ).reshape(2 * rows, 2, MLP_CHUNKS, tile)
-    mlp_orders = [forth if j % 2 == 0 else back for j in range(MLP_CHUNKS)]
-
-    times = time_embedding
-    silu_own = jax.nn.silu(times.astype(F32)).astype(BF16)
-    silu_all = silu_own[None, None]
-    silu_all = jnp.concatenate([silu_all, swap(silu_all, "core", 2, 1)], axis=1)
-    silu_all = jnp.where(core == 0, silu_all, silu_all[:, ::-1])
-    for mask in chip_bits:
-        other = swap(silu_all, "chip", chips, mask)
-        high = (chip_index & mask) > 0
-        silu_all = jnp.concatenate(
-            [jnp.where(high, other, silu_all), jnp.where(high, silu_all, other)], axis=0
-        )
-    silu_all = silu_all.reshape(latent_total, width)
+    memory_in = memory_in.reshape(2 * text_rows_w, 2 * head_cols)
+    mlp_in = jnp.stack([expander, reducer.T], axis=1).reshape(rows, 2, 2, MLP_CHUNKS, tile)
+    mlp_in = halves(mlp_in.transpose(0, 2, 3, 1, 4)).reshape(2 * rows, 2 * hidden_cols)
+    cross_w, memory_w, mlp_w = gather((chips, wide), [cross_in, memory_in, mlp_in], (False,) * 3, 2)
+
     mod_rows = modulator.shape[0]
     device = ((chip_index * 2 + core) * wide + lane) * deep + side
     silu_cols = at(silu_all.reshape(latent_total, devices, mod_rows), device, 1)
-    mod = jnp.dot(silu_cols, modulator, preferred_element_type=F32).reshape(chips, wide, width)
-    for axis, extent, mask in [("chip", chips, b) for b in chip_bits[::-1]]:
-        high = (chip_index & mask) > 0
-        low_part, high_part = jnp.split(mod, 2, axis=0)
-        mod = jnp.where(high, high_part, low_part) + swap(
-            jnp.where(high, low_part, high_part), axis, extent, mask
-        )
-    for axis, extent, mask in [("ta", wide, b) for b in bits_of(wide)[::-1]]:
-        high = (lane & mask) > 0
-        low_part, high_part = jnp.split(mod, 2, axis=1)
-        mod = jnp.where(high, high_part, low_part) + swap(
-            jnp.where(high, low_part, high_part), axis, extent, mask
-        )
-    mod = mod.reshape(1, width)
-    for axis, extent, mask in [("tb", deep, b) for b in deep_bits] + [("core", 2, 1)]:
-        mod = mod + swap(mod, axis, extent, mask)
+    silu_mine = lax.dynamic_slice_in_dim(silu_all, chip_index * 2 * local + lane, 1, 0)
+    mod = jnp.dot(silu_mine, modulator_full, preferred_element_type=F32)
 
     def to_latent(value):
         value = value.reshape(local, 2, half_len, width)
@@ -1084,8 +1092,7 @@
 
     latents_flat = jnp.transpose(latents, (1, 0, 2)).reshape(own_len, width)
     skips_flat = jnp.transpose(skips, (1, 0, 2)).reshape(own_len, width)
-    merge_index = (chip_index * 2 + core).astype(jnp.int32).reshape(1)
-    first_local, merger_full = merge(merge_index, latents_flat, skips_flat, merger_list, gains, biases)
+    first_local = merge(latents_flat, skips_flat, merger_full, gains, biases)
     first = to_latent(first_local)
     cot = to_latent(jnp.transpose(cotangent, (1, 0, 2)))
     cot_all = gather_tokens(cot)
@@ -1113,7 +1120,7 @@
     )
     self_bias = own_biases[:, 0:3].reshape(wide, 1, 3 * head_cols)
     self_low, self_pre, self_att, self_lse, part_own, part_other = self_forward(
-        chip, x_self, projector_w, self_bias, combiner_w, per_head_norm_gains, head_shifts, cosine, sine, own_len
+        x_self, self_w, self_bias, per_head_norm_gains, head_shifts, cosine, sine, own_len
     )
     x_cross, second = norm(
         [first, part_own, *scatter_tokens(part_other)], rows_of(biases[7:8], gains[3:4], biases[3:4])
@@ -1128,7 +1135,7 @@
     cross_bias = own_biases[:, 3:4]
     memory_bias = own_biases[:, 4:6].reshape(wide, 1, 2 * head_cols)
     cross_low, cross_pre, memory_low, memory_pre, cross_att, cross_lse, part_own, part_other = cross_forward(
-        chip, x_cross, text, query_w, memory_w, blender_w, cross_bias, memory_bias,
+        x_cross, text, cross_w, memory_w, cross_bias, memory_bias,
         per_head_norm_gains, head_shifts, own_len, text_len,
     )
     x_mlp, third = norm(
@@ -1137,79 +1144,60 @@
     x_mlp = gather_tokens(x_mlp)
 
     own_hidden = at(at(hidden_all, side, 1), core, 1)
-    own_hidden = jnp.stack([at(own_hidden, lane ^ i) for i in range(wide)]).reshape(wide, 1, MLP_CHUNKS, tile)
-    x_t, cot_t = x_mlp.T, cot_all.T
-    outs, backs, hidden_sums, mlp_grads = [third], [], [], []
-    for j in range(MLP_CHUNKS):
-        weights = gather_weight(mlp_in[:, :, j].reshape(2 * rows, 2 * tile), mlp_orders[j])
-        grads, out_own, out_other, back_own, back_other, hidden_sum = mlp(
-            chip, x_mlp, cot_all, x_t, cot_t, weights, own_hidden[:, :, j], own_len
-        )
-        mlp_grads.append(scatter_weight(grads, mlp_orders[j]))
-        outs += [out_own, *scatter_tokens(out_other)]
-        backs += [back_own, *scatter_tokens(back_other)]
-        hidden_sums.append(hidden_sum)
+    own_hidden = jnp.stack([at(own_hidden, lane ^ i) for i in range(wide)]).reshape(wide * MLP_CHUNKS, 1, tile)
+    mlp_g, out_own, out_other, back_own, back_other, hidden_sum = mlp(
+        x_mlp, cot_all, x_mlp.T, cot_all.T, mlp_w, own_hidden, own_len
+    )
+    (mlp_grad,) = scatter((chips, wide), [mlp_g], (False,), 3)
+    outs = [third, out_own, *scatter_tokens(out_other)]
+    backs = [back_own, *scatter_tokens(back_other)]
     block_total = sum(v.astype(F32) for v in outs) + out_bias
     block_out = from_latent(block_total.astype(BF16))
 
     third_low, mlp_sums, third_grad = norm_back(backs, third, cot, gains[4:5])
     blender_g_in = gather_tokens(third_low)
-    query_g, memory_g, blender_g, part_own, part_other, text_part, query_col, memory_col, cross_heads = (
-        cross_backward(
-            chip, x_cross, blender_g_in, text, query_w, memory_w, blender_w, cross_low, cross_pre,
-            memory_low, memory_pre, cross_att, cross_lse, per_head_norm_gains, own_len, text_len,
-        )
-    )
-    blender_grads = unhalves(scatter_weight(blender_g, back)).reshape(rows, tensor_cols).T
-    query_grads = unhalves(scatter_weight(query_g, forth)).reshape(rows, tensor_cols)
-    memory_grads = unhalves(
-        scatter_weight(memory_g, back).reshape(2 * text_rows_w, 2, head_cols)
-    )
+    cross_g, memory_g, part_own, part_other, text_part, query_col, memory_col, cross_heads = cross_backward(
+        x_cross, blender_g_in, text, cross_w, memory_w, cross_low, cross_pre,
+        memory_low, memory_pre, cross_att, cross_lse, per_head_norm_gains, own_len, text_len,
+    )
+    cross_grad, memory_grads = scatter((chips, wide), [cross_g, memory_g], (False, False), 4)
+    cross_grad = unhalves(cross_grad.reshape(2 * rows, 2, head_cols)).transpose(2, 0, 1, 3)
+    query_grads = cross_grad[0].reshape(rows, tensor_cols)
+    blender_grads = cross_grad[1].reshape(rows, tensor_cols).T
+    memory_grads = unhalves(memory_grads.reshape(2 * text_rows_w, 2, head_cols))
     memory_grads = memory_grads.transpose(0, 2, 1, 3).reshape(text_rows_w, 2, tensor_cols)
     second_low, cross_sums, second_grad = norm_back(
         [part_own, *scatter_tokens(part_other)], second, third_grad, gains[3:4]
     )
-    proj_g, comb_g, part_own, part_other, self_col, self_heads = self_backward(
-        chip, x_self, gather_tokens(second_low), projector_w, combiner_w, self_low, self_pre, self_att,
+    self_g, part_own, part_other, self_col, self_heads = self_backward(
+        x_self, gather_tokens(second_low), self_w, self_low, self_pre, self_att,
         self_lse, per_head_norm_gains, cosine, sine, own_len,
     )
     first_low, self_sums = norm_back(
         [part_own, *scatter_tokens(part_other)], first, second_grad, gains[2:3], keep=False
     )
     low_local = from_latent(first_low)
-    projector_grads = unhalves(scatter_weight(proj_g, back).reshape(2 * rows, 3, head_cols))
-    projector_grads = projector_grads.transpose(0, 2, 1, 3).reshape(rows, 3, tensor_cols)
-    combiner_grads = unhalves(scatter_weight(comb_g, forth)).reshape(rows, tensor_cols).T
     left, right, merge_in, merge_sums = merge_back(
         latents_flat, skips_flat, low_local, merger_full, gains, biases
     )
     merger_g = dot(merge_in, low_local, 0, 0).astype(BF16).reshape(chips, 2, -1, width)
-    mine, other = [], []
-    for k in range(chips):
-        block = at(merger_g, chip_index ^ k)
-        mine.append(at(block, core))
-        other.append(at(block, 1 - core))
-    received = [swap(o, "core", 2, 1) for o in other]
-    merger_p = {
-        k: (m.astype(F32) + r.astype(F32)).astype(BF16) for k, (m, r) in enumerate(zip(mine, received))
-    }
-    for mask in forth[::-1]:
-        for k in [k for k in merger_p if k & mask]:
-            received = swap(merger_p.pop(k), "chip", chips, mask)
-            merger_p[k ^ mask] = (merger_p[k ^ mask].astype(F32) + received.astype(F32)).astype(BF16)
-    value = merger_p[0].reshape(wide, deep, -1, width).astype(F32)
-    for axis, dim, extent, index, mask in [("tb", 1, deep, side, b) for b in deep_bits[::-1]] + [
-        ("ta", 0, wide, lane, b) for b in bits_of(wide)[::-1]
-    ]:
-        low_part, high_part = jnp.split(value, 2, axis=dim)
-        high = (index & mask) > 0
+    mine, other = at(merger_g, core, 1), at(merger_g, 1 - core, 1)
+    value = mine.astype(F32) + swap(other, "core", 2, 1).astype(F32)
+    value = value.reshape(chips, wide, deep, -1, width)
+    for mask in deep_bits[::-1]:
+        low_part, high_part = jnp.split(value, 2, axis=2)
+        high = (side & mask) > 0
         sent = jnp.where(high, low_part, high_part).astype(BF16)
-        value = jnp.where(high, high_part, low_part) + swap(sent, axis, extent, mask).astype(F32)
-    merger_grads = value.reshape(merger.shape)
-
-    mlp_grad = jnp.stack([g.reshape(2 * rows, 2, tile) for g in mlp_grads], axis=2)
-    expander_grads = unhalves(mlp_grad[:, 0].reshape(2 * rows, hidden_cols)).reshape(rows, 2 * hidden_cols)
-    reducer_grads = unhalves(mlp_grad[:, 1].reshape(2 * rows, hidden_cols)).reshape(rows, 2 * hidden_cols).T
+        value = jnp.where(high, high_part, low_part) + swap(sent, "tb", deep, mask).astype(F32)
+    merger_g = value.astype(BF16).reshape(chips, wide, -1, width)
+    self_grad, merger_grads = scatter((chips, wide), [self_g, merger_g], (False, True), 5)
+    self_grad = unhalves(self_grad.reshape(2 * rows, 4, head_cols)).transpose(0, 2, 1, 3)
+    projector_grads = self_grad[:, :3].reshape(rows, 3, tensor_cols)
+    combiner_grads = self_grad[:, 3].reshape(rows, tensor_cols).T
+
+    mlp_grad = unhalves(mlp_grad.reshape(2 * rows, MLP_CHUNKS, 2, tile)).transpose(3, 0, 1, 2, 4)
+    expander_grads = mlp_grad[0].reshape(rows, 2 * hidden_cols)
+    reducer_grads = mlp_grad[1].reshape(rows, 2 * hidden_cols).T
 
     text_sum = text_part
     for axis, extent, mask in [("core", 2, 1)] + [("tb", deep, b) for b in deep_bits]:
@@ -1236,14 +1224,14 @@
     modulator_grads = lax.dot_general(
         silu_cols.astype(F32), mod_all, (((0,), (0,)), ((), ())), precision=exact
     )
-    time_part = lax.dot_general(
-        mod_all, modulator.astype(F32), (((1,), (1,)), ((), ())), precision=exact
-    )
-    time_all = gather_all(time_part)
-    time_all = jnp.moveaxis(time_all.reshape(devices, latent_total, mod_rows), 0, 1)
-    time_all = time_all.reshape(chips * 2, local, wide * deep, -1)
-    time_own = at(at(time_all, chip_index * 2 + core), lane * deep + side, 1)
-    times_own = at(times.reshape(local, wide * deep, -1), lane * deep + side, 1).astype(F32)
+    mod_own = lax.dynamic_slice_in_dim(mod_all, (chip_index * 2 + core) * local, local, 0)
+    cols_own = width // (wide * deep)
+    tensor_index = lane * deep + side
+    modulator_own = lax.dynamic_slice_in_dim(modulator_full, tensor_index * cols_own, cols_own, 0)
+    time_own = lax.dot_general(
+        mod_own, modulator_own.astype(F32), (((1,), (1,)), ((), ())), precision=exact
+    )
+    times_own = lax.dynamic_slice_in_dim(times, tensor_index * cols_own, cols_own, 1).astype(F32)
     _, silu_pull = jax.vjp(jax.nn.silu, times_own)
     time_grads = silu_pull(time_own)[0]
 
@@ -1260,7 +1248,7 @@
         ],
         axis=0,
     )
-    hidden_sum = jnp.stack(hidden_sums, axis=2).reshape(wide, 1, hidden_cols)
+    hidden_sum = hidden_sum.reshape(wide, 1, hidden_cols)
     hidden_sum = all_columns(hidden_sum)
     sums = jnp.transpose(sums.reshape(21, devices, part), (1, 0, 2)).reshape(devices, -1)
     both = jnp.concatenate([sums, hidden_sum.reshape(devices, hidden_part)], axis=1)

time: 1670 us -> 1630 us (0.976)
  Pallas kernels: 465 us -> 1270 us
  waiting for transfers between devices: 518 us -> 67.5 us
  local copies, waits for them, and re-layouts: 295 us -> 137 us
  starting transfers between devices: 206 us -> 56.7 us
  other arithmetic: 159 us -> 72 us
    pallas_call x8 -> x11, Pallas kernels: 409 us -> 1220 us  [the longest x3 471 us: scatter(): pl.pallas_call(functools.partial(scatter_kernel, sizes, absolute), in_spe...]
    ppermute x182 -> x57, waiting for transfers between devices: 518 us -> 67.5 us  [swap(): return lax.ppermute(value, axis, [(i, i ^ mask) for i in range(size)])]
    ppermute x182 -> x57, starting transfers between devices: 206 us -> 56.7 us  [swap(): return lax.ppermute(value, axis, [(i, i ^ mask) for i in range(size)])]
    ppermute x30 -> x1, local copies, waits for them, and re-layouts: 68.5 us -> 1.51 us  [swap(): return lax.ppermute(value, axis, [(i, i ^ mask) for i in range(size)])]
    unnamed x303 -> x132, local copies, waits for them, and re-layouts: 38 us -> 10.7 us
    another operation x19 -> x0, other arithmetic: 26.5 us -> none  [the longest x16 23.9 us: gather_weight(): value = jnp.stack([value, other], axis=2)]
    convert_element_type x14 -> x1, other arithmetic: 25.8 us -> 2.98 us  [body(): merger_g = value.astype(BF16).reshape(chips, wide, -1, width)]
    add x20 -> x0, other arithmetic: 20.2 us -> none  [the longest x8 15.6 us: scatter_weight(): near = pieces[k ^ mask].astype(F32) + received]
  transfers between devices with their start and end apart: 182 -> 57, of which waited for: 55 -> 11; matrix products, arithmetic and copies ran while one was open for 27% -> 12% of each run, Pallas kernels for 28% -> 58%
where the time goes in v2:
time: 1630 us
  Pallas kernels  1270 us (78%)
  local copies, waits for them, and re-layouts  137 us (8%)
  other arithmetic  72 us (4%)
  waiting for transfers between devices  67.5 us (4%)
  starting transfers between devices  56.7 us (3%)
    pallas_call x3, Pallas kernels, scatter(): pl.pallas_call(functools.partial(scatter_kernel, sizes, absolute), in_spe...  471 us
    pallas_call x2, Pallas kernels, gather(): pl.pallas_call(functools.partial(gather_kernel, sizes, full), in_specs=[p...  361 us
    pallas_call x1, Pallas kernels, self_backward(): pl.pallas_call(functools.partial(self_backward_kernel, (heads, size, own)...  106 us
    pallas_call x1, Pallas kernels, mlp(): pl.pallas_call(functools.partial(mlp_kernel, own), grid=(groups * MLP_CHU...  89.7 us
    pallas_call x1, Pallas kernels, self_forward(): pl.pallas_call(functools.partial(self_forward_kernel, (heads, size, own))...  81 us
    ppermute x57, waiting for transfers between devices, swap(): return lax.ppermute(value, axis, [(i, i ^ mask) for i in range(size)])  67.5 us
    pallas_call x1, Pallas kernels, cross_backward(): pl.pallas_call(functools.partial(cross_backward_kernel, (heads, size, own...  61.2 us
    ppermute x57, starting transfers between devices, swap(): return lax.ppermute(value, axis, [(i, i ^ mask) for i in range(size)])  56.7 us
  transfers between devices with their start and end apart: 57, of which 11 were waited for; matrix products, arithmetic and copies ran while one was open for 12% of the time, Pallas kernels for 58%

profile of v2, /device:TPU:9, one launch (start us, length us, event | category | flops | bytes accessed | tf_op | source)
XLA Modules:
  0.0 1625.6 jit_solution(6727235645996602756)
XLA Ops:
  21.5 137.4 %gather.2 = (f32[4,2,4,1,3932]{4,3,2,1,0:T(1,128)}, bf16[4,2,4,88,1408]{4,3,2,1,0:T(8,128)(2,1)}, bf16[4,2,4,44,1408]{4,3,2,1,0:T(8,128)(2,1)}, bf16[4,4,352,704]{3,2,1,0:T(8,128)(2,1)}) custom-call(f32[1,3932]{1,0:T(1,128)} %broadcast_in_dim.82.refs_0_, bf16[88,1408]{1,0:T(8,128)(2,1)} %refs_1_.1, bf16[44,1408]{1,0:T(8,128)(2,1)} %refs_2_.1, ...), custom_call_target="tpu_custom_call" | custom-call | tf_op jit(solution)/shard_map/gather/pallas_call | solution.py:204
  164.1 11.7 merge.1
  184.1 6.0 reshape.583
  190.2 2.8 convolution_reduce_fusion
  195.2 3.0 collective-permute-start.3
  198.9 21.5 %collective-permute-done.4 = bf16[128,1408]{1,0:T(8,128)(2,1)S(1)} collective-permute-done((bf16[128,1408]{1,0:T(8,128)(2,1)S(1)}, bf16[128,1408]{1,0:T(8,128)(2,1)S(1)}, u32[]{:S(2)}, u32[]{:S(2)}) %collective-permute-start.4) | collective-permute-done | bytes 360480 | tf_op jit(solution)/shard_map/ppermute | solution.py:26
  220.3 5.8 collective-permute-done.3
  227.8 4.1 norm.3
  235.2 4.8 sine_multiply_fusion
  241.0 3.2 pad_maximum_fusion.x_ref
  244.1 81.0 %self_forward.1 = (bf16[4,1024,528]{2,1,0:T(8,128)(2,1)}, bf16[4,1024,352]{2,1,0:T(8,128)(2,1)}, bf16[4,1024,176]{2,1,0:T(8,128)(2,1)}, f32[4,2,1024]{2,1,0:T(2,...) custom-call(bf16[1024,1408]{1,0:T(8,128)(2,1)} %pad_maximum_fusion.x_ref, ...), custom_call_target="tpu_custom_call" | custom-call | tf_op jit(solution)/shard_map/self_forward/pallas_call | solution.py:374
  344.7 5.2 norm.4
  361.9 223.8 %gather.3 = (bf16[4,4,352,352]{3,2,1,0:T(8,128)(2,1)}, bf16[4,4,256,352]{3,2,1,0:T(8,128)(2,1)}, bf16[4,4,352,1536]{3,2,1,0:T(8,128)(2,1)}) custom-call(bf16[352,352]{1,0:T(8,128)(2,1)} %select_n.509.refs_0_, bf16[256,352]{1,0:T(8,128)(2,1)} %reshape.612.refs_1_, bf16[352,1536]{1,0:T(8,128)(2,1)} %select_n.515.refs_2_), custom_call_target="tpu_custom_call" | custom-call | tf_op jit(solution)/shard_map/gather/pallas_call | solution.py:204
  589.9 3.3 collective-permute-start.16
  597.0 39.4 %cross_forward.1 = (bf16[4,1024,176]{2,1,0:T(8,128)(2,1)}, bf16[4,1024,176]{2,1,0:T(8,128)(2,1)}, bf16[4,336,352]{2,1,0:T(8,128)(2,1)}, bf16[4,336,176]{2,1,0:T(...) custom-call(bf16[1024,1408]{1,0:T(8,128)(2,1)} %constant_dynamic-upd, ...), custom_call_target="tpu_custom_call" | custom-call | tf_op jit(solution)/shard_map/cross_forward/pallas_call | solution.py:590
  636.4 3.3 collective-permute-start.12
  643.6 5.8 norm.5
  653.2 4.7 fusion.50
  657.9 4.7 copy.241.cot_t
  662.6 4.8 fusion.51
  667.3 4.6 copy.240.x_ref
  671.9 89.7 %mlp.1 = (bf16[4,4,352,1536]{3,2,1,0:T(8,128)(2,1)}, f32[512,1408]{1,0:T(8,128)}, bf16[512,1408]{1,0:T(8,128)(2,1)}, f32[512,1408]{1,0:T(8,128)}, bf16[512,1408]{1,0:T(8,128)(2,1)}, /*index=5*/f32[12,1,256]{2,1,0:T(1,128)}) custom-call(bf16[1024,1408]{1,0:T(8,128)(2,1)} %copy.240.x_ref, bf16[1024,1408]{1,0:T(8,128)(2,1)} %get-tuple-element.243.cot_ref, ...), custom_call_target="tpu_custom_call" | custom-call | tf_op jit(solution)/shard_map/mlp/pallas_call | solution.py:754
  762.2 3.1 collective-permute-done.24.refs_1_
  765.2 7.1 norm_back.3
  776.1 4.8 add_convert_fusion
  782.6 61.2 %cross_backward.1 = (bf16[4,4,352,352]{3,2,1,0:T(8,128)(2,1)}, bf16[4,4,256,352]{3,2,1,0:T(8,128)(2,1)}, f32[512,1408]{1,0:T(8,128)}, bf16[512,1408]{1,0:T(8,128...) custom-call(bf16[1024,1408]{1,0:T(8,128)(2,1)} %constant_dynamic-update-slice_fusio, ...), custom_call_target="tpu_custom_call" | custom-call | tf_op jit(solution)/shard_map/cross_backward/pallas_call | solution.py:685
  850.7 220.1 %scatter.5 = f32[352,1536]{1,0:T(8,128)} custom-call(bf16[4,4,352,1536]{3,2,1,0:T(8,128)(2,1)} %get-tuple-element.138.refs_0_), custom_call_target="tpu_custom_call" | custom-call | tf_op jit(solution)/shard_map/scatter/pallas_call | solution.py:290
  1070.8 2.6 reshape_reshape.21
  1080.6 7.6 norm_back.4
  1100.9 94.0 %scatter.4 = (f32[352,352]{1,0:T(8,128)}, f32[256,352]{1,0:T(8,128)}) custom-call(bf16[4,4,352,352]{3,2,1,0:T(8,128)(2,1)} %get-tuple-element.134.refs_0_, bf16[4,4,256,352]{3,2,1,0:T(8,128)(2,1)} %get-tuple-element.135.refs_1_), custom_call_target="tpu_custom_call" | custom-call | tf_op jit(solution)/shard_map/scatter/pallas_call | solution.py:290
  1200.9 3.8 copy.242
  1206.6 3.2 pad_maximum_fusion.4.grad_ref
  1209.7 105.8 %self_backward.1 = (bf16[4,4,352,704]{3,2,1,0:T(8,128)(2,1)}, f32[512,1408]{1,0:T(8,128)}, bf16[512,1408]{1,0:T(8,128)(2,1)}, f32[4,1,528]{2,1,0:T(1,128)}, f32[4,88]{1,0:T(4,128)}) custom-call(bf16[1024,1408]{1,0:T(8,128)(2,1)} %pad_maximum_fusion.x_ref, bf16[1024,1408]{1,0:T(8,128)(2,1)} %pad_maximum_fusion.4.grad_ref, ...), custom_call_target="tpu_custom_call" | custom-call | tf_op jit(solution)/shard_map/self_backward/pallas_call | solution.py:489
  1325.0 3.9 collective-permute-done.36
  1328.9 5.9 collective-permute-done.35
  1339.5 6.4 norm_back.5
  1362.0 20.8 %collective-permute-done.31 = bf16[128,1408]{1,0:T(8,128)(2,1)S(1)} collective-permute-done((bf16[128,1408]{1,0:T(8,128)(2,1)S(1)}, bf16[128,1408]{1,0:T(8,128)(2,1)S(1)}, u32[]{:S(2)}, u32[]{:S(2)}) %collective-permute-start.31) | collective-permute-done | bytes 360480 | tf_op jit(solution)/shard_map/ppermute | solution.py:26
  1382.8 5.2 collective-permute-done.30
  1388.7 2.6 collective-permute-start.32
  1394.6 16.9 %merge_back.1 = (f32[512,1408]{1,0:T(8,128)}, f32[512,1408]{1,0:T(8,128)}, bf16[512,2816]{1,0:T(8,128)(2,1)}, f32[5,1408]{1,0:T(8,128)}) custom-call(bf16[512,1408]{1,0:T(8,128)(2,1)} %bitcast.250, bf16[512,1408]{1,0:T(8,128)(2,1)} %bitcast.252, bf16[512,1408]{1,0:T(8,128)(2,1)} %bitcast.261, bf16[2816,1408]{1,0:T(8,128)(2,1)} %bitcast.244, ...), custom_call_target="tpu_custom_call" | custom-call | tf_op jit(solution)/shard_map/merge_back/pallas_call | solution.py:844
  1414.9 8.8 convolution_convert_fusion
  1428.6 3.2 collective-permute-start.45
  1435.0 2.7 fusion.41
  1439.7 8.9 copy_bitcast_fusion
  1448.7 3.0 fusion
  1451.7 157.3 %scatter.3 = (f32[352,704]{1,0:T(8,128)}, f32[88,1408]{1,0:T(8,128)}) custom-call(bf16[4,4,352,704]{3,2,1,0:T(8,128)(2,1)} %get-tuple-element.123.refs_0_, bf16[4,4,88,1408]{3,2,1,0:T(8,128)(2,1)} %bitcast.248), custom_call_target="tpu_custom_call" | custom-call | tf_op jit(solution)/shard_map/scatter/pallas_call | solution.py:290
  1609.0 2.7 reshape_reshape.8
  1619.9 3.2 reshape.602
  (481 shorter events, 187.4 us)
Async XLA Ops:
  2.4 338.8 %collective-permute-start.10 = (bf16[128,2,176]{0,2,1:T(8,128)(2,1)}, bf16[128,2,176]{0,2,1:T(8,128)(2,1)}, u32[]{:S(2)}, u32[]{:S(2)}) collective-permute-start(bf16[128,2,176]{0,2,1:T(8,128)(2,1)} %get-tuple-element.315), channel_id=1, source_target_pairs={{0,4},{4,0},{1,5},{5,1},{2,6},{6,2},{3,7},{7,3},{8,12},{12,8},{9,1... | collective-permute-start | bytes 270344 | tf_op jit(solution)/shard_map/ppermute | solution.py:26
  8.6 9.6 collective-permute-start
  178.1 14.9 collective-permute-start.1
  194.8 25.5 %collective-permute-start.4 = (bf16[128,1408]{1,0:T(8,128)(2,1)S(1)}, bf16[128,1408]{1,0:T(8,128)(2,1)S(1)}, u32[]{:S(2)}, u32[]{:S(2)}) collective-permute-start(bf16[128,1408]{1,0:T(8,128)(2,1)S(1)} %get-tuple-element.289), channel_id=1, source_target_pairs={{0,3},{1,2},{2,1},{3,0},{4,7},{5,6},{6,5},{7,4},{8,11},{9,10},{10,... | collective-permute-start | bytes 1081352 | tf_op jit(solution)/shard_map/ppermute | solution.py:26
  195.2 30.9 %collective-permute-start.3 = (bf16[128,1408]{1,0:T(8,128)(2,1)S(1)}, bf16[128,1408]{1,0:T(8,128)(2,1)S(1)}, u32[]{:S(2)}, u32[]{:S(2)}) collective-permute-start(bf16[128,1408]{1,0:T(8,128)(2,1)S(1)} %get-tuple-element.290), channel_id=1, source_target_pairs={{0,2},{1,3},{2,0},{3,1},{4,6},{5,7},{6,4},{7,5},{8,10},{9,11},{10,... | collective-permute-start | bytes 1081352 | tf_op jit(solution)/shard_map/ppermute | solution.py:26
  198.2 28.0 %collective-permute-start.2 = (bf16[128,1408]{1,0:T(8,128)(2,1)S(1)}, bf16[128,1408]{1,0:T(8,128)(2,1)S(1)}, u32[]{:S(2)}, u32[]{:S(2)}) collective-permute-start(bf16[128,1408]{1,0:T(8,128)(2,1)S(1)} %get-tuple-element.291), channel_id=1, source_target_pairs={{0,1},{1,0},{2,3},{3,2},{4,5},{5,4},{6,7},{7,6},{8,9},{9,8},{10,11... | collective-permute-start | bytes 1081352 | tf_op jit(solution)/shard_map/ppermute | solution.py:26
  231.9 9.0 collective-permute-start.5
  325.1 19.6 %collective-permute-start.6 = (bf16[512,1408]{1,0:T(8,128)(2,1)}, bf16[512,1408]{1,0:T(8,128)(2,1)}, u32[]{:S(2)}, u32[]{:S(2)}) collective-permute-start(bf16[512,1408]{1,0:T(8,128)(2,1)} %get-tuple-element.86), channel_id=1, source_target_pairs={{0,4},{4,0},{1,5},{5,1},{2,6},{6,2},{3,7},{7,3},{8,12},{12,8},{9,1... | collective-permute-start | bytes 4325384 | tf_op jit(solution)/shard_map/ppermute | solution.py:26
  326.7 23.4 %collective-permute-start.9 = (bf16[176,2,176]{2,1,0:T(2,128)(2,1)S(1)}, bf16[176,2,176]{2,1,0:T(2,128)(2,1)}, u32[]{:S(2)}, u32[]{:S(2)}) collective-permute-start(bf16[176,2,176]{2,1,0:T(2,128)(2,1)S(1)} %bitcast.303), channel_id=1, source_target_pairs={{0,4},{4,0},{1,5},{5,1},{2,6},{6,2},{3,7},{7,3},{8,12},{12,8},{9,1... | collective-permute-start | bytes 371720 | tf_op jit(solution)/shard_map/ppermute | solution.py:26
  333.8 21.8 %collective-permute-start.11 = (bf16[176,3,2,256]{3,0,2,1:T(8,128)(2,1)}, bf16[176,3,2,256]{3,0,2,1:T(8,128)(2,1)}, u32[]{:S(2)}, u32[]{:S(2)}) collective-permute-start(bf16[176,3,2,256]{3,0,2,1:T(8,128)(2,1)} %copy.232), channel_id=1, source_target_pairs={{0,4},{4,0},{1,5},{5,1},{2,6},{6,2},{3,7},{7,3},{8,12},{12,8},{9,1... | collective-permute-start | bytes 1622024 | tf_op jit(solution)/shard_map/ppermute | solution.py:26
  337.5 248.3 %collective-permute-start.8 = (bf16[333,1024]{1,0:T(8,128)(2,1)}, bf16[333,1024]{1,0:T(8,128)(2,1)}, u32[]{:S(2)}, u32[]{:S(2)}) collective-permute-start(bf16[333,1024]{1,0:T(8,128)(2,1)} %bitcast.231), channel_id=1, source_target_pairs={{0,4},{4,0},{1,5},{5,1},{2,6},{6,2},{3,7},{7,3},{8,12},{12,8},{9,1... | collective-permute-start | bytes 2045960 | tf_op jit(solution)/shard_map/ppermute | solution.py:26
  341.2 246.9 %collective-permute-start.14 = (bf16[2,128,1408]{2,1,0:T(8,128)(2,1)}, bf16[2,128,1408]{2,1,0:T(8,128)(2,1)}, u32[]{:S(2)}, u32[]{:S(2)}) collective-permute-start(bf16[2,128,1408]{2,1,0:T(8,128)(2,1)} %bitcast.228), channel_id=1, source_target_pairs={{0,4},{4,0},{1,5},{5,1},{2,6},{6,2},{3,7},{7,3},{8,12},{12,8},{9,1... | collective-permute-start | bytes 2162696 | tf_op jit(solution)/shard_map/ppermute | solution.py:26
  349.9 244.5 %collective-permute-start.7 = (bf16[512,1408]{1,0:T(8,128)(2,1)}, bf16[512,1408]{1,0:T(8,128)(2,1)}, u32[]{:S(2)}, u32[]{:S(2)}) collective-permute-start(bf16[512,1408]{1,0:T(8,128)(2,1)} %get-tuple-element.88), channel_id=1, source_target_pairs={{0,4},{4,0},{1,5},{5,1},{2,6},{6,2},{3,7},{7,3},{8,12},{12,8},{9,1... | collective-permute-start | bytes 4325384 | tf_op jit(solution)/shard_map/ppermute | solution.py:26
  589.8 49.9 %collective-permute-start.17 = (bf16[128,1408]{1,0:T(8,128)(2,1)S(1)}, bf16[128,1408]{1,0:T(8,128)(2,1)}, u32[]{:S(2)}, u32[]{:S(2)}) collective-permute-start(bf16[128,1408]{1,0:T(8,128)(2,1)S(1)} %get-tuple-element.277), channel_id=1, source_target_pairs={{0,3},{1,2},{2,1},{3,0},{4,7},{5,6},{6,5},{7,4},{8,11},{9,10},{10,... | collective-permute-start | bytes 1081352 | tf_op jit(solution)/shard_map/ppermute | solution.py:26
  589.9 49.8 %collective-permute-start.16 = (bf16[128,1408]{1,0:T(8,128)(2,1)S(1)}, bf16[128,1408]{1,0:T(8,128)(2,1)}, u32[]{:S(2)}, u32[]{:S(2)}) collective-permute-start(bf16[128,1408]{1,0:T(8,128)(2,1)S(1)} %get-tuple-element.278), channel_id=1, source_target_pairs={{0,2},{1,3},{2,0},{3,1},{4,6},{5,7},{6,4},{7,5},{8,10},{9,11},{10,... | collective-permute-start | bytes 1081352 | tf_op jit(solution)/shard_map/ppermute | solution.py:26
  593.2 46.5 %collective-permute-start.15 = (bf16[128,1408]{1,0:T(8,128)(2,1)S(1)}, bf16[128,1408]{1,0:T(8,128)(2,1)}, u32[]{:S(2)}, u32[]{:S(2)}) collective-permute-start(bf16[128,1408]{1,0:T(8,128)(2,1)S(1)} %get-tuple-element.279), channel_id=1, source_target_pairs={{0,1},{1,0},{2,3},{3,2},{4,5},{5,4},{6,7},{7,6},{8,9},{9,8},{10,11... | collective-permute-start | bytes 1081352 | tf_op jit(solution)/shard_map/ppermute | solution.py:26
  636.4 7.2 collective-permute-start.12
  642.6 10.6 collective-permute-start.18
  651.0 11.5 collective-permute-start.13
  761.7 14.3 collective-permute-start.19
  772.4 8.5 collective-permute-start.25
  843.8 236.8 %collective-permute-start.26 = (bf16[512,1408]{1,0:T(8,128)(2,1)}, bf16[512,1408]{1,0:T(8,128)(2,1)}, u32[]{:S(2)}, u32[]{:S(2)}) collective-permute-start(bf16[512,1408]{1,0:T(8,128)(2,1)} %get-tuple-element.108), channel_id=1, source_target_pairs={{0,4},{4,0},{1,5},{5,1},{2,6},{6,2},{3,7},{7,3},{8,12},{12,8},{9,1... | collective-permute-start | bytes 4325384 | tf_op jit(solution)/shard_map/ppermute | solution.py:26
  846.7 231.0 %collective-permute-start.22 = (bf16[128,1408]{1,0:T(8,128)(2,1)}, bf16[128,1408]{1,0:T(8,128)(2,1)}, u32[]{:S(2)}, u32[]{:S(2)}) collective-permute-start(bf16[128,1408]{1,0:T(8,128)(2,1)} %get-tuple-element.269), channel_id=1, source_target_pairs={{0,3},{1,2},{2,1},{3,0},{4,7},{5,6},{6,5},{7,4},{8,11},{9,10},{10,... | collective-permute-start | bytes 1081352 | tf_op jit(solution)/shard_map/ppermute | solution.py:26
  847.9 229.8 %collective-permute-start.21 = (bf16[128,1408]{1,0:T(8,128)(2,1)}, bf16[128,1408]{1,0:T(8,128)(2,1)}, u32[]{:S(2)}, u32[]{:S(2)}) collective-permute-start(bf16[128,1408]{1,0:T(8,128)(2,1)} %get-tuple-element.270), channel_id=1, source_target_pairs={{0,2},{1,3},{2,0},{3,1},{4,6},{5,7},{6,4},{7,5},{8,10},{9,11},{10,... | collective-permute-start | bytes 1081352 | tf_op jit(solution)/shard_map/ppermute | solution.py:26
  849.4 228.3 %collective-permute-start.20 = (bf16[128,1408]{1,0:T(8,128)(2,1)}, bf16[128,1408]{1,0:T(8,128)(2,1)}, u32[]{:S(2)}, u32[]{:S(2)}) collective-permute-start(bf16[128,1408]{1,0:T(8,128)(2,1)} %get-tuple-element.271), channel_id=1, source_target_pairs={{0,1},{1,0},{2,3},{3,2},{4,5},{5,4},{6,7},{7,6},{8,9},{9,8},{10,11... | collective-permute-start | bytes 1081352 | tf_op jit(solution)/shard_map/ppermute | solution.py:26
  1075.4 15.9 collective-permute-start.51
  1088.2 118.4 %collective-permute-start.27 = (bf16[512,1408]{1,0:T(8,128)(2,1)}, bf16[512,1408]{1,0:T(8,128)(2,1)}, u32[]{:S(2)}, u32[]{:S(2)}) collective-permute-start(bf16[512,1408]{1,0:T(8,128)(2,1)} %get-tuple-element.110), channel_id=1, source_target_pairs={{0,4},{4,0},{1,5},{5,1},{2,6},{6,2},{3,7},{7,3},{8,12},{12,8},{9,1... | collective-permute-start | bytes 4325384 | tf_op jit(solution)/shard_map/ppermute | solution.py:26
  1090.8 108.4 %collective-permute-start.23 = (bf16[2,128,1408]{2,1,0:T(8,128)(2,1)}, bf16[2,128,1408]{2,1,0:T(8,128)(2,1)}, u32[]{:S(2)}, u32[]{:S(2)}) collective-permute-start(bf16[2,128,1408]{2,1,0:T(8,128)(2,1)} %get-tuple-element.263), channel_id=1, source_target_pairs={{0,4},{4,0},{1,5},{5,1},{2,6},{6,2},{3,7},{7,3},{8,12},{12,8},{9,1... | collective-permute-start | bytes 2162696 | tf_op jit(solution)/shard_map/ppermute | solution.py:26
  1100.9 215.1 %collective-permute-start.33 = (bf16[336,1024]{1,0:T(8,128)(2,1)}, bf16[336,1024]{1,0:T(8,128)(2,1)}, u32[]{:S(2)}, u32[]{:S(2)}) collective-permute-start(bf16[336,1024]{1,0:T(8,128)(2,1)} %convert_element_type.108), channel_id=1, source_target_pairs={{0,4},{4,0},{1,5},{5,1},{2,6},{6,2},{3,7},{7,3},{8,12},{12,8},{9,1... | collective-permute-start | bytes 2064392 | tf_op jit(solution)/shard_map/ppermute | solution.py:26
  1197.6 7.2 collective-permute-start.50
  1199.2 6.5 collective-permute-start.49
  1315.5 23.9 %collective-permute-start.28 = (bf16[512,1408]{1,0:T(8,128)(2,1)}, bf16[512,1408]{1,0:T(8,128)(2,1)}, u32[]{:S(2)}, u32[]{:S(2)}) collective-permute-start(bf16[512,1408]{1,0:T(8,128)(2,1)} %get-tuple-element.116), channel_id=1, source_target_pairs={{0,4},{4,0},{1,5},{5,1},{2,6},{6,2},{3,7},{7,3},{8,12},{12,8},{9,1... | collective-permute-start | bytes 4325384 | tf_op jit(solution)/shard_map/ppermute | solution.py:26
  1319.6 9.3 collective-permute-start.36
  1320.8 8.1 collective-permute-start.34
  1320.8 14.0 collective-permute-start.35
  1337.2 10.3 collective-permute-start.53
  1353.5 38.1 %collective-permute-start.56 = (f32[7,88]{1,0:T(8,128)S(1)}, f32[7,88]{1,0:T(8,128)S(1)}, u32[]{:S(2)}, u32[]{:S(2)}) collective-permute-start(f32[7,88]{1,0:T(8,128)S(1)} %add.427), channel_id=1, source_target_pairs={{0,16},{8,24},{16,0},{24,8},{1,17},{9,25},{17,1},{25,9},{2,18},{10... | collective-permute-start | bytes 7400 | tf_op jit(solution)/shard_map/ppermute | solution.py:26
  1356.0 5.1 collective-permute-start.40
  1358.1 24.8 %collective-permute-start.31 = (bf16[128,1408]{1,0:T(8,128)(2,1)S(1)}, bf16[128,1408]{1,0:T(8,128)(2,1)S(1)}, u32[]{:S(2)}, u32[]{:S(2)}) collective-permute-start(bf16[128,1408]{1,0:T(8,128)(2,1)S(1)} %get-tuple-element.259), channel_id=1, source_target_pairs={{0,3},{1,2},{2,1},{3,0},{4,7},{5,6},{6,5},{7,4},{8,11},{9,10},{10,... | collective-permute-start | bytes 1081352 | tf_op jit(solution)/shard_map/ppermute | solution.py:26
  1358.8 29.2 %collective-permute-start.30 = (bf16[128,1408]{1,0:T(8,128)(2,1)S(1)}, bf16[128,1408]{1,0:T(8,128)(2,1)S(1)}, u32[]{:S(2)}, u32[]{:S(2)}) collective-permute-start(bf16[128,1408]{1,0:T(8,128)(2,1)S(1)} %get-tuple-element.260), channel_id=1, source_target_pairs={{0,2},{1,3},{2,0},{3,1},{4,6},{5,7},{6,4},{7,5},{8,10},{9,11},{10,... | collective-permute-start | bytes 1081352 | tf_op jit(solution)/shard_map/ppermute | solution.py:26
  1360.7 27.3 %collective-permute-start.29 = (bf16[128,1408]{1,0:T(8,128)(2,1)S(1)}, bf16[128,1408]{1,0:T(8,128)(2,1)S(1)}, u32[]{:S(2)}, u32[]{:S(2)}) collective-permute-start(bf16[128,1408]{1,0:T(8,128)(2,1)S(1)} %get-tuple-element.261), channel_id=1, source_target_pairs={{0,1},{1,0},{2,3},{3,2},{4,5},{5,4},{6,7},{7,6},{8,9},{9,8},{10,11... | collective-permute-start | bytes 1081352 | tf_op jit(solution)/shard_map/ppermute | solution.py:26
  1361.2 31.7 %collective-permute-start.41 = (f32[2,4,1408]{2,1,0:T(4,128)S(1)}, f32[2,4,1408]{2,1,0:T(4,128)S(1)}, u32[]{:S(2)}, u32[]{:S(2)}) collective-permute-start(f32[2,4,1408]{2,1,0:T(4,128)S(1)} %pad_maximum_fusion.17), channel_id=1, source_target_pairs={{0,16},{8,24},{16,0},{24,8},{1,17},{9,25},{17,1},{25,9},{2,18},{10... | collective-permute-start | bytes 135176 | tf_op jit(solution)/shard_map/ppermute | solution.py:26
  1414.3 9.5 collective-permute-start.43
  1423.9 4.5 collective-permute-start.44
  1427.5 21.2 %collective-permute-start.42 = (bf16[4,352,1408]{2,1,0:T(8,128)(2,1)S(1)}, bf16[4,352,1408]{2,1,0:T(8,128)(2,1)S(1)}, u32[]{:S(2)}, u32[]{:S(2)}) collective-permute-start(bf16[4,352,1408]{2,1,0:T(8,128)(2,1)S(1)} %dynamic-slice_bitcast_fusion), channel_id=1, source_target_pairs={{0,4},{4,0},{1,5},{5,1},{2,6},{6,2},{3,7},{7,3},{8,12},{12,8},{9,1... | collective-permute-start | bytes 11894792 | tf_op jit(solution)/shard_map/ppermute | solution.py:26
  1432.9 4.8 collective-permute-start.46
  1437.7 10.9 collective-permute-start.47
  1612.1 4.7 collective-permute-start.48
  (59 other events, 907.3 us)

commit v3 on v2

--- a/solution.py
+++ b/solution.py
@@ -14,6 +14,7 @@
 BF16 = jnp.bfloat16
 VMEM_LIMIT = 62 * 1024 * 1024
 MLP_CHUNKS = 3
+PACES = (0.7, 0.4, 0.8, 0.8)
 QUERY_BLOCK = 512
 MESH = pl.DeviceIdType.MESH
 
@@ -112,206 +113,342 @@
     pl.semaphore_wait(barrier, len(partners))
 
 
-def gather_kernel(sizes, full, *refs):
-    chips, wide = sizes
-    n = len(full)
-    shards, outs = refs[:n], refs[n : 2 * n]
-    local_sem, z_send, z_recv, x_send, x_recv, c_send, c_recv = refs[2 * n :]
-    chip, core, lane = (lax.axis_index(name) for name in ("chip", "core", "ta"))
-    greet(chips, wide, any(full))
-    sends, arrived = [], set()
-
-    def place(w, k, i):
-        if full[w]:
-            return outs[w].at[flip(chip, k), core, flip(lane, i)]
-        return outs[w].at[flip(chip, k), i]
-
-    def send(source, target, device, send_sem, recv_sem):
-        copy = pltpu.make_async_remote_copy(
-            src_ref=source, dst_ref=target, send_sem=send_sem, recv_sem=recv_sem,
-            device_id=device, device_id_type=MESH,
-        )
+def remote(source, target, device, send_sem, recv_sem, sent):
+    copy = pltpu.make_async_remote_copy(
+        src_ref=source, dst_ref=target, send_sem=send_sem, recv_sem=recv_sem,
+        device_id=device, device_id_type=MESH,
+    )
+    if sent:
+        copy.wait_send()
+    else:
         copy.start()
-        sends.append(copy)
-
-    def take(w, k, i):
-        if k == 0 and i == 0 or (w, k, i) in arrived:
-            return
-        arrived.add((w, k, i))
-        piece = place(w, k, i)
-        sem = z_recv.at[w, i - 1] if k == 0 else x_recv.at[w, i, k - 1]
-        pltpu.make_async_copy(piece, piece, sem).wait()
-
-    def near(w, i):
-        take(w, 0, i)
-        source = shards[w] if i == 0 else place(w, 0, i)
-        for bit in bits_of(chips):
-            send(source, place(w, 0, i), {"chip": flip(chip, bit)},
-                 x_send.at[w, i, bit - 1], x_recv.at[w, i, bit - 1])
-
-    def far(w, i):
-        for k in by_distance(chips):
-            bit = link_of(k, i)
-            held = k ^ bit
-            if held:
-                take(w, held, i)
-                piece = place(w, held, i)
-                send(piece, piece, {"chip": flip(chip, bit)}, x_send.at[w, i, k - 1], x_recv.at[w, i, k - 1])
-
-    locals_ = []
-    for w in range(n):
-        copy = pltpu.make_async_copy(shards[w], place(w, 0, 0), local_sem.at[w])
-        copy.start()
-        locals_.append(copy)
-        for i in range(1, wide):
-            target = outs[w].at[chip, core, lane] if full[w] else outs[w].at[chip, i]
-            send(shards[w], target, {"ta": flip(lane, i)}, z_send.at[w, i - 1], z_recv.at[w, i - 1])
-    order = [(w, 0) for w in range(n)] + [(w, i) for w in range(n) for i in range(1, wide)]
-    for t, (w, i) in enumerate(order):
-        near(w, i)
-        if t >= 2:
-            far(*order[t - 2])
-    for w, i in order[-2:]:
-        far(w, i)
-    for copy in locals_:
-        copy.wait()
-    for w in range(n):
-        if full[w]:
-            for k in range(chips):
-                for i in range(wide):
-                    take(w, k, i)
-                send(outs[w].at[flip(chip, k), core], outs[w].at[flip(chip, k), core], {"core": 1 - core},
-                     c_send.at[w, k], c_recv.at[w, k])
-    for w in range(n):
-        for i in range(wide):
-            for k in range(chips):
-                take(w, k, i)
-        if full[w]:
-            for k in range(chips):
-                piece = outs[w].at[flip(chip, k), 1 - core]
-                pltpu.make_async_copy(piece, piece, c_recv.at[w, k]).wait()
-    for copy in sends:
-        copy.wait_send()
-
-
-def gather(sizes, shards, full, number):
-    chips, wide = sizes
-    n = len(shards)
-    shapes = [
-        ((chips, 2, wide) if f else (chips, wide)) + tuple(s.shape) for s, f in zip(shards, full)
-    ]
-    dma = pltpu.SemaphoreType.DMA
-    return pl.pallas_call(
-        functools.partial(gather_kernel, sizes, full),
-        in_specs=[pl.BlockSpec(memory_space=pltpu.VMEM)] * n,
-        out_specs=[pl.BlockSpec(memory_space=pl.ANY)] * n,
-        out_shape=[shape_of(shape, s.dtype) for shape, s in zip(shapes, shards)],
-        scratch_shapes=[
+
+
+def await_bytes(ref, sem):
+    pltpu.make_async_copy(ref, ref, sem).wait()
+
+
+def here():
+    return tuple(lax.axis_index(name) for name in ("chip", "core", "ta"))
+
+
+class Gather:
+    def __init__(self, sizes, shards, full, number, pace=1.0):
+        chips, wide = sizes
+        n = len(shards)
+        dma = pltpu.SemaphoreType.DMA
+        self.sizes, self.full, self.number, self.pace = sizes, full, number, pace
+        self.args = list(shards)
+        self.in_specs = [pl.BlockSpec(memory_space=pltpu.VMEM)] * n
+        self.out_specs = [pl.BlockSpec(memory_space=pl.ANY)] * n
+        self.out_shape = [
+            shape_of(((chips, 2, wide) if f else (chips, wide)) + tuple(v.shape), v.dtype)
+            for v, f in zip(shards, full)
+        ]
+        self.scratch = [
             dma((n,)), dma((n, wide - 1)), dma((n, wide - 1)), dma((n, wide, chips - 1)),
             dma((n, wide, chips - 1)), dma((n, chips)), dma((n, chips)),
-        ],
+        ]
+
+    def plan(self, shards, outs, scratch):
+        chips, wide = self.sizes
+        full, n = self.full, len(shards)
+        local_sem, z_send, z_recv, x_send, x_recv, c_send, c_recv = scratch
+        steps, ends, placed, arrived = [], [], [], set()
+
+        def place(w, k, i):
+            chip, core, lane = here()
+            if full[w]:
+                return outs[w].at[flip(chip, k), core, flip(lane, i)]
+            return outs[w].at[flip(chip, k), i]
+
+        def take(w, k, i):
+            if k == 0 and i == 0 or (w, k, i) in arrived:
+                return
+            arrived.add((w, k, i))
+            sem = z_recv.at[w, i - 1] if k == 0 else x_recv.at[w, i, k - 1]
+            steps.append(lambda: await_bytes(place(w, k, i), sem))
+
+        def pass_on(w, k, i, bit, source, sent=False):
+            chip = here()[0]
+            target = place(w, k ^ bit, i)
+            remote(source() if source else target, target, {"chip": flip(chip, bit)},
+                   x_send.at[w, i, k - 1], x_recv.at[w, i, k - 1], sent)
+
+        def near(w, i):
+            take(w, 0, i)
+            for bit in bits_of(chips):
+                source = (lambda: shards[w]) if i == 0 else None
+                steps.append(lambda bit=bit: pass_on(w, bit, i, bit, source))
+                ends.append(lambda bit=bit: pass_on(w, bit, i, bit, source, True))
+
+        def far(w, i):
+            for k in by_distance(chips):
+                bit = link_of(k, i)
+                if k ^ bit:
+                    take(w, k ^ bit, i)
+                    steps.append(lambda k=k, bit=bit: pass_on(w, k, i, bit, None))
+                    ends.append(lambda k=k, bit=bit: pass_on(w, k, i, bit, None, True))
+
+        def along(w, i, sent=False):
+            chip, core, lane = here()
+            target = outs[w].at[chip, core, lane] if full[w] else outs[w].at[chip, i]
+            remote(shards[w], target, {"ta": flip(lane, i)}, z_send.at[w, i - 1], z_recv.at[w, i - 1], sent)
+
+        def over(w, k, sent=False):
+            chip, core, _ = here()
+            piece = outs[w].at[flip(chip, k), core]
+            remote(piece, piece, {"core": 1 - core}, c_send.at[w, k], c_recv.at[w, k], sent)
+
+        def got(w, k):
+            chip, core, _ = here()
+            await_bytes(outs[w].at[flip(chip, k), 1 - core], c_recv.at[w, k])
+
+        steps.append(lambda: greet(chips, wide, any(full)))
+        for w in range(n):
+            steps.append(lambda w=w: pltpu.make_async_copy(shards[w], place(w, 0, 0), local_sem.at[w]).start())
+            placed.append(len(ends))
+            ends.append(lambda w=w: pltpu.make_async_copy(shards[w], place(w, 0, 0), local_sem.at[w]).wait())
+            for i in range(1, wide):
+                steps.append(lambda w=w, i=i: along(w, i))
+                ends.append(lambda w=w, i=i: along(w, i, True))
+        for w in range(n):
+            near(w, 0)
+        first = len(steps)
+        order = [(w, 0) for w in range(n)] + [(w, i) for w in range(n) for i in range(1, wide)]
+        for t, (w, i) in enumerate(order):
+            if t >= n:
+                near(w, i)
+            if t >= 2:
+                far(*order[t - 2])
+        for w, i in order[-2:]:
+            far(w, i)
+        for w in range(n):
+            if full[w]:
+                steps.append(ends[placed[w]])
+                ends[placed[w]] = lambda: None
+                for k in range(chips):
+                    for i in range(wide):
+                        take(w, k, i)
+                    steps.append(lambda w=w, k=k: over(w, k))
+        for w in range(n):
+            for i in range(wide):
+                for k in range(chips):
+                    take(w, k, i)
+            if full[w]:
+                for k in range(chips):
+                    steps.append(lambda w=w, k=k: got(w, k))
+                    ends.append(lambda w=w, k=k: over(w, k, True))
+        return steps + ends, first
+
+
+class Scatter:
+    def __init__(self, sizes, entries, absolute, number, pace=1.0):
+        chips, wide = sizes
+        n = len(entries)
+        dma = pltpu.SemaphoreType.DMA
+        self.sizes, self.absolute, self.number, self.pace = sizes, absolute, number, pace
+        self.args, self.where = [], []
+        for array, start, cols in entries:
+            known = [j for j, a in enumerate(self.args) if a is array]
+            if not known:
+                self.args.append(array)
+            self.where.append((known[0] if known else len(self.args) - 1, start, cols))
+        ends = [(array.shape[2], cols) for array, _, cols in entries]
+        self.in_specs = [pl.BlockSpec(memory_space=pl.ANY)] * len(self.args)
+        self.out_specs = [pl.BlockSpec(memory_space=pltpu.VMEM)] * n
+        self.out_shape = [shape_of(e, F32) for e in ends]
+        self.scratch = (
+            [pltpu.VMEM((wide, chips - 1) + e, BF16) for e in ends]
+            + [pltpu.VMEM((wide - 1,) + e, BF16) for e in ends]
+            + [pltpu.VMEM((2,) + e, BF16) for e in ends]
+            + [
+                dma((n, wide, chips - 1)), dma((n, wide, chips - 1)), dma((n, wide - 1)),
+                dma((n, wide - 1)), dma((n, 2)),
+            ]
+        )
+
+    def plan(self, arrays, outs, scratch):
+        chips, wide = self.sizes
+        absolute, n = self.absolute, len(outs)
+        nearby, along, stage = scratch[:n], scratch[n : 2 * n], scratch[2 * n : 3 * n]
+        x_send, x_recv, z_send, z_recv, stage_sem = scratch[3 * n :]
+        steps, ends = [], []
+
+        def own(w, k, i):
+            chip, _, lane = here()
+            j, start, cols = self.where[w]
+            slot = flip(lane, i) if absolute[w] else i
+            if cols == arrays[j].shape[3]:
+                return arrays[j].at[flip(chip, k), slot]
+            return arrays[j].at[flip(chip, k), slot, :, pl.ds(start, cols)]
+
+        def children(q, i):
+            return [k for k in by_distance(chips) if k ^ link_of(k, i) == q]
+
+        def load(w, q, i, turn):
+            pltpu.make_async_copy(own(w, q, i), stage[w].at[turn], stage_sem.at[w, turn]).start()
+
+        def total(w, q, i, turn):
+            pltpu.make_async_copy(own(w, q, i), stage[w].at[turn], stage_sem.at[w, turn]).wait()
+            value = stage[w][turn].astype(F32)
+            for k in children(q, i):
+                await_bytes(nearby[w].at[i, k - 1], x_recv.at[w, i, k - 1])
+                value = value + nearby[w][i, k - 1].astype(F32)
+            return value
+
+        def pass_on(source, w, k, i, sent=False):
+            chip = here()[0]
+            remote(source, nearby[w].at[i, k - 1], {"chip": flip(chip, link_of(k, i))},
+                   x_send.at[w, i, k - 1], x_recv.at[w, i, k - 1], sent)
+
+        def relay(w, k, i, turn):
+            place = children(k, i)[0] - 1
+            nearby[w][i, place] = total(w, k, i, turn).astype(BF16)
+            pass_on(nearby[w].at[i, place], w, k, i)
+
+        def onward(w, i, sent=False):
+            lane = here()[2]
+            remote(nearby[w].at[i, children(0, i)[0] - 1], along[w].at[i - 1], {"ta": flip(lane, i)},
+                   z_send.at[w, i - 1], z_recv.at[w, i - 1], sent)
+
+        def finish(w, i, turn):
+            value = total(w, 0, i, turn)
+            if i == 0:
+                outs[w][...] = value
+                return
+            nearby[w][i, children(0, i)[0] - 1] = value.astype(BF16)
+            onward(w, i)
+
+        def last(w):
+            value = outs[w][...]
+            for i in range(1, wide):
+                await_bytes(along[w].at[i - 1], z_recv.at[w, i - 1])
+                value = value + along[w][i - 1].astype(F32)
+            outs[w][...] = value
+
+        slots = (*range(1, wide), 0)
+        sums = []
+        raw = {w: [] for w in range(n)}
+        for w in range(n):
+            for i in slots:
+                for k in by_distance(chips)[::-1]:
+                    if not children(k, i):
+                        raw[w].append(lambda w=w, k=k, i=i: pass_on(own(w, k, i), w, k, i))
+                    if children(k, i):
+                        ends.append(lambda w=w, k=k, i=i: pass_on(
+                            nearby[w].at[i, children(k, i)[0] - 1], w, k, i, True))
+                    else:
+                        ends.append(lambda w=w, k=k, i=i: pass_on(own(w, k, i), w, k, i, True))
+            mine = [(w, k, i) for i in slots for k in by_distance(chips)[::-1] if children(k, i)]
+            mine += [(w, 0, i) for i in slots]
+            for turn, (_, k, i) in enumerate(mine):
+                sums.append((w, k, i, turn % 2))
+            for i in range(1, wide):
+                ends.append(lambda w=w, i=i: onward(w, i, True))
+        steps.append(lambda: greet(chips, wide, False))
+        steps += raw[0]
+        steps += raw[1] if n > 1 else []
+        first = len(steps)
+        for w in range(n):
+            mine = [t for t in sums if t[0] == w]
+            steps.append(lambda t=mine[0]: load(*t))
+            for j, (_, k, i, turn) in enumerate(mine):
+                if j + 1 < len(mine):
+                    steps.append(lambda t=mine[j + 1]: load(*t))
+                if k:
+                    steps.append(lambda w=w, k=k, i=i, turn=turn: relay(w, k, i, turn))
+                else:
+                    steps.append(lambda w=w, i=i, turn=turn: finish(w, i, turn))
+            if w + 2 < n:
+                steps += raw[w + 2]
+        for w in range(n):
+            steps.append(lambda w=w: last(w))
+        return steps + ends, first
+
+
+def alone(work, name):
+    a, o = len(work.args), len(work.out_shape)
+
+    def kernel(*refs):
+        for step in work.plan(refs[:a], refs[a : a + o], refs[a + o :])[0]:
+            step()
+
+    return pl.pallas_call(
+        kernel,
+        in_specs=work.in_specs,
+        out_specs=work.out_specs,
+        out_shape=work.out_shape,
+        scratch_shapes=work.scratch,
         compiler_params=pltpu.CompilerParams(
-            collective_id=number, has_side_effects=True, vmem_limit_bytes=VMEM_LIMIT
+            collective_id=work.number, has_side_effects=True, vmem_limit_bytes=VMEM_LIMIT
         ),
-        name="gather",
-    )(*shards)
-
-
-def scatter_kernel(sizes, absolute, *refs):
-    chips, wide = sizes
-    n = len(absolute)
-    sources, outs, nearby, along = (refs[j * n : (j + 1) * n] for j in range(4))
-    x_send, x_recv, z_send, z_recv = refs[4 * n :]
-    chip, lane = lax.axis_index("chip"), lax.axis_index("ta")
-    greet(chips, wide, False)
-    sends = []
-
-    def send(source, target, device, send_sem, recv_sem):
-        copy = pltpu.make_async_remote_copy(
-            src_ref=source, dst_ref=target, send_sem=send_sem, recv_sem=recv_sem,
-            device_id=device, device_id_type=MESH,
-        )
-        copy.start()
-        sends.append(copy)
-
-    def own(w, k, i):
-        return sources[w].at[flip(chip, k), flip(lane, i) if absolute[w] else i]
-
-    def children(q, i):
-        return [k for k in by_distance(chips) if k ^ link_of(k, i) == q]
-
-    def total(w, q, i):
-        value = own(w, q, i)[...].astype(F32)
-        for k in children(q, i):
-            piece = nearby[w].at[i, k - 1]
-            pltpu.make_async_copy(piece, piece, x_recv.at[w, i, k - 1]).wait()
-            value = value + piece[...].astype(F32)
-        return value
-
-    def pass_on(source, w, k, i):
-        send(source, nearby[w].at[i, k - 1], {"chip": flip(chip, link_of(k, i))},
-             x_send.at[w, i, k - 1], x_recv.at[w, i, k - 1])
-
-    order = [(w, i) for w in range(n) for i in (*range(1, wide), 0)]
-    for w, i in order:
-        for k in by_distance(chips)[::-1]:
-            if not children(k, i):
-                pass_on(own(w, k, i), w, k, i)
-    for w, i in order:
-        for k in by_distance(chips)[::-1]:
-            if children(k, i):
-                place = nearby[w].at[i, children(k, i)[0] - 1]
-                place[...] = total(w, k, i).astype(BF16)
-                pass_on(place, w, k, i)
-    for w, i in order:
-        value = total(w, 0, i)
-        if i == 0:
-            outs[w][...] = value
-        else:
-            place = nearby[w].at[i, children(0, i)[0] - 1]
-            place[...] = value.astype(BF16)
-            send(place, along[w].at[i - 1], {"ta": flip(lane, i)}, z_send.at[w, i - 1], z_recv.at[w, i - 1])
-    for w in range(n):
-        value = outs[w][...]
-        for i in range(1, wide):
-            piece = along[w].at[i - 1]
-            pltpu.make_async_copy(piece, piece, z_recv.at[w, i - 1]).wait()
-            value = value + piece[...].astype(F32)
-        outs[w][...] = value
-    for copy in sends:
-        copy.wait_send()
-
-
-def scatter(sizes, parts, absolute, number):
-    chips, wide = sizes
-    n = len(parts)
-    ends = [tuple(p.shape[2:]) for p in parts]
-    dma = pltpu.SemaphoreType.DMA
-    return pl.pallas_call(
-        functools.partial(scatter_kernel, sizes, absolute),
-        in_specs=[pl.BlockSpec(memory_space=pltpu.VMEM)] * n,
-        out_specs=[pl.BlockSpec(memory_space=pltpu.VMEM)] * n,
-        out_shape=[shape_of(e, F32) for e in ends],
-        scratch_shapes=[pltpu.VMEM((wide, chips - 1) + e, BF16) for e in ends]
-        + [pltpu.VMEM((wide - 1,) + e, BF16) for e in ends]
-        + [
-            dma((n, wide, chips - 1)), dma((n, wide, chips - 1)), dma((n, wide - 1)), dma((n, wide - 1)),
-        ],
+        name=name,
+    )(*work.args)
+
+
+def beside(kernel, args, groups, in_specs, out_specs, out_shape, scratch, name, points, work=None):
+    if work is None:
+        return pl.pallas_call(
+            lambda *refs: kernel(lambda point: None, *refs),
+            grid=(groups,), in_specs=in_specs, out_specs=out_specs, out_shape=out_shape,
+            scratch_shapes=scratch, compiler_params=params(), name=name,
+        )(*args), ()
+    a, o, s = len(in_specs), len(out_specs), len(scratch)
+    b, p = len(work.args), len(work.out_shape)
+
+    def mixed(*refs):
+        ins, refs = refs[:a], refs[a:]
+        work_ins, refs = refs[:b], refs[b:]
+        outs, refs = refs[:o], refs[o:]
+        work_outs, refs = refs[:p], refs[p:]
+        steps, first = work.plan(work_ins, work_outs, refs[s:])
+        slots = groups * points
+        table = [[] for _ in range(slots)]
+        table[0] = steps[:first]
+        rest = steps[first:]
+        until = int(len(rest) * work.pace)
+        for j, step in enumerate(rest):
+            slot = 1 + j * (slots - 2) // until if j < until else slots - 1
+            table[slot].append(step)
+
+        def pulse(point):
+            for group in range(groups):
+                part = table[group * points + point]
+                if part:
+
+                    @pl.when(pl.program_id(0) == group)
+                    def _():
+                        for step in part:
+                            step()
+
+        kernel(pulse, *ins, *outs, *refs[:s])
+
+    out = pl.pallas_call(
+        mixed,
+        grid=(groups,),
+        in_specs=list(in_specs) + work.in_specs,
+        out_specs=list(out_specs) + work.out_specs,
+        out_shape=list(out_shape) + work.out_shape,
+        scratch_shapes=list(scratch) + work.scratch,
         compiler_params=pltpu.CompilerParams(
-            collective_id=number, has_side_effects=True, vmem_limit_bytes=VMEM_LIMIT
+            dimension_semantics=("arbitrary",), vmem_limit_bytes=VMEM_LIMIT,
+            collective_id=work.number, has_side_effects=True,
         ),
-        name="scatter",
-    )(*parts)
+        name=name,
+    )(*args, *work.args)
+    return out[:o], out[o:]
 
 
 def column_sum(values):
     return jnp.sum(values, axis=0, keepdims=True)
 
 
-def self_forward_kernel(counts, x_ref, w_ref, bias_ref, gains, shifts, cosine, sine, low_ref, pre_ref, att_ref,
+def self_forward_kernel(counts, pulse, x_ref, w_ref, bias_ref, gains, shifts, cosine, sine, low_ref, pre_ref, att_ref,
                         lse_ref, own_ref, other_ref, acc):
     heads, size, own = counts
     step = pl.program_id(0)
+    pulse(0)
     width = heads * size
     weights = flat(w_ref)
     packed = dot(x_ref[...], weights[:, : 3 * width], 1, 0) + bias_ref[0]
@@ -362,18 +499,18 @@
     def _():
         own_ref[...] = acc[:own, :]
         other_ref[...] = acc[own:, :].astype(BF16)
-
-
-def self_forward(x, weights, bias, gains, shifts, cosine, sine, own):
+    pulse(1)
+
+
+def self_forward(x, weights, bias, gains, shifts, cosine, sine, own, work=None):
     length, width = x.shape
     chips, groups, rows, all_cols = weights.shape
     size = gains.shape[1]
     small = all_cols // 4
     cols = 3 * small
     heads = small // size
-    return pl.pallas_call(
-        functools.partial(self_forward_kernel, (heads, size, own)),
-        grid=(groups,),
+    return beside(
+        functools.partial(self_forward_kernel, (heads, size, own)), (x, weights, bias, gains, shifts, cosine, sine), groups,
         in_specs=[whole(x.shape), of_chips(all_cols, weights.shape), per_step(bias.shape)]
         + [whole(gains.shape), whole(shifts.shape), whole(cosine.shape), whole(sine.shape)],
         out_specs=[
@@ -384,7 +521,7 @@
             whole((own, width)),
             whole((length - own, width)),
         ],
-        scratch_shapes=[pltpu.VMEM((length, width), F32)],
+        scratch=[pltpu.VMEM((length, width), F32)],
         out_shape=[
             shape_of((groups, length, cols), BF16),
             shape_of((groups, length, 2 * small), BF16),
@@ -393,9 +530,8 @@
             shape_of((own, width), F32),
             shape_of((length - own, width), BF16),
         ],
-        compiler_params=params(),
-        name="self_forward",
-    )(x, weights, bias, gains, shifts, cosine, sine)
+        name="self_forward", points=2, work=work,
+    )
 
 
 def attention_back(query, key, value, out_grad, logs, block, limit=None):
@@ -420,10 +556,11 @@
     return jnp.concatenate(query_parts, axis=0), key_grad, value_grad
 
 
-def self_backward_kernel(counts, x_ref, grad_ref, w_ref, low_ref, pre_ref, att_ref, lse_ref, gains, cosine, sine,
-                         w_out, own_ref, other_ref, column_ref, head_ref, acc, grad_t, x_t):
+def self_backward_kernel(counts, pulse, x_t, grad_ref, w_ref, low_ref, pre_ref, att_ref, lse_ref, gains, cosine, sine,
+                         w_out, own_ref, other_ref, column_ref, head_ref, acc, grad_t):
     heads, size, own = counts
     step = pl.program_id(0)
+    pulse(0)
     width = heads * size
     scale = size**-0.5
     weights = flat(w_ref)
@@ -432,7 +569,6 @@
     @pl.when(step == 0)
     def _():
         grad_t[...] = jnp.transpose(grad_ref[...])
-        x_t[...] = jnp.transpose(x_ref[...])
 
     out_grad = dot(grad_ref[...], weights[:, 3 * width :], 1, 0).astype(BF16)
     comb_grad = dot(grad_t[...], att_ref[0], 1, 0).astype(BF16)
@@ -456,6 +592,7 @@
         query_grads.append(head_norm_back(dq, q_hat, q_inverse, gains[0:1, :]))
         key_grads.append(head_norm_back(dk, k_hat, k_inverse, gains[1:2, :]))
         value_grads.append(dv)
+        pulse(h + 1)
     packed = jnp.concatenate(query_grads + key_grads + value_grads, axis=1).astype(BF16)
     column_ref[0] = column_sum(packed.astype(F32))
     term = dot(packed, weights[:, : 3 * width], 1, 1)
@@ -477,19 +614,19 @@
     def _():
         own_ref[...] = acc[:own, :]
         other_ref[...] = acc[own:, :].astype(BF16)
-
-
-def self_backward(x, grad, weights, low, pre, att, lse, gains, cosine, sine, own):
-    length, width = x.shape
+    pulse(heads + 1)
+
+
+def self_backward(x_t, grad, weights, low, pre, att, lse, gains, cosine, sine, own, work=None):
+    width, length = x_t.shape
     chips, groups, rows, all_cols = weights.shape
     size = gains.shape[1]
     small = all_cols // 4
     cols = 3 * small
     heads = small // size
-    return pl.pallas_call(
-        functools.partial(self_backward_kernel, (heads, size, own)),
-        grid=(groups,),
-        in_specs=[whole(x.shape), whole(grad.shape), of_chips(all_cols, weights.shape)]
+    return beside(
+        functools.partial(self_backward_kernel, (heads, size, own)), (x_t, grad, weights, low, pre, att, lse, gains, cosine, sine), groups,
+        in_specs=[whole(x_t.shape), whole(grad.shape), of_chips(all_cols, weights.shape)]
         + [per_step(v.shape) for v in (low, pre, att, lse)]
         + [whole(gains.shape), whole(cosine.shape), whole(sine.shape)],
         out_specs=[
@@ -499,9 +636,8 @@
             per_step((groups, 1, cols)),
             whole((4, size)),
         ],
-        scratch_shapes=[
+        scratch=[
             pltpu.VMEM((length, width), F32),
-            pltpu.VMEM((width, length), BF16),
             pltpu.VMEM((width, length), BF16),
         ],
         out_shape=[
@@ -511,15 +647,15 @@
             shape_of((groups, 1, cols), F32),
             shape_of((4, size), F32),
         ],
-        compiler_params=params(),
-        name="self_backward",
-    )(x, grad, weights, low, pre, att, lse, gains, cosine, sine)
-
-
-def cross_forward_kernel(counts, x_ref, text_ref, w_ref, memory_w, bias_ref, memory_bias, gains, shifts, low_ref,
+        name="self_backward", points=heads + 2, work=work,
+    )
+
+
+def cross_forward_kernel(counts, pulse, x_ref, text_ref, w_ref, memory_w, bias_ref, memory_bias, gains, shifts, low_ref,
                          pre_ref, memory_ref, memory_pre, att_ref, lse_ref, own_ref, other_ref, acc):
     heads, size, own, limit = counts
     step = pl.program_id(0)
+    pulse(0)
     width = heads * size
     weights = flat(w_ref)
     pre = dot(x_ref[...], weights[:, :width], 1, 0) + bias_ref[0]
@@ -571,9 +707,10 @@
     def _():
         own_ref[...] = acc[:own, :]
         other_ref[...] = acc[own:, :].astype(BF16)
-
-
-def cross_forward(x, text, weights, memory_w, bias, memory_bias, gains, shifts, own, limit):
+    pulse(1)
+
+
+def cross_forward(x, text, weights, memory_w, bias, memory_bias, gains, shifts, own, limit, work=None):
     length, width = x.shape
     groups, small = weights.shape[1], weights.shape[3] // 2
     text_rows = text.shape[0]
@@ -587,26 +724,25 @@
         ((groups, length, small), BF16),
         ((groups, heads, length), F32),
     ]
-    return pl.pallas_call(
-        functools.partial(cross_forward_kernel, (heads, size, own, limit)),
-        grid=(groups,),
+    return beside(
+        functools.partial(cross_forward_kernel, (heads, size, own, limit)), (x, text, weights, memory_w, bias, memory_bias, gains, shifts), groups,
         in_specs=[whole(x.shape), whole(text.shape)]
         + [of_chips(v.shape[3], v.shape) for v in (weights, memory_w)]
         + [per_step(bias.shape), per_step(memory_bias.shape), whole(gains.shape), whole(shifts.shape)],
         out_specs=[per_step(s) for s, _ in saved] + [whole((own, width)), whole((length - own, width))],
-        scratch_shapes=[pltpu.VMEM((length, width), F32)],
+        scratch=[pltpu.VMEM((length, width), F32)],
         out_shape=[shape_of(*s) for s in saved]
         + [shape_of((own, width), F32), shape_of((length - own, width), BF16)],
-        compiler_params=params(),
-        name="cross_forward",
-    )(x, text, weights, memory_w, bias, memory_bias, gains, shifts)
-
-
-def cross_backward_kernel(counts, x_ref, grad_ref, text_ref, w_ref, memory_w, low_ref, pre_ref, memory_ref,
+        name="cross_forward", points=2, work=work,
+    )
+
+
+def cross_backward_kernel(counts, pulse, x_ref, grad_ref, text_ref, w_ref, memory_w, low_ref, pre_ref, memory_ref,
                           memory_pre, att_ref, lse_ref, gains, w_out, memory_out, own_ref, other_ref, text_out,
                           column_ref, memory_column, head_ref, acc, grad_t, x_t, text_t):
     heads, size, own, limit = counts
     step = pl.program_id(0)
+    pulse(0)
     width = heads * size
     scale = size**-0.5
     weights = flat(w_ref)
@@ -639,6 +775,7 @@
         query_grads.append(head_norm_back(dq, q_hat, q_inverse, gains[2:3, :]))
         key_grads.append(head_norm_back(dk, k_hat, k_inverse, gains[3:4, :]))
         value_grads.append(dv)
+        pulse(h + 1)
     packed = jnp.concatenate(query_grads, axis=1).astype(BF16)
     memory_grad = jnp.concatenate(key_grads + value_grads, axis=1).astype(BF16)
     column_ref[0] = column_sum(packed.astype(F32))
@@ -666,9 +803,10 @@
     def _():
         own_ref[...] = acc[:own, :]
         other_ref[...] = acc[own:, :].astype(BF16)
-
-
-def cross_backward(x, grad, text, weights, memory_w, low, pre, memory, memory_pre, att, lse, gains, own, limit):
+    pulse(heads + 1)
+
+
+def cross_backward(x, grad, text, weights, memory_w, low, pre, memory, memory_pre, att, lse, gains, own, limit, work=None):
     length, width = x.shape
     groups, small = weights.shape[1], weights.shape[3] // 2
     size = gains.shape[1]
@@ -682,33 +820,31 @@
         ((groups, 1, 2 * small), F32, True),
         ((3, size), F32, False),
     ]
-    return pl.pallas_call(
-        functools.partial(cross_backward_kernel, (heads, size, own, limit)),
-        grid=(groups,),
+    return beside(
+        functools.partial(cross_backward_kernel, (heads, size, own, limit)), (x, grad, text, *pieces, low, pre, memory, memory_pre, att, lse, gains), groups,
         in_specs=[whole(x.shape), whole(grad.shape), whole(text.shape)]
         + [of_chips(p.shape[3], p.shape) for p in pieces]
         + [per_step(v.shape) for v in (low, pre, memory, memory_pre, att, lse)]
         + [whole(gains.shape)],
         out_specs=[of_chips(p.shape[3], p.shape) for p in pieces]
         + [per_step(s) if stepped else whole(s) for s, _, stepped in tail],
-        scratch_shapes=[
+        scratch=[
             pltpu.VMEM((length, width), F32),
             pltpu.VMEM((width, length), BF16),
             pltpu.VMEM((width, length), BF16),
             pltpu.VMEM((text.shape[1], text.shape[0]), BF16),
         ],
         out_shape=[shape_of(p.shape, BF16) for p in pieces] + [shape_of(s, d) for s, d, _ in tail],
-        compiler_params=params(),
-        name="cross_backward",
-    )(x, grad, text, *pieces, low, pre, memory, memory_pre, att, lse, gains)
-
-
-def mlp_kernel(own, x_ref, cot_ref, x_t, cot_t, w_ref, bias_ref, w_out, out_own, out_other, back_own, back_other,
+        name="cross_backward", points=heads + 2, work=work,
+    )
+
+
+def mlp_kernel(own, x_ref, cot_ref, x_t, cot_t, w_ref, rest_ref, bias_ref, w_out, out_own, out_other, back_own, back_other,
                hidden_ref, acc, back):
     step = pl.program_id(0)
     chips, _, rows, cols = w_ref.shape
     tile = cols // 2
-    w = flat(w_ref)
+    w = jnp.where(step % MLP_CHUNKS == 0, flat(w_ref), flat(rest_ref))
     hidden = dot(x_ref[...], w[:, :tile], 1, 0) + bias_ref[0]
     square = hidden * hidden
     inner = 0.7978845608028654 * hidden * (1.0 + 0.044715 * square)
@@ -744,9 +880,16 @@
         back_other[...] = back[own:, :].astype(BF16)
 
 
-def mlp(x, cot, x_t, cot_t, weights, bias, own):
+def mlp(x, cot, x_t, cot_t, weights, rest, bias, own):
     length, width = x.shape
-    chips, groups, rows, cols = weights.shape
+    chips, groups, rows, tile = weights.shape
+    cols = tile * MLP_CHUNKS
+    shape = (chips, groups, rows, cols)
+    first = pl.BlockSpec((chips, 1, rows, tile), lambda i: (0, i // MLP_CHUNKS, 0, 0))
+    others = pl.BlockSpec(
+        (chips, 1, rows, tile),
+        lambda i: (0, i // MLP_CHUNKS, 0, jnp.maximum(i % MLP_CHUNKS - 1, 0)),
+    )
     part = pl.BlockSpec(
         (chips, 1, rows, cols // MLP_CHUNKS), lambda i: (0, i // MLP_CHUNKS, 0, i % MLP_CHUNKS)
     )
@@ -754,15 +897,15 @@
     return pl.pallas_call(
         functools.partial(mlp_kernel, own),
         grid=(groups * MLP_CHUNKS,),
-        in_specs=[whole(v.shape) for v in (x, cot, x_t, cot_t)] + [part, per_step(bias.shape)],
+        in_specs=[whole(v.shape) for v in (x, cot, x_t, cot_t)] + [first, others, per_step(bias.shape)],
         out_specs=[part] + [whole(s) for s, _ in tail] + [per_step(bias.shape)],
         scratch_shapes=[pltpu.VMEM((length, width), F32), pltpu.VMEM((length, width), F32)],
-        out_shape=[shape_of(weights.shape, BF16)]
+        out_shape=[shape_of(shape, BF16)]
         + [shape_of(*s) for s in tail]
         + [shape_of(bias.shape, F32)],
         compiler_params=params(),
         name="mlp",
-    )(x, cot, x_t, cot_t, weights, bias)
+    )(x, cot, x_t, cot_t, weights, rest, bias)
 
 
 def row_spec(block, width):
@@ -994,6 +1137,7 @@
     silu_own = jax.nn.silu(times.astype(F32)).astype(BF16)
     small = jnp.concatenate([small, silu_own.astype(F32).reshape(-1)])[None]
     rows, tile = projector.shape[0], hidden_cols // MLP_CHUNKS
+    mesh_sizes = (chips, wide)
 
     def with_tb(value):
         value = value[None]
@@ -1007,8 +1151,9 @@
 
     self_in = jnp.concatenate([projector, combiner.T[:, None]], axis=1)
     self_in = halves(self_in.reshape(rows, 4, 2, head_cols).transpose(0, 2, 1, 3)).reshape(2 * rows, -1)
-    small_all, merger_full, modulator_full, self_w = gather(
-        (chips, wide), [with_tb(small), with_tb(merger), with_tb(modulator), self_in], (True, True, True, False), 1
+    small_all, merger_full, modulator_full, self_w = alone(
+        Gather(mesh_sizes, [with_tb(small), with_tb(merger), with_tb(modulator), self_in], (True, True, True, False), 1),
+        "gather",
     )
     merger_full = merger_full.reshape(2 * width, width)
     modulator_full = modulator_full.reshape(width, width)
@@ -1042,7 +1187,7 @@
     memory_in = memory_in.reshape(2 * text_rows_w, 2 * head_cols)
     mlp_in = jnp.stack([expander, reducer.T], axis=1).reshape(rows, 2, 2, MLP_CHUNKS, tile)
     mlp_in = halves(mlp_in.transpose(0, 2, 3, 1, 4)).reshape(2 * rows, 2 * hidden_cols)
-    cross_w, memory_w, mlp_w = gather((chips, wide), [cross_in, memory_in, mlp_in], (False,) * 3, 2)
+    mlp_parts = [mlp_in[:, : 2 * tile], mlp_in[:, 2 * tile :]]
 
     mod_rows = modulator.shape[0]
     device = ((chip_index * 2 + core) * wide + lane) * deep + side
@@ -1119,9 +1264,11 @@
         norm([first], rows_of(zero_row, gains[2:3], biases[2:3] + biases[6:7] + mod), keep=False)
     )
     self_bias = own_biases[:, 0:3].reshape(wide, 1, 3 * head_cols)
-    self_low, self_pre, self_att, self_lse, part_own, part_other = self_forward(
-        x_self, self_w, self_bias, per_head_norm_gains, head_shifts, cosine, sine, own_len
-    )
+    outs, (cross_w, memory_w, mlp_first) = self_forward(
+        x_self, self_w, self_bias, per_head_norm_gains, head_shifts, cosine, sine, own_len,
+        Gather(mesh_sizes, [cross_in, memory_in, mlp_parts[0]], (False,) * 3, 2, PACES[0]),
+    )
+    self_low, self_pre, self_att, self_lse, part_own, part_other = outs
     x_cross, second = norm(
         [first, part_own, *scatter_tokens(part_other)], rows_of(biases[7:8], gains[3:4], biases[3:4])
     )
@@ -1134,10 +1281,12 @@
     text = jnp.pad(text, ((0, text_pad), (0, 0)))
     cross_bias = own_biases[:, 3:4]
     memory_bias = own_biases[:, 4:6].reshape(wide, 1, 2 * head_cols)
-    cross_low, cross_pre, memory_low, memory_pre, cross_att, cross_lse, part_own, part_other = cross_forward(
+    outs, (mlp_rest,) = cross_forward(
         x_cross, text, cross_w, memory_w, cross_bias, memory_bias,
         per_head_norm_gains, head_shifts, own_len, text_len,
-    )
+        Gather(mesh_sizes, [mlp_parts[1]], (False,), 3, PACES[1]),
+    )
+    cross_low, cross_pre, memory_low, memory_pre, cross_att, cross_lse, part_own, part_other = outs
     x_mlp, third = norm(
         [second, part_own, *scatter_tokens(part_other)], rows_of(biases[8:9], gains[4:5], biases[4:5])
     )
@@ -1146,9 +1295,9 @@
     own_hidden = at(at(hidden_all, side, 1), core, 1)
     own_hidden = jnp.stack([at(own_hidden, lane ^ i) for i in range(wide)]).reshape(wide * MLP_CHUNKS, 1, tile)
     mlp_g, out_own, out_other, back_own, back_other, hidden_sum = mlp(
-        x_mlp, cot_all, x_mlp.T, cot_all.T, mlp_w, own_hidden, own_len
-    )
-    (mlp_grad,) = scatter((chips, wide), [mlp_g], (False,), 3)
+        x_mlp, cot_all, x_mlp.T, cot_all.T, mlp_first, mlp_rest, own_hidden, own_len
+    )
+    mlp_entries = [(mlp_g, 2 * tile * j, 2 * tile) for j in range(MLP_CHUNKS)]
     outs = [third, out_own, *scatter_tokens(out_other)]
     backs = [back_own, *scatter_tokens(back_other)]
     block_total = sum(v.astype(F32) for v in outs) + out_bias
@@ -1156,23 +1305,21 @@
 
     third_low, mlp_sums, third_grad = norm_back(backs, third, cot, gains[4:5])
     blender_g_in = gather_tokens(third_low)
-    cross_g, memory_g, part_own, part_other, text_part, query_col, memory_col, cross_heads = cross_backward(
+    outs, mlp_grad_first = cross_backward(
         x_cross, blender_g_in, text, cross_w, memory_w, cross_low, cross_pre,
         memory_low, memory_pre, cross_att, cross_lse, per_head_norm_gains, own_len, text_len,
-    )
-    cross_grad, memory_grads = scatter((chips, wide), [cross_g, memory_g], (False, False), 4)
-    cross_grad = unhalves(cross_grad.reshape(2 * rows, 2, head_cols)).transpose(2, 0, 1, 3)
-    query_grads = cross_grad[0].reshape(rows, tensor_cols)
-    blender_grads = cross_grad[1].reshape(rows, tensor_cols).T
-    memory_grads = unhalves(memory_grads.reshape(2 * text_rows_w, 2, head_cols))
-    memory_grads = memory_grads.transpose(0, 2, 1, 3).reshape(text_rows_w, 2, tensor_cols)
+        Scatter(mesh_sizes, mlp_entries[:1], (False,), 4, PACES[2]),
+    )
+    cross_g, memory_g, part_own, part_other, text_part, query_col, memory_col, cross_heads = outs
     second_low, cross_sums, second_grad = norm_back(
         [part_own, *scatter_tokens(part_other)], second, third_grad, gains[3:4]
     )
-    self_g, part_own, part_other, self_col, self_heads = self_backward(
-        x_self, gather_tokens(second_low), self_w, self_low, self_pre, self_att,
+    outs, mlp_grad_rest = self_backward(
+        x_self.T, gather_tokens(second_low), self_w, self_low, self_pre, self_att,
         self_lse, per_head_norm_gains, cosine, sine, own_len,
-    )
+        Scatter(mesh_sizes, mlp_entries[1:], (False,) * (MLP_CHUNKS - 1), 5, PACES[3]),
+    )
+    self_g, part_own, part_other, self_col, self_heads = outs
     first_low, self_sums = norm_back(
         [part_own, *scatter_tokens(part_other)], first, second_grad, gains[2:3], keep=False
     )
@@ -1190,11 +1337,23 @@
         sent = jnp.where(high, low_part, high_part).astype(BF16)
         value = jnp.where(high, high_part, low_part) + swap(sent, "tb", deep, mask).astype(F32)
     merger_g = value.astype(BF16).reshape(chips, wide, -1, width)
-    self_grad, merger_grads = scatter((chips, wide), [self_g, merger_g], (False, True), 5)
+    self_grad, cross_grad, memory_grads, merger_grads = alone(
+        Scatter(
+            mesh_sizes, [(v, 0, v.shape[3]) for v in (self_g, cross_g, memory_g, merger_g)],
+            (False, False, False, True), 6,
+        ),
+        "scatter",
+    )
+    cross_grad = unhalves(cross_grad.reshape(2 * rows, 2, head_cols)).transpose(2, 0, 1, 3)
+    query_grads = cross_grad[0].reshape(rows, tensor_cols)
+    blender_grads = cross_grad[1].reshape(rows, tensor_cols).T
+    memory_grads = unhalves(memory_grads.reshape(2 * text_rows_w, 2, head_cols))
+    memory_grads = memory_grads.transpose(0, 2, 1, 3).reshape(text_rows_w, 2, tensor_cols)
     self_grad = unhalves(self_grad.reshape(2 * rows, 4, head_cols)).transpose(0, 2, 1, 3)
     projector_grads = self_grad[:, :3].reshape(rows, 3, tensor_cols)
     combiner_grads = self_grad[:, 3].reshape(rows, tensor_cols).T
 
+    mlp_grad = jnp.stack([*mlp_grad_first, *mlp_grad_rest], axis=1)
     mlp_grad = unhalves(mlp_grad.reshape(2 * rows, MLP_CHUNKS, 2, tile)).transpose(3, 0, 1, 2, 4)
     expander_grads = mlp_grad[0].reshape(rows, 2 * hidden_cols)
     reducer_grads = mlp_grad[1].reshape(rows, 2 * hidden_cols).T

time: 1630 us -> 1470 us (0.902)
  Pallas kernels: 1270 us -> 1060 us
  local copies, waits for them, and re-layouts: 137 us -> 162 us
  waiting for transfers between devices: 67.5 us -> 91.6 us
    pallas_call x9 -> x6, Pallas kernels: 1120 us -> 900 us  [the longest x4 567 us: beside(): pl.pallas_call(mixed, grid=(groups,), in_specs=list(in_specs) + work.in_s...]
    ppermute x57, waiting for transfers between devices: 67.5 us -> 91.6 us  [swap(): return lax.ppermute(value, axis, [(i, i ^ mask) for i in range(size)])]
  transfers between devices with their start and end apart: 57 -> 57, of which waited for: 11 -> 16; matrix products, arithmetic and copies ran while one was open for 12% -> 14% of each run, Pallas kernels for 58% -> 22%
where the time goes in v3:
time: 1470 us
  Pallas kernels  1060 us (72%)
  local copies, waits for them, and re-layouts  162 us (11%)
  waiting for transfers between devices  91.6 us (6%)
  other arithmetic  76.8 us (5%)
  starting transfers between devices  65.1 us (4%)
  matrix products  15.2 us (1%)
    pallas_call x4, Pallas kernels, beside(): pl.pallas_call(mixed, grid=(groups,), in_specs=list(in_specs) + work.in_s...  567 us
    pallas_call x2, Pallas kernels, alone(): pl.pallas_call(kernel, in_specs=work.in_specs, out_specs=work.out_specs,...  334 us
    ppermute x57, waiting for transfers between devices, swap(): return lax.ppermute(value, axis, [(i, i ^ mask) for i in range(size)])  91.6 us
    pallas_call x1, Pallas kernels, mlp(): pl.pallas_call(functools.partial(mlp_kernel, own), grid=(groups * MLP_CHU...  90.4 us
    ppermute x57, starting transfers between devices, swap(): return lax.ppermute(value, axis, [(i, i ^ mask) for i in range(size)])  65.1 us
  transfers between devices with their start and end apart: 57, of which 16 were waited for; matrix products, arithmetic and copies ran while one was open for 14% of the time, Pallas kernels for 22%

profile of v3, /device:TPU:9, one launch (start us, length us, event | category | flops | bytes accessed | tf_op | source)
XLA Modules:
  0.0 1469.1 jit_solution(3247542085295810275)
XLA Ops:
  32.6 137.6 %gather.1 = (f32[4,2,4,1,3932]{4,3,2,1,0:T(1,128)}, bf16[4,2,4,88,1408]{4,3,2,1,0:T(8,128)(2,1)}, bf16[4,2,4,44,1408]{4,3,2,1,0:T(8,128)(2,1)}, bf16[4,4,352,704]{3,2,1,0:T(8,128)(2,1)}) custom-call(f32[1,3932]{1,0:T(1,128)} %broadcast_in_dim.82.refs_0_, bf16[88,1408]{1,0:T(8,128)(2,1)} %refs_1_.1, bf16[44,1408]{1,0:T(8,128)(2,1)} %refs_2_.1, ...), custom_call_target="tpu_custom_call" | custom-call | tf_op jit(solution)/shard_map/gather/pallas_call | solution.py:377
  175.4 11.9 merge.1
  192.0 3.0 sine_multiply_fusion
  200.8 6.0 reshape.589
  206.8 2.8 convolution_reduce_fusion
  211.7 3.0 collective-permute-start.3
  215.4 21.4 %collective-permute-done.4 = bf16[128,1408]{1,0:T(8,128)(2,1)S(1)} collective-permute-done((bf16[128,1408]{1,0:T(8,128)(2,1)S(1)}, bf16[128,1408]{1,0:T(8,128)(2,1)S(1)}, u32[]{:S(2)}, u32[]{:S(2)}) %collective-permute-start.4) | collective-permute-done | bytes 360480 | tf_op jit(solution)/shard_map/ppermute | solution.py:27
  236.8 5.8 collective-permute-done.3
  244.3 4.1 norm.3
  270.9 4.6 fusion.52
  275.5 4.5 copy.250.refs_0_
  280.1 156.4 %self_forward.1 = (bf16[4,1024,528]{2,1,0:T(8,128)(2,1)}, bf16[4,1024,352]{2,1,0:T(8,128)(2,1)}, bf16[4,1024,176]{2,1,0:T(8,128)(2,1)}, f32[4,2,1024]{2,1,0:T(2,...) custom-call(bf16[1024,1408]{1,0:T(8,128)(2,1)} %copy.250.refs_0_, ...), custom_call_target="tpu_custom_call" | custom-call | tf_op jit(solution)/shard_map/self_forward/pallas_call | solution.py:427
  436.4 3.6 collective-permute-start.9
  447.3 5.2 norm.4
  468.8 139.0 %cross_forward.1 = (bf16[4,1024,176]{2,1,0:T(8,128)(2,1)}, bf16[4,1024,176]{2,1,0:T(8,128)(2,1)}, bf16[4,336,352]{2,1,0:T(8,128)(2,1)}, bf16[4,336,176]{2,1,0:T(...) custom-call(bf16[1024,1408]{1,0:T(8,128)(2,1)} %constant_dynamic-upd, ...), custom_call_target="tpu_custom_call" | custom-call | tf_op jit(solution)/shard_map/cross_forward/pallas_call | solution.py:427
  612.8 5.7 norm.5
  622.4 4.6 fusion.50
  627.0 4.7 copy.259.cot_t
  631.7 4.7 fusion.51
  636.4 4.6 copy.258.x_ref
  641.0 90.4 %mlp.1 = (bf16[4,4,352,1536]{3,2,1,0:T(8,128)(2,1)}, f32[512,1408]{1,0:T(8,128)}, bf16[512,1408]{1,0:T(8,128)(2,1)}, f32[512,1408]{1,0:T(8,128)}, bf16[512,1408]{1,0:T(8,128)(2,1)}, /*index=5*/f32[12,1,256]{2,1,0:T(1,128)}) custom-call(bf16[1024,1408]{1,0:T(8,128)(2,1)} %copy.258.x_ref, bf16[1024,1408]{1,0:T(8,128)(2,1)} %get-tuple-element.253.cot_ref, ...), custom_call_target="tpu_custom_call" | custom-call | tf_op jit(solution)/shard_map/mlp/pallas_call | solution.py:897
  732.2 3.0 collective-permute-done.24.refs_1_
  735.1 7.1 norm_back.3
  742.4 3.6 add_convert_fusion
  746.7 13.2 collective-permute-start.21
  761.0 21.3 %collective-permute-done.21 = bf16[128,1408]{1,0:T(8,128)(2,1)S(1)} collective-permute-done((bf16[128,1408]{1,0:T(8,128)(2,1)S(1)}, bf16[128,1408]{1,0:T(8,128)(2,1)S(1)}, u32[]{:S(2)}, u32[]{:S(2)}) %collective-permute-start.21) | collective-permute-done | bytes 360480 | tf_op jit(solution)/shard_map/ppermute | solution.py:27
  786.4 103.3 %cross_backward.1 = (bf16[4,4,352,352]{3,2,1,0:T(8,128)(2,1)}, bf16[4,4,256,352]{3,2,1,0:T(8,128)(2,1)}, f32[512,1408]{1,0:T(8,128)}, bf16[512,1408]{1,0:T(8,128...) custom-call(bf16[1024,1408]{1,0:T(8,128)(2,1)} %constant_dynamic-upd, ...), custom_call_target="tpu_custom_call" | custom-call | tf_op jit(solution)/shard_map/cross_backward/pallas_call | solution.py:427
  889.8 2.8 collective-permute-start.26
  898.3 7.6 norm_back.4
  909.7 3.8 copy.260
  926.3 5.7 collective-permute-done.35
  933.8 3.2 pad_maximum_fusion.4.refs_1_
  937.0 168.1 %self_backward.1 = (bf16[4,4,352,704]{3,2,1,0:T(8,128)(2,1)}, f32[512,1408]{1,0:T(8,128)}, bf16[512,1408]{1,0:T(8,128)(2,1)}, f32[4,1,528]{2,1,0:T(1,128)}, f32[...) custom-call(bf16[1408,1024]{1,0:T(8,128)(2,1)} %get-tuple-element.250.refs_0_, ...), custom_call_target="tpu_custom_call" | custom-call | tf_op jit(solution)/shard_map/self_backward/pallas_call | solution.py:427
  1105.1 3.3 collective-permute-start.28
  1124.0 6.5 norm_back.5
  1131.2 3.1 collective-permute-start.37
  1146.6 20.7 %collective-permute-done.31 = bf16[128,1408]{1,0:T(8,128)(2,1)S(1)} collective-permute-done((bf16[128,1408]{1,0:T(8,128)(2,1)S(1)}, bf16[128,1408]{1,0:T(8,128)(2,1)S(1)}, u32[]{:S(2)}, u32[]{:S(2)}) %collective-permute-start.31) | collective-permute-done | bytes 360480 | tf_op jit(solution)/shard_map/ppermute | solution.py:27
  1167.3 7.0 collective-permute-done.30
  1183.5 2.8 maximum_select_fusion.5
  1186.4 17.1 %merge_back.1 = (f32[512,1408]{1,0:T(8,128)}, f32[512,1408]{1,0:T(8,128)}, bf16[512,2816]{1,0:T(8,128)(2,1)}, f32[5,1408]{1,0:T(8,128)}) custom-call(bf16[512,1408]{1,0:T(8,128)(2,1)} %bitcast.250, bf16[512,1408]{1,0:T(8,128)(2,1)} %bitcast.252, bf16[512,1408]{1,0:T(8,128)(2,1)} %bitcast.259, bf16[2816,1408]{1,0:T(8,128)(2,1)} %bitcast.244, ...), custom_call_target="tpu_custom_call" | custom-call | tf_op jit(solution)/shard_map/merge_back/pallas_call | solution.py:987
  1207.2 8.7 convolution_convert_fusion
  1217.2 4.6 dynamic-slice_bitcast_fusion
  1222.4 3.2 collective-permute-start.45
  1228.5 2.7 fusion.41
  1232.6 7.0 copy_bitcast_fusion
  1243.1 6.3 fusion
  1249.4 195.9 %scatter.1 = (f32[352,704]{1,0:T(8,128)}, f32[352,352]{1,0:T(8,128)}, f32[256,352]{1,0:T(8,128)}, f32[88,1408]{1,0:T(8,128)}) custom-call(bf16[4,4,352,704]{3,2,1,0:T(8,128)(2,1)} %get-tuple-element.129.refs_0_, bf16[4,4,352,352]{3,2,1,0:T(8,128)(2,1)} %get-tuple-element.130.refs_1_, bf16[4,4,256,352]{3,2,1,0:T(8,128)(2,1)} %get-tuple-element.131.refs_2_, ...), custom_call_target="tpu_custom_call" | custom-call | tf_op jit(solution)/shard_map/scatter/pallas_call | solution.py:377
  1463.6 3.2 reshape.608
  (518 shorter events, 208.1 us)
Async XLA Ops:
  2.4 193.9 %collective-permute-start.7 = (bf16[128,2,176]{0,2,1:T(8,128)(2,1)}, bf16[128,2,176]{0,2,1:T(8,128)(2,1)}, u32[]{:S(2)}, u32[]{:S(2)}) collective-permute-start(bf16[128,2,176]{0,2,1:T(8,128)(2,1)} %get-tuple-element.325), channel_id=1, source_target_pairs={{0,4},{4,0},{1,5},{5,1},{2,6},{6,2},{3,7},{7,3},{8,12},{12,8},{9,1... | collective-permute-start | bytes 270344 | tf_op jit(solution)/shard_map/ppermute | solution.py:27
  7.9 243.1 %collective-permute-start.6 = (bf16[176,2,176]{2,1,0:T(2,128)(2,1)}, bf16[176,2,176]{2,1,0:T(2,128)(2,1)}, u32[]{:S(2)}, u32[]{:S(2)}) collective-permute-start(bf16[176,2,176]{2,1,0:T(2,128)(2,1)} %bitcast.236), channel_id=1, source_target_pairs={{0,4},{4,0},{1,5},{5,1},{2,6},{6,2},{3,7},{7,3},{8,12},{12,8},{9,1... | collective-permute-start | bytes 371720 | tf_op jit(solution)/shard_map/ppermute | solution.py:27
  13.2 248.1 %collective-permute-start.8 = (bf16[176,3,2,256]{3,0,2,1:T(8,128)(2,1)}, bf16[176,3,2,256]{3,0,2,1:T(8,128)(2,1)}, u32[]{:S(2)}, u32[]{:S(2)}) collective-permute-start(bf16[176,3,2,256]{3,0,2,1:T(8,128)(2,1)} %copy.247), channel_id=1, source_target_pairs={{0,4},{4,0},{1,5},{5,1},{2,6},{6,2},{3,7},{7,3},{8,12},{12,8},{9,1... | collective-permute-start | bytes 1622024 | tf_op jit(solution)/shard_map/ppermute | solution.py:27
  17.3 12.0 collective-permute-start
  189.7 19.9 %collective-permute-start.1 = (bf16[2,128,1408]{2,1,0:T(8,128)(2,1)}, bf16[2,128,1408]{2,1,0:T(8,128)(2,1)}, u32[]{:S(2)}, u32[]{:S(2)}) collective-permute-start(bf16[2,128,1408]{2,1,0:T(8,128)(2,1)} %get-tuple-element.303), channel_id=1, source_target_pairs={{0,4},{4,0},{1,5},{5,1},{2,6},{6,2},{3,7},{7,3},{8,12},{12,8},{9,1... | collective-permute-start | bytes 2162696 | tf_op jit(solution)/shard_map/ppermute | solution.py:27
  211.4 25.5 %collective-permute-start.4 = (bf16[128,1408]{1,0:T(8,128)(2,1)S(1)}, bf16[128,1408]{1,0:T(8,128)(2,1)S(1)}, u32[]{:S(2)}, u32[]{:S(2)}) collective-permute-start(bf16[128,1408]{1,0:T(8,128)(2,1)S(1)} %get-tuple-element.299), channel_id=1, source_target_pairs={{0,3},{1,2},{2,1},{3,0},{4,7},{5,6},{6,5},{7,4},{8,11},{9,10},{10,... | collective-permute-start | bytes 1081352 | tf_op jit(solution)/shard_map/ppermute | solution.py:27
  211.7 30.9 %collective-permute-start.3 = (bf16[128,1408]{1,0:T(8,128)(2,1)S(1)}, bf16[128,1408]{1,0:T(8,128)(2,1)S(1)}, u32[]{:S(2)}, u32[]{:S(2)}) collective-permute-start(bf16[128,1408]{1,0:T(8,128)(2,1)S(1)} %get-tuple-element.300), channel_id=1, source_target_pairs={{0,2},{1,3},{2,0},{3,1},{4,6},{5,7},{6,4},{7,5},{8,10},{9,11},{10,... | collective-permute-start | bytes 1081352 | tf_op jit(solution)/shard_map/ppermute | solution.py:27
  214.7 27.9 %collective-permute-start.2 = (bf16[128,1408]{1,0:T(8,128)(2,1)S(1)}, bf16[128,1408]{1,0:T(8,128)(2,1)S(1)}, u32[]{:S(2)}, u32[]{:S(2)}) collective-permute-start(bf16[128,1408]{1,0:T(8,128)(2,1)S(1)} %get-tuple-element.301), channel_id=1, source_target_pairs={{0,1},{1,0},{2,3},{3,2},{4,5},{5,4},{6,7},{7,6},{8,9},{9,8},{10,11... | collective-permute-start | bytes 1081352 | tf_op jit(solution)/shard_map/ppermute | solution.py:27
  250.0 20.8 %collective-permute-start.5 = (bf16[512,1408]{0,1:T(8,128)(2,1)S(1)}, bf16[512,1408]{0,1:T(8,128)(2,1)}, u32[]{:S(2)}, u32[]{:S(2)}) collective-permute-start(bf16[512,1408]{0,1:T(8,128)(2,1)S(1)} %copy.238), channel_id=1, source_target_pairs={{0,4},{4,0},{1,5},{5,1},{2,6},{6,2},{3,7},{7,3},{8,12},{12,8},{9,1... | collective-permute-start | bytes 4325384 | tf_op jit(solution)/shard_map/ppermute | solution.py:27
  436.4 10.9 collective-permute-start.9
  442.5 15.7 %collective-permute-start.11 = (bf16[333,1024]{1,0:T(8,128)(2,1)}, bf16[333,1024]{1,0:T(8,128)(2,1)}, u32[]{:S(2)}, u32[]{:S(2)}) collective-permute-start(bf16[333,1024]{1,0:T(8,128)(2,1)} %bitcast.231), channel_id=1, source_target_pairs={{0,4},{4,0},{1,5},{5,1},{2,6},{6,2},{3,7},{7,3},{8,12},{12,8},{9,1... | collective-permute-start | bytes 2045960 | tf_op jit(solution)/shard_map/ppermute | solution.py:27
  446.3 14.1 collective-permute-start.14
  452.6 13.6 collective-permute-start.10
  462.3 146.5 %collective-permute-start.17 = (bf16[128,1408]{1,0:T(8,128)(2,1)S(1)}, bf16[128,1408]{1,0:T(8,128)(2,1)}, u32[]{:S(2)}, u32[]{:S(2)}) collective-permute-start(bf16[128,1408]{1,0:T(8,128)(2,1)S(1)} %get-tuple-element.287), channel_id=1, source_target_pairs={{0,3},{1,2},{2,1},{3,0},{4,7},{5,6},{6,5},{7,4},{8,11},{9,10},{10,... | collective-permute-start | bytes 1081352 | tf_op jit(solution)/shard_map/ppermute | solution.py:27
  462.3 146.5 %collective-permute-start.16 = (bf16[128,1408]{1,0:T(8,128)(2,1)S(1)}, bf16[128,1408]{1,0:T(8,128)(2,1)}, u32[]{:S(2)}, u32[]{:S(2)}) collective-permute-start(bf16[128,1408]{1,0:T(8,128)(2,1)S(1)} %get-tuple-element.288), channel_id=1, source_target_pairs={{0,2},{1,3},{2,0},{3,1},{4,6},{5,7},{6,4},{7,5},{8,10},{9,11},{10,... | collective-permute-start | bytes 1081352 | tf_op jit(solution)/shard_map/ppermute | solution.py:27
  463.9 144.9 %collective-permute-start.15 = (bf16[128,1408]{1,0:T(8,128)(2,1)S(1)}, bf16[128,1408]{1,0:T(8,128)(2,1)}, u32[]{:S(2)}, u32[]{:S(2)}) collective-permute-start(bf16[128,1408]{1,0:T(8,128)(2,1)S(1)} %get-tuple-element.289), channel_id=1, source_target_pairs={{0,1},{1,0},{2,3},{3,2},{4,5},{5,4},{6,7},{7,6},{8,9},{9,8},{10,11... | collective-permute-start | bytes 1081352 | tf_op jit(solution)/shard_map/ppermute | solution.py:27
  607.8 5.0 collective-permute-start.12
  611.7 10.7 collective-permute-start.18
  620.2 11.5 collective-permute-start.13
  731.6 10.8 collective-permute-start.19
  742.2 41.8 %collective-permute-start.25 = (bf16[512,1408]{1,0:T(8,128)(2,1)}, bf16[512,1408]{1,0:T(8,128)(2,1)S(1)}, u32[]{:S(2)}, u32[]{:S(2)}) collective-permute-start(bf16[512,1408]{1,0:T(8,128)(2,1)} %get-tuple-element.105), channel_id=1, source_target_pairs={{0,4},{4,0},{1,5},{5,1},{2,6},{6,2},{3,7},{7,3},{8,12},{12,8},{9,1... | collective-permute-start | bytes 4325384 | tf_op jit(solution)/shard_map/ppermute | solution.py:27
  746.1 14.9 %collective-permute-start.22 = (bf16[128,1408]{1,0:T(8,128)(2,1)S(1)}, bf16[128,1408]{1,0:T(8,128)(2,1)S(1)}, u32[]{:S(2)}, u32[]{:S(2)}) collective-permute-start(bf16[128,1408]{1,0:T(8,128)(2,1)S(1)} %get-tuple-element.279), channel_id=1, source_target_pairs={{0,3},{1,2},{2,1},{3,0},{4,7},{5,6},{6,5},{7,4},{8,11},{9,10},{10,... | collective-permute-start | bytes 1081352 | tf_op jit(solution)/shard_map/ppermute | solution.py:27
  746.7 35.7 %collective-permute-start.21 = (bf16[128,1408]{1,0:T(8,128)(2,1)S(1)}, bf16[128,1408]{1,0:T(8,128)(2,1)S(1)}, u32[]{:S(2)}, u32[]{:S(2)}) collective-permute-start(bf16[128,1408]{1,0:T(8,128)(2,1)S(1)} %get-tuple-element.280), channel_id=1, source_target_pairs={{0,2},{1,3},{2,0},{3,1},{4,6},{5,7},{6,4},{7,5},{8,10},{9,11},{10,... | collective-permute-start | bytes 1081352 | tf_op jit(solution)/shard_map/ppermute | solution.py:27
  759.8 22.9 %collective-permute-start.20 = (bf16[128,1408]{1,0:T(8,128)(2,1)S(1)}, bf16[128,1408]{1,0:T(8,128)(2,1)S(1)}, u32[]{:S(2)}, u32[]{:S(2)}) collective-permute-start(bf16[128,1408]{1,0:T(8,128)(2,1)S(1)} %get-tuple-element.281), channel_id=1, source_target_pairs={{0,1},{1,0},{2,3},{3,2},{4,5},{5,4},{6,7},{7,6},{8,9},{9,8},{10,11... | collective-permute-start | bytes 1081352 | tf_op jit(solution)/shard_map/ppermute | solution.py:27
  889.8 8.6 collective-permute-start.26
  895.2 12.9 collective-permute-start.23
  897.0 17.1 %collective-permute-start.33 = (bf16[336,1024]{1,0:T(8,128)(2,1)}, bf16[336,1024]{1,0:T(8,128)(2,1)}, u32[]{:S(2)}, u32[]{:S(2)}) collective-permute-start(bf16[336,1024]{1,0:T(8,128)(2,1)} %convert_element_type.108), channel_id=1, source_target_pairs={{0,4},{4,0},{1,5},{5,1},{2,6},{6,2},{3,7},{7,3},{8,12},{12,8},{9,1... | collective-permute-start | bytes 2064392 | tf_op jit(solution)/shard_map/ppermute | solution.py:27
  905.9 27.9 %collective-permute-start.27 = (bf16[512,1408]{1,0:T(8,128)(2,1)}, bf16[512,1408]{1,0:T(8,128)(2,1)}, u32[]{:S(2)}, u32[]{:S(2)}) collective-permute-start(bf16[512,1408]{1,0:T(8,128)(2,1)} %get-tuple-element.116), channel_id=1, source_target_pairs={{0,4},{4,0},{1,5},{5,1},{2,6},{6,2},{3,7},{7,3},{8,12},{12,8},{9,1... | collective-permute-start | bytes 4325384 | tf_op jit(solution)/shard_map/ppermute | solution.py:27
  920.4 5.9 collective-permute-start.36
  920.9 5.4 collective-permute-start.34
  920.9 11.1 collective-permute-start.35
  1105.1 18.8 %collective-permute-start.28 = (bf16[512,1408]{1,0:T(8,128)(2,1)}, bf16[512,1408]{1,0:T(8,128)(2,1)}, u32[]{:S(2)}, u32[]{:S(2)}) collective-permute-start(bf16[512,1408]{1,0:T(8,128)(2,1)} %get-tuple-element.122), channel_id=1, source_target_pairs={{0,4},{4,0},{1,5},{5,1},{2,6},{6,2},{3,7},{7,3},{8,12},{12,8},{9,1... | collective-permute-start | bytes 4325384 | tf_op jit(solution)/shard_map/ppermute | solution.py:27
  1111.4 5.4 collective-permute-start.52
  1118.2 21.7 %collective-permute-start.51 = (f32[176,3,2,256]{3,0,2,1:T(8,128)}, f32[176,3,2,256]{3,0,2,1:T(8,128)}, u32[]{:S(2)}, u32[]{:S(2)}) collective-permute-start(f32[176,3,2,256]{3,0,2,1:T(8,128)} %get-tuple-element.259), channel_id=1, source_target_pairs={{0,4},{4,0},{1,5},{5,1},{2,6},{6,2},{3,7},{7,3},{8,12},{12,8},{9,1... | collective-permute-start | bytes 3244040 | tf_op jit(solution)/shard_map/ppermute | solution.py:27
  1122.8 11.6 collective-permute-start.55
  1142.8 24.5 %collective-permute-start.31 = (bf16[128,1408]{1,0:T(8,128)(2,1)S(1)}, bf16[128,1408]{1,0:T(8,128)(2,1)S(1)}, u32[]{:S(2)}, u32[]{:S(2)}) collective-permute-start(bf16[128,1408]{1,0:T(8,128)(2,1)S(1)} %get-tuple-element.269), channel_id=1, source_target_pairs={{0,3},{1,2},{2,1},{3,0},{4,7},{5,6},{6,5},{7,4},{8,11},{9,10},{10,... | collective-permute-start | bytes 1081352 | tf_op jit(solution)/shard_map/ppermute | solution.py:27
  1143.9 30.3 %collective-permute-start.30 = (bf16[128,1408]{1,0:T(8,128)(2,1)S(1)}, bf16[128,1408]{1,0:T(8,128)(2,1)S(1)}, u32[]{:S(2)}, u32[]{:S(2)}) collective-permute-start(bf16[128,1408]{1,0:T(8,128)(2,1)S(1)} %get-tuple-element.270), channel_id=1, source_target_pairs={{0,2},{1,3},{2,0},{3,1},{4,6},{5,7},{6,4},{7,5},{8,10},{9,11},{10,... | collective-permute-start | bytes 1081352 | tf_op jit(solution)/shard_map/ppermute | solution.py:27
  1145.7 28.6 %collective-permute-start.29 = (bf16[128,1408]{1,0:T(8,128)(2,1)S(1)}, bf16[128,1408]{1,0:T(8,128)(2,1)S(1)}, u32[]{:S(2)}, u32[]{:S(2)}) collective-permute-start(bf16[128,1408]{1,0:T(8,128)(2,1)S(1)} %get-tuple-element.271), channel_id=1, source_target_pairs={{0,1},{1,0},{2,3},{3,2},{4,5},{5,4},{6,7},{7,6},{8,9},{9,8},{10,11... | collective-permute-start | bytes 1081352 | tf_op jit(solution)/shard_map/ppermute | solution.py:27
  1145.7 36.9 %collective-permute-start.41 = (f32[2,4,1408]{2,1,0:T(4,128)S(1)}, f32[2,4,1408]{2,1,0:T(4,128)}, u32[]{:S(2)}, u32[]{:S(2)}) collective-permute-start(f32[2,4,1408]{2,1,0:T(4,128)S(1)} %pad_maximum_fusion.17), channel_id=1, source_target_pairs={{0,16},{8,24},{16,0},{24,8},{1,17},{9,25},{17,1},{25,9},{2,18},{10... | collective-permute-start | bytes 135176 | tf_op jit(solution)/shard_map/ppermute | solution.py:27
  1175.8 7.7 collective-permute-start.32
  1206.4 9.7 collective-permute-start.43
  1216.2 6.2 collective-permute-start.44
  1221.8 21.3 %collective-permute-start.42 = (bf16[4,352,1408]{2,1,0:T(8,128)(2,1)}, bf16[4,352,1408]{2,1,0:T(8,128)(2,1)}, u32[]{:S(2)}, u32[]{:S(2)}) collective-permute-start(bf16[4,352,1408]{2,1,0:T(8,128)(2,1)} %dynamic-slice_bitcast_fusion), channel_id=1, source_target_pairs={{0,4},{4,0},{1,5},{5,1},{2,6},{6,2},{3,7},{7,3},{8,12},{12,8},{9,1... | collective-permute-start | bytes 11894792 | tf_op jit(solution)/shard_map/ppermute | solution.py:27
  1222.4 4.6 collective-permute-start.45
  1231.2 8.4 collective-permute-start.47
  1447.7 5.9 collective-permute-start.50
  1449.9 5.5 collective-permute-start.49
  1453.0 6.2 collective-permute-start.48
  (76 other events, 1008.2 us)

commit v4 on v3

--- a/solution.py
+++ b/solution.py
@@ -327,41 +327,44 @@
                 value = value + along[w][i - 1].astype(F32)
             outs[w][...] = value
 
-        slots = (*range(1, wide), 0)
-        sums = []
-        raw = {w: [] for w in range(n)}
-        for w in range(n):
-            for i in slots:
-                for k in by_distance(chips)[::-1]:
-                    if not children(k, i):
-                        raw[w].append(lambda w=w, k=k, i=i: pass_on(own(w, k, i), w, k, i))
-                    if children(k, i):
-                        ends.append(lambda w=w, k=k, i=i: pass_on(
-                            nearby[w].at[i, children(k, i)[0] - 1], w, k, i, True))
-                    else:
-                        ends.append(lambda w=w, k=k, i=i: pass_on(own(w, k, i), w, k, i, True))
-            mine = [(w, k, i) for i in slots for k in by_distance(chips)[::-1] if children(k, i)]
-            mine += [(w, 0, i) for i in slots]
-            for turn, (_, k, i) in enumerate(mine):
-                sums.append((w, k, i, turn % 2))
-            for i in range(1, wide):
+        units = [(w, i) for w in range(n) for i in (*range(1, wide), 0)]
+        far_first = by_distance(chips)[::-1]
+        raw, sums, turns = [], [], [0] * n
+        for w, i in units:
+            raw.append([])
+            for k in far_first:
+                if children(k, i):
+                    ends.append(lambda w=w, k=k, i=i: pass_on(
+                        nearby[w].at[i, children(k, i)[0] - 1], w, k, i, True))
+                else:
+                    raw[-1].append(lambda w=w, k=k, i=i: pass_on(own(w, k, i), w, k, i))
+                    ends.append(lambda w=w, k=k, i=i: pass_on(own(w, k, i), w, k, i, True))
+            if i:
                 ends.append(lambda w=w, i=i: onward(w, i, True))
+        for u in range(len(units) + 1):
+            if u < len(units):
+                sums += [(u, k) for k in far_first if children(k, units[u][1])]
+            if u:
+                sums.append((u - 1, 0))
+        todo = []
+        for u, k in sums:
+            w, i = units[u]
+            todo.append((u, w, k, i, turns[w] % 2))
+            turns[w] += 1
         steps.append(lambda: greet(chips, wide, False))
-        steps += raw[0]
-        steps += raw[1] if n > 1 else []
+        for part in raw[:3]:
+            steps += part
         first = len(steps)
-        for w in range(n):
-            mine = [t for t in sums if t[0] == w]
-            steps.append(lambda t=mine[0]: load(*t))
-            for j, (_, k, i, turn) in enumerate(mine):
-                if j + 1 < len(mine):
-                    steps.append(lambda t=mine[j + 1]: load(*t))
-                if k:
-                    steps.append(lambda w=w, k=k, i=i, turn=turn: relay(w, k, i, turn))
-                else:
-                    steps.append(lambda w=w, i=i, turn=turn: finish(w, i, turn))
-            if w + 2 < n:
-                steps += raw[w + 2]
+        steps.append(lambda t=todo[0]: load(*t[1:]))
+        for j, (u, w, k, i, turn) in enumerate(todo):
+            if j + 1 < len(todo):
+                steps.append(lambda t=todo[j + 1]: load(*t[1:]))
+            if k:
+                steps.append(lambda w=w, k=k, i=i, turn=turn: relay(w, k, i, turn))
+                if u + 3 < len(units) and todo[j + 1][0] != u:
+                    steps += raw[u + 3]
+            else:
+                steps.append(lambda w=w, i=i, turn=turn: finish(w, i, turn))
         for w in range(n):
             steps.append(lambda w=w: last(w))
         return steps + ends, first

time: 1470 us -> 1430 us (0.973)
  Pallas kernels: 1060 us -> 1020 us
    pallas_call x4, Pallas kernels: 567 us -> 541 us  [beside(): pl.pallas_call(mixed, grid=(groups,), in_specs=list(in_specs) + work.in_s...]
  transfers between devices with their start and end apart: 57 -> 57, of which waited for: 16 -> 17; matrix products, arithmetic and copies ran while one was open for 14% -> 14% of each run, Pallas kernels for 22% -> 23%
where the time goes in v4:
time: 1430 us
  Pallas kernels  1020 us (71%)
  local copies, waits for them, and re-layouts  162 us (11%)
  waiting for transfers between devices  92 us (6%)
  other arithmetic  76.8 us (5%)
  starting transfers between devices  61.1 us (4%)
  matrix products  15.2 us (1%)
    pallas_call x4, Pallas kernels, beside(): pl.pallas_call(mixed, grid=(groups,), in_specs=list(in_specs) + work.in_s...  541 us
    pallas_call x2, Pallas kernels, alone(): pl.pallas_call(kernel, in_specs=work.in_specs, out_specs=work.out_specs,...  321 us
    ppermute x57, waiting for transfers between devices, swap(): return lax.ppermute(value, axis, [(i, i ^ mask) for i in range(size)])  92 us
    pallas_call x1, Pallas kernels, mlp(): pl.pallas_call(functools.partial(mlp_kernel, own), grid=(groups * MLP_CHU...  90.4 us
    ppermute x57, starting transfers between devices, swap(): return lax.ppermute(value, axis, [(i, i ^ mask) for i in range(size)])  61.1 us
  transfers between devices with their start and end apart: 57, of which 17 were waited for; matrix products, arithmetic and copies ran while one was open for 14% of the time, Pallas kernels for 23%

profile of v4, /device:TPU:9, one launch (start us, length us, event | category | flops | bytes accessed | tf_op | source)
XLA Modules:
  0.0 1427.9 jit_solution(9386835405948291404)
XLA Ops:
  32.6 137.6 %gather.1 = (f32[4,2,4,1,3932]{4,3,2,1,0:T(1,128)}, bf16[4,2,4,88,1408]{4,3,2,1,0:T(8,128)(2,1)}, bf16[4,2,4,44,1408]{4,3,2,1,0:T(8,128)(2,1)}, bf16[4,4,352,704]{3,2,1,0:T(8,128)(2,1)}) custom-call(f32[1,3932]{1,0:T(1,128)} %broadcast_in_dim.82.refs_0_, bf16[88,1408]{1,0:T(8,128)(2,1)} %refs_1_.1, bf16[44,1408]{1,0:T(8,128)(2,1)} %refs_2_.1, ...), custom_call_target="tpu_custom_call" | custom-call | tf_op jit(solution)/shard_map/gather/pallas_call | solution.py:380
  175.4 11.9 merge.1
  192.0 3.0 sine_multiply_fusion
  200.8 6.0 reshape.589
  206.8 2.8 convolution_reduce_fusion
  211.7 3.0 collective-permute-start.3
  215.4 21.4 %collective-permute-done.4 = bf16[128,1408]{1,0:T(8,128)(2,1)S(1)} collective-permute-done((bf16[128,1408]{1,0:T(8,128)(2,1)S(1)}, bf16[128,1408]{1,0:T(8,128)(2,1)S(1)}, u32[]{:S(2)}, u32[]{:S(2)}) %collective-permute-start.4) | collective-permute-done | bytes 360480 | tf_op jit(solution)/shard_map/ppermute | solution.py:27
  236.8 5.8 collective-permute-done.3
  244.3 4.1 norm.3
  251.0 2.6 broadcast_select_fusion
  263.9 2.6 copy.249
  270.9 4.6 fusion.52
  275.5 4.5 copy.250.refs_0_
  280.1 156.4 %self_forward.1 = (bf16[4,1024,528]{2,1,0:T(8,128)(2,1)}, bf16[4,1024,352]{2,1,0:T(8,128)(2,1)}, bf16[4,1024,176]{2,1,0:T(8,128)(2,1)}, f32[4,2,1024]{2,1,0:T(2,...) custom-call(bf16[1024,1408]{1,0:T(8,128)(2,1)} %copy.250.refs_0_, ...), custom_call_target="tpu_custom_call" | custom-call | tf_op jit(solution)/shard_map/self_forward/pallas_call | solution.py:430
  436.4 3.6 collective-permute-start.9
  447.3 5.2 norm.4
  468.8 139.0 %cross_forward.1 = (bf16[4,1024,176]{2,1,0:T(8,128)(2,1)}, bf16[4,1024,176]{2,1,0:T(8,128)(2,1)}, bf16[4,336,352]{2,1,0:T(8,128)(2,1)}, bf16[4,336,176]{2,1,0:T(...) custom-call(bf16[1024,1408]{1,0:T(8,128)(2,1)} %constant_dynamic-upd, ...), custom_call_target="tpu_custom_call" | custom-call | tf_op jit(solution)/shard_map/cross_forward/pallas_call | solution.py:430
  612.8 5.7 norm.5
  622.4 4.6 fusion.50
  627.0 4.7 copy.259.cot_t
  631.7 4.7 fusion.51
  636.4 4.6 copy.258.x_ref
  641.0 90.4 %mlp.1 = (bf16[4,4,352,1536]{3,2,1,0:T(8,128)(2,1)}, f32[512,1408]{1,0:T(8,128)}, bf16[512,1408]{1,0:T(8,128)(2,1)}, f32[512,1408]{1,0:T(8,128)}, bf16[512,1408]{1,0:T(8,128)(2,1)}, /*index=5*/f32[12,1,256]{2,1,0:T(1,128)}) custom-call(bf16[1024,1408]{1,0:T(8,128)(2,1)} %copy.258.x_ref, bf16[1024,1408]{1,0:T(8,128)(2,1)} %get-tuple-element.253.cot_ref, ...), custom_call_target="tpu_custom_call" | custom-call | tf_op jit(solution)/shard_map/mlp/pallas_call | solution.py:900
  732.2 3.0 collective-permute-done.24.refs_1_
  735.1 7.1 norm_back.3
  742.4 3.6 add_convert_fusion
  746.7 13.2 collective-permute-start.21
  761.0 21.3 %collective-permute-done.21 = bf16[128,1408]{1,0:T(8,128)(2,1)S(1)} collective-permute-done((bf16[128,1408]{1,0:T(8,128)(2,1)S(1)}, bf16[128,1408]{1,0:T(8,128)(2,1)S(1)}, u32[]{:S(2)}, u32[]{:S(2)}) %collective-permute-start.21) | collective-permute-done | bytes 360480 | tf_op jit(solution)/shard_map/ppermute | solution.py:27
  786.4 98.5 %cross_backward.1 = (bf16[4,4,352,352]{3,2,1,0:T(8,128)(2,1)}, bf16[4,4,256,352]{3,2,1,0:T(8,128)(2,1)}, f32[512,1408]{1,0:T(8,128)}, bf16[512,1408]{1,0:T(8,128...) custom-call(bf16[1024,1408]{1,0:T(8,128)(2,1)} %constant_dynamic-upd, ...), custom_call_target="tpu_custom_call" | custom-call | tf_op jit(solution)/shard_map/cross_backward/pallas_call | solution.py:430
  892.2 7.6 norm_back.4
  903.6 3.8 copy.260
  919.9 5.5 collective-permute-done.35
  927.2 3.2 pad_maximum_fusion.4.refs_1_
  930.4 147.5 %self_backward.1 = (bf16[4,4,352,704]{3,2,1,0:T(8,128)(2,1)}, f32[512,1408]{1,0:T(8,128)}, bf16[512,1408]{1,0:T(8,128)(2,1)}, f32[4,1,528]{2,1,0:T(1,128)}, f32[...) custom-call(bf16[1408,1024]{1,0:T(8,128)(2,1)} %get-tuple-element.250.refs_0_, ...), custom_call_target="tpu_custom_call" | custom-call | tf_op jit(solution)/shard_map/self_backward/pallas_call | solution.py:430
  1094.8 6.5 norm_back.5
  1102.1 3.1 collective-permute-start.37
  1117.0 21.2 %collective-permute-done.31 = bf16[128,1408]{1,0:T(8,128)(2,1)S(1)} collective-permute-done((bf16[128,1408]{1,0:T(8,128)(2,1)S(1)}, bf16[128,1408]{1,0:T(8,128)(2,1)S(1)}, u32[]{:S(2)}, u32[]{:S(2)}) %collective-permute-start.31) | collective-permute-done | bytes 360480 | tf_op jit(solution)/shard_map/ppermute | solution.py:27
  1138.3 5.6 collective-permute-done.30
  1153.5 2.8 maximum_select_fusion.5
  1156.3 17.1 %merge_back.1 = (f32[512,1408]{1,0:T(8,128)}, f32[512,1408]{1,0:T(8,128)}, bf16[512,2816]{1,0:T(8,128)(2,1)}, f32[5,1408]{1,0:T(8,128)}) custom-call(bf16[512,1408]{1,0:T(8,128)(2,1)} %bitcast.250, bf16[512,1408]{1,0:T(8,128)(2,1)} %bitcast.252, bf16[512,1408]{1,0:T(8,128)(2,1)} %bitcast.259, bf16[2816,1408]{1,0:T(8,128)(2,1)} %bitcast.244, ...), custom_call_target="tpu_custom_call" | custom-call | tf_op jit(solution)/shard_map/merge_back/pallas_call | solution.py:990
  1177.2 8.7 convolution_convert_fusion
  1187.4 4.6 dynamic-slice_bitcast_fusion
  1192.6 3.2 collective-permute-start.45
  1199.3 2.7 fusion.41
  1203.5 7.0 copy_bitcast_fusion
  1214.0 6.3 fusion
  1220.3 183.7 %scatter.1 = (f32[352,704]{1,0:T(8,128)}, f32[352,352]{1,0:T(8,128)}, f32[256,352]{1,0:T(8,128)}, f32[88,1408]{1,0:T(8,128)}) custom-call(bf16[4,4,352,704]{3,2,1,0:T(8,128)(2,1)} %get-tuple-element.129.refs_0_, bf16[4,4,352,352]{3,2,1,0:T(8,128)(2,1)} %get-tuple-element.130.refs_1_, bf16[4,4,256,352]{3,2,1,0:T(8,128)(2,1)} %get-tuple-element.131.refs_2_, ...), custom_call_target="tpu_custom_call" | custom-call | tf_op jit(solution)/shard_map/scatter/pallas_call | solution.py:380
  1422.4 3.2 reshape.608
  (518 shorter events, 206.5 us)
Async XLA Ops:
  2.4 193.9 %collective-permute-start.7 = (bf16[128,2,176]{0,2,1:T(8,128)(2,1)}, bf16[128,2,176]{0,2,1:T(8,128)(2,1)}, u32[]{:S(2)}, u32[]{:S(2)}) collective-permute-start(bf16[128,2,176]{0,2,1:T(8,128)(2,1)} %get-tuple-element.325), channel_id=1, source_target_pairs={{0,4},{4,0},{1,5},{5,1},{2,6},{6,2},{3,7},{7,3},{8,12},{12,8},{9,1... | collective-permute-start | bytes 270344 | tf_op jit(solution)/shard_map/ppermute | solution.py:27
  7.9 243.1 %collective-permute-start.6 = (bf16[176,2,176]{2,1,0:T(2,128)(2,1)}, bf16[176,2,176]{2,1,0:T(2,128)(2,1)}, u32[]{:S(2)}, u32[]{:S(2)}) collective-permute-start(bf16[176,2,176]{2,1,0:T(2,128)(2,1)} %bitcast.236), channel_id=1, source_target_pairs={{0,4},{4,0},{1,5},{5,1},{2,6},{6,2},{3,7},{7,3},{8,12},{12,8},{9,1... | collective-permute-start | bytes 371720 | tf_op jit(solution)/shard_map/ppermute | solution.py:27
  13.2 248.1 %collective-permute-start.8 = (bf16[176,3,2,256]{3,0,2,1:T(8,128)(2,1)}, bf16[176,3,2,256]{3,0,2,1:T(8,128)(2,1)}, u32[]{:S(2)}, u32[]{:S(2)}) collective-permute-start(bf16[176,3,2,256]{3,0,2,1:T(8,128)(2,1)} %copy.247), channel_id=1, source_target_pairs={{0,4},{4,0},{1,5},{5,1},{2,6},{6,2},{3,7},{7,3},{8,12},{12,8},{9,1... | collective-permute-start | bytes 1622024 | tf_op jit(solution)/shard_map/ppermute | solution.py:27
  17.3 12.0 collective-permute-start
  189.7 19.9 %collective-permute-start.1 = (bf16[2,128,1408]{2,1,0:T(8,128)(2,1)}, bf16[2,128,1408]{2,1,0:T(8,128)(2,1)}, u32[]{:S(2)}, u32[]{:S(2)}) collective-permute-start(bf16[2,128,1408]{2,1,0:T(8,128)(2,1)} %get-tuple-element.303), channel_id=1, source_target_pairs={{0,4},{4,0},{1,5},{5,1},{2,6},{6,2},{3,7},{7,3},{8,12},{12,8},{9,1... | collective-permute-start | bytes 2162696 | tf_op jit(solution)/shard_map/ppermute | solution.py:27
  211.4 25.5 %collective-permute-start.4 = (bf16[128,1408]{1,0:T(8,128)(2,1)S(1)}, bf16[128,1408]{1,0:T(8,128)(2,1)S(1)}, u32[]{:S(2)}, u32[]{:S(2)}) collective-permute-start(bf16[128,1408]{1,0:T(8,128)(2,1)S(1)} %get-tuple-element.299), channel_id=1, source_target_pairs={{0,3},{1,2},{2,1},{3,0},{4,7},{5,6},{6,5},{7,4},{8,11},{9,10},{10,... | collective-permute-start | bytes 1081352 | tf_op jit(solution)/shard_map/ppermute | solution.py:27
  211.7 30.9 %collective-permute-start.3 = (bf16[128,1408]{1,0:T(8,128)(2,1)S(1)}, bf16[128,1408]{1,0:T(8,128)(2,1)S(1)}, u32[]{:S(2)}, u32[]{:S(2)}) collective-permute-start(bf16[128,1408]{1,0:T(8,128)(2,1)S(1)} %get-tuple-element.300), channel_id=1, source_target_pairs={{0,2},{1,3},{2,0},{3,1},{4,6},{5,7},{6,4},{7,5},{8,10},{9,11},{10,... | collective-permute-start | bytes 1081352 | tf_op jit(solution)/shard_map/ppermute | solution.py:27
  214.7 27.9 %collective-permute-start.2 = (bf16[128,1408]{1,0:T(8,128)(2,1)S(1)}, bf16[128,1408]{1,0:T(8,128)(2,1)S(1)}, u32[]{:S(2)}, u32[]{:S(2)}) collective-permute-start(bf16[128,1408]{1,0:T(8,128)(2,1)S(1)} %get-tuple-element.301), channel_id=1, source_target_pairs={{0,1},{1,0},{2,3},{3,2},{4,5},{5,4},{6,7},{7,6},{8,9},{9,8},{10,11... | collective-permute-start | bytes 1081352 | tf_op jit(solution)/shard_map/ppermute | solution.py:27
  250.0 20.8 %collective-permute-start.5 = (bf16[512,1408]{0,1:T(8,128)(2,1)S(1)}, bf16[512,1408]{0,1:T(8,128)(2,1)}, u32[]{:S(2)}, u32[]{:S(2)}) collective-permute-start(bf16[512,1408]{0,1:T(8,128)(2,1)S(1)} %copy.238), channel_id=1, source_target_pairs={{0,4},{4,0},{1,5},{5,1},{2,6},{6,2},{3,7},{7,3},{8,12},{12,8},{9,1... | collective-permute-start | bytes 4325384 | tf_op jit(solution)/shard_map/ppermute | solution.py:27
  436.4 10.9 collective-permute-start.9
  442.5 15.7 %collective-permute-start.11 = (bf16[333,1024]{1,0:T(8,128)(2,1)}, bf16[333,1024]{1,0:T(8,128)(2,1)}, u32[]{:S(2)}, u32[]{:S(2)}) collective-permute-start(bf16[333,1024]{1,0:T(8,128)(2,1)} %bitcast.231), channel_id=1, source_target_pairs={{0,4},{4,0},{1,5},{5,1},{2,6},{6,2},{3,7},{7,3},{8,12},{12,8},{9,1... | collective-permute-start | bytes 2045960 | tf_op jit(solution)/shard_map/ppermute | solution.py:27
  446.3 14.1 collective-permute-start.14
  452.6 13.6 collective-permute-start.10
  462.3 146.5 %collective-permute-start.17 = (bf16[128,1408]{1,0:T(8,128)(2,1)S(1)}, bf16[128,1408]{1,0:T(8,128)(2,1)}, u32[]{:S(2)}, u32[]{:S(2)}) collective-permute-start(bf16[128,1408]{1,0:T(8,128)(2,1)S(1)} %get-tuple-element.287), channel_id=1, source_target_pairs={{0,3},{1,2},{2,1},{3,0},{4,7},{5,6},{6,5},{7,4},{8,11},{9,10},{10,... | collective-permute-start | bytes 1081352 | tf_op jit(solution)/shard_map/ppermute | solution.py:27
  462.3 146.5 %collective-permute-start.16 = (bf16[128,1408]{1,0:T(8,128)(2,1)S(1)}, bf16[128,1408]{1,0:T(8,128)(2,1)}, u32[]{:S(2)}, u32[]{:S(2)}) collective-permute-start(bf16[128,1408]{1,0:T(8,128)(2,1)S(1)} %get-tuple-element.288), channel_id=1, source_target_pairs={{0,2},{1,3},{2,0},{3,1},{4,6},{5,7},{6,4},{7,5},{8,10},{9,11},{10,... | collective-permute-start | bytes 1081352 | tf_op jit(solution)/shard_map/ppermute | solution.py:27
  463.9 144.9 %collective-permute-start.15 = (bf16[128,1408]{1,0:T(8,128)(2,1)S(1)}, bf16[128,1408]{1,0:T(8,128)(2,1)}, u32[]{:S(2)}, u32[]{:S(2)}) collective-permute-start(bf16[128,1408]{1,0:T(8,128)(2,1)S(1)} %get-tuple-element.289), channel_id=1, source_target_pairs={{0,1},{1,0},{2,3},{3,2},{4,5},{5,4},{6,7},{7,6},{8,9},{9,8},{10,11... | collective-permute-start | bytes 1081352 | tf_op jit(solution)/shard_map/ppermute | solution.py:27
  607.8 5.0 collective-permute-start.12
  611.7 10.7 collective-permute-start.18
  620.2 11.5 collective-permute-start.13
  731.6 10.8 collective-permute-start.19
  742.2 41.8 %collective-permute-start.25 = (bf16[512,1408]{1,0:T(8,128)(2,1)}, bf16[512,1408]{1,0:T(8,128)(2,1)S(1)}, u32[]{:S(2)}, u32[]{:S(2)}) collective-permute-start(bf16[512,1408]{1,0:T(8,128)(2,1)} %get-tuple-element.105), channel_id=1, source_target_pairs={{0,4},{4,0},{1,5},{5,1},{2,6},{6,2},{3,7},{7,3},{8,12},{12,8},{9,1... | collective-permute-start | bytes 4325384 | tf_op jit(solution)/shard_map/ppermute | solution.py:27
  746.1 14.9 %collective-permute-start.22 = (bf16[128,1408]{1,0:T(8,128)(2,1)S(1)}, bf16[128,1408]{1,0:T(8,128)(2,1)S(1)}, u32[]{:S(2)}, u32[]{:S(2)}) collective-permute-start(bf16[128,1408]{1,0:T(8,128)(2,1)S(1)} %get-tuple-element.279), channel_id=1, source_target_pairs={{0,3},{1,2},{2,1},{3,0},{4,7},{5,6},{6,5},{7,4},{8,11},{9,10},{10,... | collective-permute-start | bytes 1081352 | tf_op jit(solution)/shard_map/ppermute | solution.py:27
  746.7 35.7 %collective-permute-start.21 = (bf16[128,1408]{1,0:T(8,128)(2,1)S(1)}, bf16[128,1408]{1,0:T(8,128)(2,1)S(1)}, u32[]{:S(2)}, u32[]{:S(2)}) collective-permute-start(bf16[128,1408]{1,0:T(8,128)(2,1)S(1)} %get-tuple-element.280), channel_id=1, source_target_pairs={{0,2},{1,3},{2,0},{3,1},{4,6},{5,7},{6,4},{7,5},{8,10},{9,11},{10,... | collective-permute-start | bytes 1081352 | tf_op jit(solution)/shard_map/ppermute | solution.py:27
  759.8 22.9 %collective-permute-start.20 = (bf16[128,1408]{1,0:T(8,128)(2,1)S(1)}, bf16[128,1408]{1,0:T(8,128)(2,1)S(1)}, u32[]{:S(2)}, u32[]{:S(2)}) collective-permute-start(bf16[128,1408]{1,0:T(8,128)(2,1)S(1)} %get-tuple-element.281), channel_id=1, source_target_pairs={{0,1},{1,0},{2,3},{3,2},{4,5},{5,4},{6,7},{7,6},{8,9},{9,8},{10,11... | collective-permute-start | bytes 1081352 | tf_op jit(solution)/shard_map/ppermute | solution.py:27
  885.0 7.2 collective-permute-start.26
  889.1 12.9 collective-permute-start.23
  890.9 17.1 %collective-permute-start.33 = (bf16[336,1024]{1,0:T(8,128)(2,1)}, bf16[336,1024]{1,0:T(8,128)(2,1)}, u32[]{:S(2)}, u32[]{:S(2)}) collective-permute-start(bf16[336,1024]{1,0:T(8,128)(2,1)} %convert_element_type.108), channel_id=1, source_target_pairs={{0,4},{4,0},{1,5},{5,1},{2,6},{6,2},{3,7},{7,3},{8,12},{12,8},{9,1... | collective-permute-start | bytes 2064392 | tf_op jit(solution)/shard_map/ppermute | solution.py:27
  899.7 27.5 %collective-permute-start.27 = (bf16[512,1408]{1,0:T(8,128)(2,1)}, bf16[512,1408]{1,0:T(8,128)(2,1)}, u32[]{:S(2)}, u32[]{:S(2)}) collective-permute-start(bf16[512,1408]{1,0:T(8,128)(2,1)} %get-tuple-element.116), channel_id=1, source_target_pairs={{0,4},{4,0},{1,5},{5,1},{2,6},{6,2},{3,7},{7,3},{8,12},{12,8},{9,1... | collective-permute-start | bytes 4325384 | tf_op jit(solution)/shard_map/ppermute | solution.py:27
  914.3 5.5 collective-permute-start.36
  914.7 5.2 collective-permute-start.34
  914.7 10.6 collective-permute-start.35
  1077.9 16.9 %collective-permute-start.28 = (bf16[512,1408]{1,0:T(8,128)(2,1)}, bf16[512,1408]{1,0:T(8,128)(2,1)}, u32[]{:S(2)}, u32[]{:S(2)}) collective-permute-start(bf16[512,1408]{1,0:T(8,128)(2,1)} %get-tuple-element.122), channel_id=1, source_target_pairs={{0,4},{4,0},{1,5},{5,1},{2,6},{6,2},{3,7},{7,3},{8,12},{12,8},{9,1... | collective-permute-start | bytes 4325384 | tf_op jit(solution)/shard_map/ppermute | solution.py:27
  1082.3 5.4 collective-permute-start.52
  1089.1 20.9 %collective-permute-start.51 = (f32[176,3,2,256]{3,0,2,1:T(8,128)}, f32[176,3,2,256]{3,0,2,1:T(8,128)}, u32[]{:S(2)}, u32[]{:S(2)}) collective-permute-start(f32[176,3,2,256]{3,0,2,1:T(8,128)} %get-tuple-element.259), channel_id=1, source_target_pairs={{0,4},{4,0},{1,5},{5,1},{2,6},{6,2},{3,7},{7,3},{8,12},{12,8},{9,1... | collective-permute-start | bytes 3244040 | tf_op jit(solution)/shard_map/ppermute | solution.py:27
  1093.6 11.6 collective-permute-start.55
  1113.4 24.8 %collective-permute-start.31 = (bf16[128,1408]{1,0:T(8,128)(2,1)S(1)}, bf16[128,1408]{1,0:T(8,128)(2,1)S(1)}, u32[]{:S(2)}, u32[]{:S(2)}) collective-permute-start(bf16[128,1408]{1,0:T(8,128)(2,1)S(1)} %get-tuple-element.269), channel_id=1, source_target_pairs={{0,3},{1,2},{2,1},{3,0},{4,7},{5,6},{6,5},{7,4},{8,11},{9,10},{10,... | collective-permute-start | bytes 1081352 | tf_op jit(solution)/shard_map/ppermute | solution.py:27
  1113.9 30.0 %collective-permute-start.30 = (bf16[128,1408]{1,0:T(8,128)(2,1)S(1)}, bf16[128,1408]{1,0:T(8,128)(2,1)S(1)}, u32[]{:S(2)}, u32[]{:S(2)}) collective-permute-start(bf16[128,1408]{1,0:T(8,128)(2,1)S(1)} %get-tuple-element.270), channel_id=1, source_target_pairs={{0,2},{1,3},{2,0},{3,1},{4,6},{5,7},{6,4},{7,5},{8,10},{9,11},{10,... | collective-permute-start | bytes 1081352 | tf_op jit(solution)/shard_map/ppermute | solution.py:27
  1115.9 27.9 %collective-permute-start.29 = (bf16[128,1408]{1,0:T(8,128)(2,1)S(1)}, bf16[128,1408]{1,0:T(8,128)(2,1)S(1)}, u32[]{:S(2)}, u32[]{:S(2)}) collective-permute-start(bf16[128,1408]{1,0:T(8,128)(2,1)S(1)} %get-tuple-element.271), channel_id=1, source_target_pairs={{0,1},{1,0},{2,3},{3,2},{4,5},{5,4},{6,7},{7,6},{8,9},{9,8},{10,11... | collective-permute-start | bytes 1081352 | tf_op jit(solution)/shard_map/ppermute | solution.py:27
  1116.2 36.4 %collective-permute-start.41 = (f32[2,4,1408]{2,1,0:T(4,128)S(1)}, f32[2,4,1408]{2,1,0:T(4,128)}, u32[]{:S(2)}, u32[]{:S(2)}) collective-permute-start(f32[2,4,1408]{2,1,0:T(4,128)S(1)} %pad_maximum_fusion.17), channel_id=1, source_target_pairs={{0,16},{8,24},{16,0},{24,8},{1,17},{9,25},{17,1},{25,9},{2,18},{10... | collective-permute-start | bytes 135176 | tf_op jit(solution)/shard_map/ppermute | solution.py:27
  1145.4 8.1 collective-permute-start.32
  1176.3 9.7 collective-permute-start.43
  1186.1 6.4 collective-permute-start.44
  1192.0 22.0 %collective-permute-start.42 = (bf16[4,352,1408]{2,1,0:T(8,128)(2,1)}, bf16[4,352,1408]{2,1,0:T(8,128)(2,1)}, u32[]{:S(2)}, u32[]{:S(2)}) collective-permute-start(bf16[4,352,1408]{2,1,0:T(8,128)(2,1)} %dynamic-slice_bitcast_fusion), channel_id=1, source_target_pairs={{0,4},{4,0},{1,5},{5,1},{2,6},{6,2},{3,7},{7,3},{8,12},{12,8},{9,1... | collective-permute-start | bytes 11894792 | tf_op jit(solution)/shard_map/ppermute | solution.py:27
  1197.3 4.7 collective-permute-start.46
  1202.0 8.5 collective-permute-start.47
  1406.4 6.0 collective-permute-start.50
  1408.7 5.5 collective-permute-start.49
  1411.8 6.2 collective-permute-start.48
  (76 other events, 987.1 us)
